TPU v7x, 32 devices: a whole 2x2x4 slice. The times are simulated.
32 devices in a mesh: blk: 8 (over z, y), line: 4 (over x, core).
Axes of the slice: x: 2, y: 2, z: 4, core: 2. Of those that a mesh axis runs over, the one named last changes fastest.
Arguments:
- density: float32 [8, 64, 4096], P('blk', 'line'), may hold values from 0.5 to 1.5
- momentum: float32 [8, 3, 64, 4096], P('blk', None, 'line'), may hold values from -0.5 to 0.5
- energy: float32 [8, 64, 4096], P('blk', 'line'), may hold values from 2 to 4
- adjoint: float32 [8, 5, 64, 4096], P('blk', None, 'line'), may hold values from -6 to 6
- partners: int32 [8, 4], P('blk'), may hold values from 0 to 7
- counts: int32 [8], P('blk'), may hold values from 1 to 4, as said below
- orient: int32 [8, 4], P('blk'), may hold values from 0 to 1
Outputs:
- residual: float32 [8, 5, 64, 4096], P('blk', None, 'line')
- correction: float32 [8], P('blk')
Inputs may be any that keep to these rules, and one draw needn't show every extreme that they name: `partners`: slots at or past counts[b] are padding and are not read. `counts`: some block lists 4 partners.
All inputs are finite; a program needn't handle non-finite values.
Results may differ from a plain program's by a relative error of at most 0.0003.
Values sent between devices are 32-bit elements; how exact they have to be, the bound alone decides.
No kernel may reach another device: no remote copies, remote signals or barrier semaphores. Data moves between devices by JAX's collectives and lax.ppermute only.
A program may use at most 64 MiB of HBM per device.

v0:
```python
import jax
import jax.numpy as jnp
from jax import lax
from jax.sharding import PartitionSpec as P

stencil_one = 0.75
stencil_two = -0.15
stencil_three = 1.0 / 60.0
gamma_less = 0.4
viscosity = 0.5
conduction = 1.5
penalty = 4.0


def difference(fields, direction, start_row, extent):
    length = fields.shape[direction]

    def shifted(offset):
        return lax.slice_in_dim(fields, 3 + offset, length - 3 + offset, axis=direction)

    shape_list = [1] * fields.ndim
    shape_list[direction] = length - 6
    global_row = (start_row + 3 + jnp.arange(length - 6, dtype=jnp.int32)).reshape(shape_list)
    central_one = shifted(1) - shifted(-1)
    central_two = shifted(2) - shifted(-2)
    central_three = shifted(3) - shifted(-3)
    interior = stencil_one * central_one + stencil_two * central_two + stencil_three * central_three
    fourth = 2.0 / 3.0 * central_one - 1.0 / 12.0 * central_two
    second = 0.5 * central_one
    forward = shifted(1) - shifted(0)
    backward = shifted(0) - shifted(-1)
    result = jnp.where((global_row == 2) | (global_row == extent - 3), fourth, interior)
    result = jnp.where((global_row == 1) | (global_row == extent - 2), second, result)
    result = jnp.where(global_row == 0, forward, result)
    result = jnp.where(global_row == extent - 1, backward, result)
    return result


def primitives(fields):
    density_raw = fields[:, 0:1]
    density_safe = jnp.where(density_raw == 0.0, 1.0, density_raw)
    velocity = fields[:, 1:4] / density_safe
    kinetic = 0.5 * jnp.sum(fields[:, 1:4] * velocity, axis=1, keepdims=True)
    pressure = gamma_less * (fields[:, 4:5] - kinetic)
    return (velocity, pressure, density_safe)


def direction_residual(fields, direction, start_row, extent, normal_index):
    velocity, pressure, density_safe = primitives(fields)
    primitive = jnp.concatenate([velocity, pressure / density_safe], axis=1)
    gradient = difference(primitive, direction, start_row, extent)
    length = fields.shape[direction]
    middle = lax.slice_in_dim(fields, 3, length - 3, axis=direction)
    mid_velocity = lax.slice_in_dim(velocity, 3, length - 3, axis=direction)
    mid_pressure = lax.slice_in_dim(pressure, 3, length - 3, axis=direction)
    normal_speed = mid_velocity[:, normal_index : normal_index + 1]
    selector = (jnp.arange(3) == normal_index).astype(fields.dtype).reshape(1, 3, 1, 1)
    convective = jnp.concatenate(
        [
            middle[:, normal_index + 1 : normal_index + 2],
            middle[:, 1:4] * normal_speed + mid_pressure * selector,
            (middle[:, 4:5] + mid_pressure) * normal_speed,
        ],
        axis=1,
    )
    viscous = jnp.concatenate(
        [
            jnp.zeros_like(normal_speed),
            viscosity * gradient[:, 0:3],
            viscosity * conduction * gradient[:, 3:4],
        ],
        axis=1,
    )
    return difference(convective - viscous, direction, start_row + 3, extent)


def per_device(density, momentum, energy, adjoint, partners, counts, orient):
    state = jnp.concatenate([density[:, None], momentum, energy[:, None]], axis=1)
    xrows = state.shape[2]
    yextent = state.shape[3]
    line_count = lax.axis_size("line")
    block_count = lax.axis_size("blk")
    xextent = xrows * line_count
    lines = lax.all_to_all(state, "line", split_axis=3, concat_axis=2, tiled=True)
    padded_lines = jnp.pad(lines, ((0, 0), (0, 0), (6, 6), (0, 0)))
    line_part = direction_residual(padded_lines, 2, -6, xextent, 0)
    xpart = lax.all_to_all(line_part, "line", split_axis=2, concat_axis=3, tiled=True)
    padded_y = jnp.pad(state, ((0, 0), (0, 0), (0, 0), (6, 6)))
    ypart = direction_residual(padded_y, 3, -6, yextent, 1)
    result = xpart + ypart
    bottom_row = state[:, :, :, 0]
    gathered = lax.all_gather(bottom_row, "blk", axis=0, tiled=True)
    slots = jnp.arange(partners.shape[1], dtype=jnp.int32)
    listed = partners[0]
    count_here = counts[0]
    weights = jnp.where(slots < count_here, 1.0 / count_here.astype(jnp.float32), jnp.float32(0.0))
    onehot = (listed[:, None] == jnp.arange(block_count, dtype=jnp.int32)[None, :]).astype(
        jnp.float32
    ) * weights[:, None]
    picked = jnp.einsum("kb,bvx->kvx", onehot, gathered, precision=lax.Precision.HIGHEST)
    signs = (
        jnp.ones((partners.shape[1], 5), jnp.float32)
        .at[:, 2]
        .set(1.0 - 2.0 * orient[0].astype(jnp.float32))
    )
    target = jnp.sum(picked * signs[:, :, None], axis=0)[None]
    result = result.at[:, :, :, yextent - 1].add(penalty * (state[:, :, :, yextent - 1] - target))
    total = lax.psum(jnp.sum(adjoint * result), "line")
    correction = (total / (xextent * yextent)).reshape(1)
    return (result, correction)


def solution(mesh):
    return jax.shard_map(
        per_device,
        mesh=mesh,
        in_specs=(
            P("blk", "line", None),
            P("blk", None, "line", None),
            P("blk", "line", None),
            P("blk", None, "line", None),
            P("blk", None),
            P("blk"),
            P("blk", None),
        ),
        out_specs=(P("blk", None, "line", None), P("blk")),
        check_vma=False,
    )
```

profile of v0, /device:TPU:1, one launch (start us, length us, event | category | flops | bytes accessed | tf_op | source)
XLA Modules:
  0.0 211.3 jit_solution(9206048323847633590)
XLA Ops:
  0.6 1.4 pad_maximum_fusion
  2.0 14.9 %copy.63 = f32[1,5,16,4096]{2,0,1,3:T(1,128)} copy(f32[1,5,16,4096]{3,2,1,0:T(8,128)S(1)} %pad_maximum_fusion) | data formatting | bytes 2621440 | tf_op jit(solution)/shard_map/concatenate | solution.py:78
  16.9 0.5 broadcast.383
  17.4 34.3 %reduce.12 = f32[4096,5,16]{2,1,0:T(8,128)} reduce(f32[4096,5,1,16]{3,2,1,0:T(1,128)} %bitcast.52, f32[]{:T(128)} %broadcast.383), dimensions={2}, to_apply=%bitcast.41.reduce_sub_computation | reduce | bytes 2621444
  51.7 9.3 %reshape.473 = f32[4,1,81920]{2,1,0:T(1,128)} reshape(f32[4096,5,16]{2,1,0:T(8,128)} %reduce.12) | data formatting | bytes 2621440
  61.0 4.3 %all-to-all-start = ((f32[4,1,81920]{2,1,0:T(1,128)}), f32[4,1,81920]{2,1,0:T(1,128)S(1)}, u32[]{:S(2)}, u32[]{:S(2)}) async-start(f32[4,1,81920]{2,1,0:T(1,128)} %reshape.473), calls=%async_computation | async-start | bytes 2621440 | tf_op jit(solution)/shard_map/all_to_all | solution.py:84
  65.3 0.6 compare_or_fusion.2
  65.9 0.6 fusion.80
  66.5 0.1 fusion.59
  66.7 0.7 compare_reduce_fusion
  67.4 0.5 multiply_reduce_fusion.2
  67.9 0.2 fusion.58
  68.1 1.3 pad_slice_fusion.35
  69.4 1.7 fusion.35
  71.2 1.0 copy-done.3
  72.2 0.7 slice-done
  72.9 0.1 copy.75
  73.0 25.3 %all-gather = f32[8,5,16,1]{2,3,1,0:T(1,128)S(1)} all-gather(f32[1,5,16,1]{2,3,1,0:T(1,128)S(1)} %copy.75), channel_id=2, replica_groups=mesh['blk'=8,'line'=4] {'blk'}, dimensions={0}, use_global_device_ids=true | all-gather | bytes 2880 | tf_op jit(solution)/shard_map/all_gather | solution.py:92
  99.0 0.6 fusion.79
  99.7 0.2 fusion.27
  100.0 0.1 copy.73
  100.1 2.2 %fusion.46 = f32[1,3,16,4102]{3,2,1,0:T(8,128)} fusion(f32[1,5,16,4096]{3,2,1,0:T(8,128)S(1)} %copy-done.1, f32[3]{0:T(128)S(1)} %compare_convert_fusion, f32[16,4102]{1,0:T(8,128)} %get-tuple-element.45, f32[16,4102]{1,0:T(8,128)} %get-tuple-element.43), kind=kLoop, calls=%fused_computation.96 | loop fusion | flops 590688 | bytes 2623372 | tf_op jit(solution)/shard_map/add | solution.py:61
  102.3 1.7 slice_multiply_fusion.3
  104.0 5.5 %reduce.13 = f32[4,81920]{1,0:T(4,128)} reduce(f32[4,1,81920]{2,1,0:T(1,128)S(1)} %all-to-all-done, f32[]{:T(128)} %broadcast.383), dimensions={1}, to_apply=%all_to_all.26.reduce_sub_computation | reduce | bytes 2621444 | tf_op jit(solution)/shard_map/all_to_all | solution.py:84
  109.5 27.3 %reshape.474 = f32[4096,5,1,16]{3,2,1,0:T(1,128)} reshape(f32[4,81920]{1,0:T(4,128)} %reduce.13) | data formatting | bytes 2621440
  136.8 19.8 %copy.64 = f32[1,5,16,4096]{3,2,1,0:T(8,128)} copy(f32[1,5,16,4096]{2,0,1,3:T(1,128)} %bitcast.53) | data formatting | bytes 2621440 | tf_op jit(solution)/shard_map/all_to_all | solution.py:84
  156.5 2.2 %all_to_all.27 = f32[1,5,16,4,1024]{4,3,2,1,0:T(4,128)S(1)} reshape(f32[1,5,16,4096]{3,2,1,0:T(8,128)} %copy.64) | data formatting | bytes 2621440 | tf_op jit(solution)/shard_map/all_to_all | solution.py:84
  158.7 0.7 copy.65
  159.5 0.2 multiply_reduce_fusion.1
  159.8 0.1 fusion.56
  159.9 0.5 copy-done.4
  160.4 1.5 fusion.20
  162.0 0.1 pad_slice_fusion.17
  162.1 0.2 fusion.43
  162.4 0.3 maximum_subtract_fusion
  162.7 1.4 fusion.12
  164.1 2.4 %copy.66 = f32[1,5,64,1024]{3,0,1,2:T(1,128)} copy(f32[1,5,64,1024]{3,2,1,0:T(8,128)S(1)} %fusion.12) | data formatting | bytes 2621440 | tf_op jit(solution)/shard_map/jit(_where)/select_n | solution.py:35
  166.5 10.7 %all-to-all-start.1 = ((f32[1,5,64,1024]{3,0,1,2:T(1,128)}), f32[1,5,64,1024]{3,0,1,2:T(1,128)}, u32[]{:S(2)}, u32[]{:S(2)}) async-start(f32[1,5,64,1024]{3,0,1,2:T(1,128)} %copy.66), calls=%async_computation.1 | async-start | bytes 2621440 | tf_op jit(solution)/shard_map/all_to_all | solution.py:87
  177.2 1.5 maximum_subtract_fusion.1
  178.7 14.8 %all-to-all-done.1 = f32[1,5,64,1024]{3,0,1,2:T(1,128)} async-done(((f32[1,5,64,1024]{3,0,1,2:T(1,128)}), f32[1,5,64,1024]{3,0,1,2:T(1,128)}, u32[]{:S(2)}, u32[]{:S(2)}) %all-to-all-start.1) | async-done | bytes 1310752 | tf_op jit(solution)/shard_map/all_to_all | solution.py:87
  193.5 1.6 copy.67
  195.1 0.1 copy.76
  195.2 2.1 fusion.6
  197.3 1.0 copy-done.2
  198.4 0.1 fusion.61
  198.5 1.8 scatter-add.4
  200.3 2.7 %multiply_reduce_fusion = f32[]{:T(128)} fusion(f32[1,5,16,4096]{3,2,1,0:T(8,128)} %param.14, f32[1,5,16,4096]{3,2,1,0:T(8,128)} %scatter-add.4), kind=kLoop, calls=%fused_computation.50 | loop fusion | flops 655359 | bytes 2621444 | tf_op jit(solution)/shard_map/reduce_sum | solution.py:108
  202.9 6.6 %psum.7 = f32[]{:T(128)} all-reduce(f32[]{:T(128)} %multiply_reduce_fusion), channel_id=1, replica_groups=mesh['blk'=8,'line'=4] {'line'}, use_global_device_ids=true, to_apply=%region_5.6 | all-reduce | flops 1 | bytes 8 | tf_op jit(solution)/shard_map/psum | solution.py:108
  (32 shorter events, 0.3 us)
Async XLA Ops:
  2.0 66.1 %copy-start = (f32[1,5,16,4096]{3,2,1,0:T(8,128)}, f32[1,5,16,4096]{3,2,1,0:T(8,128)S(1)}, u32[]{:S(2)}) copy-start(f32[1,5,16,4096]{3,2,1,0:T(8,128)S(1)} %pad_maximum_fusion) | copy-start | bytes 3932164
  61.0 43.0 %all-to-all-start = ((f32[4,1,81920]{2,1,0:T(1,128)}), f32[4,1,81920]{2,1,0:T(1,128)S(1)}, u32[]{:S(2)}, u32[]{:S(2)}) async-start(f32[4,1,81920]{2,1,0:T(1,128)} %reshape.473), calls=%async_computation | async-start | bytes 2621440 | tf_op jit(solution)/shard_map/all_to_all | solution.py:84
  71.2 1.0 copy-start.3
  72.2 0.8 slice-start
  72.2 26.9 %copy-start.7 = (s32[1,4]{1,0:T(1,128)S(1)}, s32[1,4]{1,0:T(1,128)}, u32[]{:S(2)}) copy-start(s32[1,4]{1,0:T(1,128)} %param.17) | copy-start | bytes 52
  72.2 27.6 %copy-start.8 = (s32[1,4]{1,0:T(1,128)S(1)}, s32[1,4]{1,0:T(1,128)}, u32[]{:S(2)}) copy-start(s32[1,4]{1,0:T(1,128)} %param.15) | copy-start | bytes 52
  72.2 27.9 %copy-start.1 = (f32[1,5,16,4096]{3,2,1,0:T(8,128)S(1)}, f32[1,5,16,4096]{3,2,1,0:T(8,128)}, u32[]{:S(2)}) copy-start(f32[1,5,16,4096]{3,2,1,0:T(8,128)} %copy-done) | copy-start | bytes 3932164
  159.8 0.7 copy-start.4
  159.8 0.7 copy-start.5
  159.8 0.7 copy-start.6
  166.5 27.0 %all-to-all-start.1 = ((f32[1,5,64,1024]{3,0,1,2:T(1,128)}), f32[1,5,64,1024]{3,0,1,2:T(1,128)}, u32[]{:S(2)}, u32[]{:S(2)}) async-start(f32[1,5,64,1024]{3,0,1,2:T(1,128)} %copy.66), calls=%async_computation.1 | async-start | bytes 2621440 | tf_op jit(solution)/shard_map/all_to_all | solution.py:87
  197.3 1.1 copy-start.2
where the time goes:
time: 213 us; the launch traced here: 211 us
  local copies, waits for them, and re-layouts  84.1 us (39%)
  other arithmetic  61.9 us (29%)
  blocking collectives  31.9 us (15%)
  starting transfers between devices  14.9 us (7%)
  waiting for transfers between devices  14.8 us (7%)
  between operations  3.43 us (2%)
    unnamed x22, local copies, waits for them, and re-layouts  39.8 us
    unnamed x1, other arithmetic  34.3 us
    all_gather x1, blocking collectives, per_device(): gathered = lax.all_gather(bottom_row, 'blk', axis=0, tiled=True)  25.3 us
    all_to_all x3, local copies, waits for them, and re-layouts, per_device(): lax.all_to_all(state, 'line', split_axis=3, concat_axis=2, tiled=True)  22.7 us
    concatenate x1, local copies, waits for them, and re-layouts, per_device(): jnp.concatenate([density[:, None], momentum, energy[:, None]], axis=1)  14.9 us
    all_to_all x1, waiting for transfers between devices, per_device(): lax.all_to_all(line_part, 'line', split_axis=2, concat_axis=3, tiled=True)  14.8 us
    all_to_all x1, starting transfers between devices, per_device(): lax.all_to_all(line_part, 'line', split_axis=2, concat_axis=3, tiled=True)  10.7 us
    psum x1, blocking collectives, per_device(): total = lax.psum(jnp.sum(adjoint * result), 'line')  6.59 us
  transfers between devices with their start and end apart: 2, of which 1 were waited for; matrix products, arithmetic and copies ran while one was open for 6% of the time, Pallas kernels for 0%

commit v1 on v0

v1 whole, which is shorter than its diff:
```python
import functools

import jax
import jax.numpy as jnp
from jax import lax
from jax.experimental import pallas as pl
from jax.experimental.pallas import tpu as pltpu
from jax.sharding import PartitionSpec as P

STENCIL = (0.75, -0.15, 1.0 / 60.0)
gamma_less = 0.4
viscosity = 0.5
conduction = 1.5
penalty = 4.0
LANES = 128
SUB = 8
CHUNK = 4
F32 = jnp.float32
VMEM_LIMIT = 20 * 1024 * 1024

_ONE = {k: STENCIL[k - 1] for k in (1, 2, 3)}
_ONE.update({-k: -STENCIL[k - 1] for k in (1, 2, 3)})
TWICE = [sum(_ONE[a] * _ONE[b] for a in _ONE for b in _ONE if a + b == m) for m in range(7)]


def tile_iota(axis):
    return lax.broadcasted_iota(jnp.int32, (SUB, LANES), axis)


def coefficients(index, extent):
    inside = (index >= 0) & (index < extent)
    end = (index == 0) | (index == extent - 1)
    second = (index == 1) | (index == extent - 2)
    fourth = (index == 2) | (index == extent - 3)
    one = jnp.where(fourth, 2.0 / 3.0, jnp.where(second, 0.5, jnp.where(end, 1.0, STENCIL[0])))
    two = jnp.where(fourth, -1.0 / 12.0, jnp.where(second | end, 0.0, STENCIL[1]))
    three = jnp.where(fourth | second | end, 0.0, STENCIL[2])
    point = jnp.where(index == 0, -1.0, jnp.where(index == extent - 1, 1.0, 0.0))
    return [jnp.where(inside, c, 0.0).astype(F32) for c in (one, two, three, point)]


def load_state(refs, rt, t):
    density, momentum, energy = refs
    rows = slice(rt * SUB, (rt + 1) * SUB)
    cols = pl.ds(t * LANES if isinstance(t, int) else pl.multiple_of(t * LANES, LANES), LANES)
    return [density[rows, cols]] + [momentum[a, rows, cols] for a in range(3)] + [energy[rows, cols]]


def primitive_of(state):
    rho, m0, m1, m2, e = state
    inv = 1.0 / rho
    u = [m0 * inv, m1 * inv, m2 * inv]
    p = gamma_less * (e - 0.5 * (m0 * u[0] + m1 * u[1] + m2 * u[2]))
    return u, p, p * inv


def convective(state, u, p, d):
    n = u[d]
    out = [state[1 + d]]
    for a in range(3):
        f = state[1 + a] * n
        out.append(f + p if a == d else f)
    out.append((state[4] + p) * n)
    return out


def contribution(state, up):
    u, p, temp = primitive_of(state)
    conv = convective(state, u, p, 0)
    row = tile_iota(0)
    shift = (lambda x, m: pltpu.roll(x, m, 0)) if up else (lambda x, m: pltpu.roll(x, SUB - m, 0))
    sign = -1.0 if up else 1.0
    keep = [None] + [(row < m) if up else (row >= SUB - m) for m in range(1, 7)]
    out = []
    for var in range(5):
        acc = None
        for m in (1, 2, 3):
            term = shift(conv[var], m) * jnp.where(keep[m], sign * STENCIL[m - 1], 0.0)
            acc = term if acc is None else acc + term
        if var:
            prim = u[var - 1] if var < 4 else temp
            scale = -viscosity * (conduction if var == 4 else 1.0)
            for m in range(1, 7):
                acc = acc + shift(prim, m) * jnp.where(keep[m], scale * TWICE[m], 0.0)
        out.append(acc)
    mass, first, second = out[0], out[1], out[2]
    if up:
        first = jnp.where(row >= 6, pltpu.roll(mass, 6, 0), first)
        second = jnp.where(row == 6, pltpu.roll(mass, 4, 0), second)
    else:
        first = jnp.where(row < 2, pltpu.roll(mass, 3, 0), first)
        second = jnp.where(row == 0, pltpu.roll(mass, 1, 0), second)
    return [first, second, out[3], out[4]]


def unpack(tiles, up):
    row = tile_iota(0)
    first, second, third, fourth = tiles
    if up:
        mass = jnp.where(row < 2, pltpu.roll(first, 2, 0), 0.0) + jnp.where(row == 2, pltpu.roll(second, 4, 0), 0.0)
        keep = row < 6
    else:
        mass = jnp.where((row == 5) | (row == 6), pltpu.roll(first, 5, 0), 0.0) + jnp.where(
            row == 7, pltpu.roll(second, 7, 0), 0.0)
        keep = row >= 2
    return [mass] + [jnp.where(keep, x, 0.0) for x in (first, second, third, fourth)]


def pack_kernel(across, density, momentum, energy, out_ref, *rest):
    refs = (density, momentum, energy)
    tiles = density.shape[1] // LANES
    row_tiles = density.shape[0] // SUB
    odd = lax.rem(lax.axis_index("line"), 2)

    def side(up):
        rt = row_tiles - 1 if up else 0

        def body(t, carry):
            cols = pl.ds(pl.multiple_of(t * LANES, LANES), LANES)
            for n, x in enumerate(contribution(load_state(refs, rt, t), up)):
                out_ref[n, :, cols] = x
            return carry

        lax.fori_loop(0, tiles, body, 0, unroll=2)

    up_when = 1 if across else 0

    @pl.when(odd == up_when)
    def _():
        side(True)

    @pl.when(odd != up_when)
    def _():
        side(False)

    if rest:
        (slots,) = rest
        width = slot_width(row_tiles)
        per = LANES // width
        block = lax.axis_index("blk")
        lane = tile_iota(1)
        base = lax.rem(block, per) * width
        value = jnp.zeros((SUB, LANES), F32)
        for rt in range(row_tiles):
            for var, x in enumerate(load_state(refs, rt, 0)):
                value = jnp.where(lane == base + (var * row_tiles + rt), x[:, 0:1], value)
        for n in range(slots.shape[0]):
            slots[n] = jnp.where(block // per == n, value, 0.0)


def slot_width(row_tiles):
    width = 1
    while width < 5 * row_tiles:
        width *= 2
    return width


def whole():
    return pl.BlockSpec(memory_space=pltpu.VMEM)


def params():
    return pltpu.CompilerParams(vmem_limit_bytes=VMEM_LIMIT)


def lane_shifts(tiles):
    lane = tile_iota(1)
    count = len(tiles) - 2
    got = [{0: tiles[j + 1]} for j in range(count)]
    for k in (1, 2, 3):
        ahead = [pltpu.roll(x, LANES - k, 1) for x in tiles[1:]]
        behind = [pltpu.roll(x, k, 1) for x in tiles[:-1]]
        for j in range(count):
            got[j][k] = jnp.where(lane < LANES - k, ahead[j], ahead[j + 1])
            got[j][-k] = jnp.where(lane >= k, behind[j + 1], behind[j])
    return got


def apply(weights, at):
    one, two, three, point = weights
    return one * (at(1) - at(-1)) + two * (at(2) - at(-2)) + three * (at(3) - at(-3)) + point * at(0)


def flux_kernel(density, momentum, energy, fy_ref, xd_ref, prim, press, fx, xcoef, ycoef):
    refs = (density, momentum, energy)
    rows, cols = density.shape
    row_tiles, tiles = rows // SUB, cols // LANES
    line = lax.axis_index("line")
    extent = rows * lax.axis_size("line")
    zero = jnp.zeros((SUB, LANES), F32)

    for g in range(row_tiles + 1):
        for c, w in enumerate(coefficients(line * rows - 3 + g * SUB + tile_iota(0), extent)):
            xcoef[0, g, c] = w
    for r in range(row_tiles):
        for c, w in enumerate(coefficients(line * rows + r * SUB + tile_iota(0), extent)):
            xcoef[1, r, c] = w
    for n, start in enumerate((0, LANES, cols - LANES)):
        for c, w in enumerate(coefficients(start + tile_iota(1), cols)):
            ycoef[n, c] = w

    for var in range(5):
        for r in range(row_tiles):
            fy_ref[var, 0, r * SUB:(r + 1) * SUB, :] = zero
            fy_ref[var, tiles + 1, r * SUB:(r + 1) * SUB, :] = zero
    for var in range(4):
        for r in range(row_tiles + 2):
            prim[var, 0, r * SUB:(r + 1) * SUB, :] = zero
            prim[var, tiles + 1, r * SUB:(r + 1) * SUB, :] = zero
    for j in range(CHUNK):
        for r in range(row_tiles + 1):
            fx[j, 0, r * SUB:(r + 1) * SUB, :] = zero

    def first(t, carry):
        for rt in range(row_tiles):
            u, p, temp = primitive_of(load_state(refs, rt, t))
            at = slice((rt + 1) * SUB, (rt + 2) * SUB)
            for var, x in enumerate(u + [temp]):
                prim[var, t + 1, at, :] = x
            press[t, rt * SUB:(rt + 1) * SUB, :] = p
        for var in range(4):
            prim[var, t + 1, 0:SUB, :] = zero
            prim[var, t + 1, (row_tiles + 1) * SUB:(row_tiles + 2) * SUB, :] = zero
        return carry

    lax.fori_loop(0, tiles, first, 0, unroll=2)

    def second(step, carry):
        t0 = step * CHUNK
        for rt in range(row_tiles):
            at = slice((rt + 1) * SUB, (rt + 2) * SUB)
            own = slice(rt * SUB, (rt + 1) * SUB)
            grads = []
            for var in range(4):
                window = [prim[var, t0 + j, at, :] for j in range(CHUNK + 2)]
                shifted = lane_shifts(window)
                scale = viscosity * (conduction if var == 3 else 1.0)
                line_of = []
                for j in range(CHUNK):
                    which = jnp.where(t0 + j == 0, 0, jnp.where(t0 + j == tiles - 1, 2, 1))
                    w = [ycoef[which, c] for c in range(4)]
                    line_of.append(scale * apply(w, lambda k, j=j: shifted[j][k]))
                grads.append(line_of)
            for j in range(CHUNK):
                t = t0 + j
                state = load_state(refs, rt, t)
                u = [prim[a, t + 1, at, :] for a in range(3)]
                p = press[t, own, :]
                for var, f in enumerate(convective(state, u, p, 1)):
                    fy_ref[var, t + 1, own, :] = f - grads[var - 1][j] if var else f
        for j in range(CHUNK):
            t = t0 + j
            for var in range(4):
                scale = -viscosity * (conduction if var == 3 else 1.0)
                for g in range(row_tiles + 1):
                    w = [xcoef[0, g, c] for c in range(4)]
                    base = SUB - 3 + g * SUB
                    fx[j, var + 1, g * SUB:(g + 1) * SUB, :] = scale * apply(
                        w, lambda k: prim[var, t + 1, base + k:base + k + SUB, :])
            for rt in range(row_tiles):
                at = slice((rt + 1) * SUB, (rt + 2) * SUB)
                own = slice(rt * SUB, (rt + 1) * SUB)
                state = load_state(refs, rt, t)
                u = [prim[a, t + 1, at, :] for a in range(3)]
                for var, f in enumerate(convective(state, u, press[t, own, :], 0)):
                    place = slice(3 + rt * SUB, 3 + (rt + 1) * SUB)
                    fx[j, var, place, :] = fx[j, var, place, :] + f if var else f
            for var in range(5):
                for rt in range(row_tiles):
                    w = [xcoef[1, rt, c] for c in range(4)]
                    base = 3 + rt * SUB
                    xd_ref[var, t, rt * SUB:(rt + 1) * SUB, :] = apply(
                        w, lambda k: fx[j, var, base + k:base + k + SUB, :])
        return carry

    lax.fori_loop(0, tiles // CHUNK, second, 0)


def volume_kernel(density, momentum, energy, adjoint, fy, xd, res_ref, sum_ref, ycoef):
    refs = (density, momentum, energy)
    rows, cols = density.shape
    row_tiles, tiles = rows // SUB, cols // LANES
    for n, start in enumerate((0, LANES, cols - LANES)):
        for c, w in enumerate(coefficients(start + tile_iota(1), cols)):
            ycoef[n, c] = w

    def body(step, acc):
        t0 = step * CHUNK
        for rt in range(row_tiles):
            own = slice(rt * SUB, (rt + 1) * SUB)
            for var in range(5):
                shifted = lane_shifts([fy[var, t0 + j, own, :] for j in range(CHUNK + 2)])
                for j in range(CHUNK):
                    t = t0 + j
                    which = jnp.where(t == 0, 0, jnp.where(t == tiles - 1, 2, 1))
                    w = [ycoef[which, c] for c in range(4)]
                    r = xd[var, t, own, :] + apply(w, lambda k: shifted[j][k])
                    res_ref[var, t, own, :] = r
                    acc = acc + adjoint[var, own, pl.ds(pl.multiple_of(t * LANES, LANES), LANES)] * r
        return acc

    acc = lax.fori_loop(0, tiles // CHUNK, body, jnp.zeros((SUB, LANES), F32))
    last = tiles - 1
    weight = jnp.where(tile_iota(1) == LANES - 1, penalty, 0.0)
    for rt in range(row_tiles):
        own = slice(rt * SUB, (rt + 1) * SUB)
        for var, x in enumerate(load_state(refs, rt, last)):
            extra = weight * x
            res_ref[var, last, own, :] = res_ref[var, last, own, :] + extra
            acc = acc + adjoint[var, own, last * LANES:] * extra
    sum_ref[...] = acc


def border_kernel(partners, counts, orient, chip, across, slots, res, adjoint, total, out_ref, sum_ref):
    rows, cols = adjoint.shape[1:]
    row_tiles, tiles = rows // SUB, cols // LANES
    odd = lax.rem(lax.axis_index("line"), 2) == 1

    def body(t, acc):
        at = pl.ds(pl.multiple_of(t * LANES, LANES), LANES)
        near = [chip[n, :, at] for n in range(4)]
        far = [across[n, :, at] for n in range(4)]
        below = unpack([jnp.where(odd, a, b) for a, b in zip(near, far)], True)
        above = unpack([jnp.where(odd, b, a) for a, b in zip(near, far)], False)
        for var in range(5):
            for rt in range(row_tiles):
                own = slice(rt * SUB, (rt + 1) * SUB)
                r = res[var, t, own, :]
                for there, extra in ((0, below[var]), (row_tiles - 1, above[var])):
                    if rt == there:
                        r = r + extra
                        acc = acc + adjoint[var, own, at] * extra
                out_ref[var, own, at] = r
        return acc

    acc = lax.fori_loop(0, tiles, body, total[...], unroll=2)

    width = slot_width(row_tiles)
    per = LANES // width
    lane = tile_iota(1)
    count = counts[0]
    share = 1.0 / jnp.full((SUB, LANES), count).astype(F32)
    flipped = (lane % width) // row_tiles == 2
    target = jnp.zeros((SUB, LANES), F32)
    for n in range(slots.shape[0]):
        weight = jnp.zeros((SUB, LANES), F32)
        for k in range(partners.shape[1]):
            turn = 1.0 - 2.0 * jnp.full((SUB, LANES), orient[0, k]).astype(F32)
            hit = (lane // width + n * per == partners[0, k]) & (k < count)
            weight = weight + jnp.where(hit, share * jnp.where(flipped, turn, 1.0), 0.0)
        target = target + weight * slots[n]
    step = width
    while step < LANES:
        target = target + pltpu.roll(target, step, 1)
        step *= 2
    for var in range(5):
        for rt in range(row_tiles):
            own = slice(rt * SUB, (rt + 1) * SUB)
            moved = pltpu.roll(target, LANES - 1 - (var * row_tiles + rt), 1)
            extra = jnp.where(lane == LANES - 1, -penalty * moved, 0.0)
            cut = slice((tiles - 1) * LANES, tiles * LANES)
            out_ref[var, own, cut] = out_ref[var, own, cut] + extra
            acc = acc + adjoint[var, own, cut] * extra
    sum_ref[...] = jnp.full((SUB, LANES), jnp.sum(acc))


def per_device(density, momentum, energy, adjoint, partners, counts, orient):
    rows, cols = density.shape[1:]
    row_tiles, tiles = rows // SUB, cols // LANES
    lines, blocks = lax.axis_size("line"), lax.axis_size("blk")
    state = (density[0], momentum[0], energy[0])
    shape = jax.ShapeDtypeStruct
    pieces = -(-blocks * slot_width(row_tiles) // LANES)
    packed = shape((4, SUB, cols), F32)

    def pack(is_across):
        outs = [packed, shape((pieces, SUB, LANES), F32)] if is_across else [packed]
        return pl.pallas_call(
            functools.partial(pack_kernel, is_across), out_shape=outs,
            in_specs=[whole()] * 3, out_specs=[whole()] * len(outs), compiler_params=params(),
            cost_estimate=pl.CostEstimate(flops=10**6, bytes_accessed=3 * 10**6, transcendentals=0),
        )(*state)

    send_far, slots = pack(True)
    (send_near,) = pack(False)
    far = lax.ppermute(send_far, "line", [p for i in range(1, lines - 1, 2) for p in ((i, i + 1), (i + 1, i))])
    near = lax.ppermute(send_near, "line", [(i, i ^ 1) for i in range(lines)])
    hop = 1
    while hop < blocks:
        slots = slots + lax.ppermute(slots, "blk", [(i, i ^ hop) for i in range(blocks)])
        hop *= 2

    fy, xd = pl.pallas_call(
        flux_kernel,
        out_shape=[shape((5, tiles + 2, rows, LANES), F32), shape((5, tiles, rows, LANES), F32)],
        in_specs=[whole()] * 3, out_specs=[whole()] * 2,
        scratch_shapes=[
            pltpu.VMEM((4, tiles + 2, rows + 2 * SUB, LANES), F32),
            pltpu.VMEM((tiles, rows, LANES), F32),
            pltpu.VMEM((CHUNK, 5, rows + SUB, LANES), F32),
            pltpu.VMEM((2, row_tiles + 1, 4, SUB, LANES), F32),
            pltpu.VMEM((3, 4, SUB, LANES), F32),
        ],
        compiler_params=params(),
        cost_estimate=pl.CostEstimate(flops=10**8, bytes_accessed=10**7, transcendentals=0),
    )(*state)
    res, total = pl.pallas_call(
        volume_kernel,
        out_shape=[shape((5, tiles, rows, LANES), F32), shape((SUB, LANES), F32)],
        in_specs=[whole()] * 6, out_specs=[whole()] * 2,
        scratch_shapes=[pltpu.VMEM((3, 4, SUB, LANES), F32)],
        compiler_params=params(),
        cost_estimate=pl.CostEstimate(flops=10**8, bytes_accessed=10**7, transcendentals=0),
    )(*state, adjoint[0], fy, xd)
    smem = pl.BlockSpec(memory_space=pltpu.SMEM)
    result, part = pl.pallas_call(
        border_kernel,
        out_shape=[shape((5, rows, cols), F32), shape((SUB, LANES), F32)],
        in_specs=[smem] * 3 + [whole()] * 6, out_specs=[whole()] * 2,
        compiler_params=params(),
        cost_estimate=pl.CostEstimate(flops=10**6, bytes_accessed=4 * 10**6, transcendentals=0),
    )(partners, counts, orient, near, far, slots, res, adjoint[0], total)
    whole_sum = part
    if lines <= 4:
        for s in range(1, lines):
            whole_sum = whole_sum + lax.ppermute(part, "line", [(i, (i + s) % lines) for i in range(lines)])
    else:
        whole_sum = lax.psum(part, "line")
    correction = whole_sum[0, 0:1] / (rows * lines * cols)
    return result[None], correction


def solution(mesh):
    return jax.shard_map(
        per_device,
        mesh=mesh,
        in_specs=(
            P("blk", "line", None),
            P("blk", None, "line", None),
            P("blk", "line", None),
            P("blk", None, "line", None),
            P("blk", None),
            P("blk"),
            P("blk", None),
        ),
        out_specs=(P("blk", None, "line", None), P("blk")),
        check_vma=False,
    )
```

time: 213 us -> 35.3 us (0.17)
  local copies, waits for them, and re-layouts: 84.1 us -> 3.55 us
  other arithmetic: 61.9 us -> 0.02 us
  blocking collectives: 31.9 us -> 0 us
  Pallas kernels: 0 us -> 10.9 us
  waiting for transfers between devices: 14.8 us -> 4.26 us
    unnamed x22 -> x12, local copies, waits for them, and re-layouts: 39.8 us -> 3.04 us
    unnamed x1 -> x0, other arithmetic: 34.3 us -> none
    all_gather x1 -> x0, blocking collectives: 25.3 us -> none  [per_device(): gathered = lax.all_gather(bottom_row, 'blk', axis=0, tiled=True)]
    all_to_all x5 -> x0, local copies, waits for them, and re-layouts: 24.4 us -> none  [the longest x3 22.7 us: per_device(): lax.all_to_all(state, 'line', split_axis=3, concat_axis=2, tiled=True)]
    concatenate x2 -> x0, local copies, waits for them, and re-layouts: 14.9 us -> none  [the longest x1 14.9 us: per_device(): jnp.concatenate([density[:, None], momentum, energy[:, None]], axis=1)]
    all_to_all x2 -> x0, starting transfers between devices: 14.9 us -> none  [the longest x1 10.7 us: per_device(): lax.all_to_all(line_part, 'line', split_axis=2, concat_axis=3, tiled=True)]
    all_to_all x2 -> x0, waiting for transfers between devices: 14.8 us -> none  [the longest x1 14.8 us: per_device(): lax.all_to_all(line_part, 'line', split_axis=2, concat_axis=3, tiled=True)]
    ppermute x0 -> x8, starting transfers between devices: none -> 13.2 us  [the longest x3 4.98 us: per_device(): lax.ppermute(slots, 'blk', [(i, i ^ hop) for i in range(blocks)])]
  transfers between devices with their start and end apart: 2 -> 8, of which waited for: 1 -> 3; matrix products, arithmetic and copies ran while one was open for 6% -> 0% of each run, Pallas kernels for 0% -> 22%
where the time goes in v1:
time: 35.3 us; the launch traced here: 35 us
  starting transfers between devices  13.2 us (37%)
  Pallas kernels  10.9 us (31%)
  waiting for transfers between devices  4.26 us (12%)
  local copies, waits for them, and re-layouts  3.55 us (10%)
  between operations  3.18 us (9%)
    ppermute x3, starting transfers between devices, per_device(): lax.ppermute(slots, 'blk', [(i, i ^ hop) for i in range(blocks)])  4.98 us
    ppermute x1, starting transfers between devices, per_device(): lax.ppermute(send_far, 'line', [p for i in range(1, lines - 1, 2) for p i...  4.63 us
    pallas_call x1, Pallas kernels, per_device(): pl.pallas_call(flux_kernel, out_shape=[shape((5, tiles + 2, rows, LANES),...  3.67 us
    ppermute x3, starting transfers between devices, per_device(): lax.ppermute(part, 'line', [(i, (i + s) % lines) for i in range(lines)])  3.49 us
    pallas_call x1, Pallas kernels, per_device(): pl.pallas_call(volume_kernel, out_shape=[shape((5, tiles, rows, LANES), F...  3.16 us
    unnamed x12, local copies, waits for them, and re-layouts  3.04 us
    ppermute x3, waiting for transfers between devices, per_device(): lax.ppermute(part, 'line', [(i, (i + s) % lines) for i in range(lines)])  3.03 us
    pallas_call x1, Pallas kernels, per_device(): pl.pallas_call(border_kernel, out_shape=[shape((5, rows, cols), F32), sha...  2.47 us
  transfers between devices with their start and end apart: 8, of which 3 were waited for; matrix products, arithmetic and copies ran while one was open for 0% of the time, Pallas kernels for 22%

profile of v1, /device:TPU:1, one launch (start us, length us, event | category | flops | bytes accessed | tf_op | source)
XLA Modules:
  0.0 35.0 jit_solution(6594532159002455662)
XLA Ops:
  0.6 0.0 copy-start
  0.6 1.1 %copy-done = f32[1,3,16,4096]{3,2,1,0:T(8,128)S(1)} copy-done((f32[1,3,16,4096]{3,2,1,0:T(8,128)S(1)}, f32[1,3,16,4096]{3,2,1,0:T(8,128)}, u32[]{:S(2)}) %copy-start) | copy-done | bytes 786456
  1.8 0.0 copy-start.2
  1.8 0.9 %copy-done.2 = f32[1,16,4096]{2,1,0:T(8,128)S(1)} copy-done((f32[1,16,4096]{2,1,0:T(8,128)S(1)}, f32[1,16,4096]{2,1,0:T(8,128)}, u32[]{:S(2)}) %copy-start.2) | copy-done | bytes 262168
  2.7 0.0 copy-start.3
  2.7 0.9 %copy-done.3 = f32[1,16,4096]{2,1,0:T(8,128)S(1)} copy-done((f32[1,16,4096]{2,1,0:T(8,128)S(1)}, f32[1,16,4096]{2,1,0:T(8,128)}, u32[]{:S(2)}) %copy-start.3) | copy-done | bytes 262168
  3.7 0.8 %shard_map.87 = (f32[4,8,4096]{2,1,0:T(8,128)S(1)}, f32[1,8,128]{2,1,0:T(8,128)S(1)}) custom-call(f32[16,4096]{1,0:T(8,128)S(1)} %bitcast.12, f32[3,16,4096]{2,1,0:T(8,128)S(1)} %bitcast.6, f32[16,4096]{1,0:T(8,128)S(1)} %bitcast.16), custom_call_target="tpu_custom_call" | custom-call | flops 1000000 | bytes 3000000 | tf_op jit(solution)/shard_map/pallas_call | solution.py:378
  4.5 0.0 copy-start.1
  4.5 4.6 %collective-permute-start.1 = (f32[4,8,4096]{2,1,0:T(8,128)S(1)}, f32[4,8,4096]{2,1,0:T(8,128)S(1)}, u32[]{:S(2)}, u32[]{:S(2)}) collective-permute-start(f32[4,8,4096]{2,1,0:T(8,128)S(1)} %get-tuple-element.10), channel_id=1, source_target_pairs={{1,2},{2,1},{5,6},{6,5},{9,10},{10,9},{13,14},{14,13},{17,18},{18,... | collective-permute-start | bytes 1572872 | tf_op jit(solution)/shard_map/ppermute | solution.py:386
  9.1 0.8 %shard_map.86 = f32[4,8,4096]{2,1,0:T(8,128)S(1)} custom-call(f32[16,4096]{1,0:T(8,128)S(1)} %bitcast.13, f32[3,16,4096]{2,1,0:T(8,128)S(1)} %bitcast.7, f32[16,4096]{1,0:T(8,128)S(1)} %bitcast.17), custom_call_target="tpu_custom_call" | custom-call | flops 1000000 | bytes 3000000 | tf_op jit(solution)/shard_map/pallas_call | solution.py:378
  9.9 0.1 collective-permute-start
  10.0 1.3 %collective-permute-start.2 = (f32[1,8,128]{2,1,0:T(8,128)S(1)}, f32[1,8,128]{2,1,0:T(8,128)S(1)}, u32[]{:S(2)}, u32[]{:S(2)}) collective-permute-start(f32[1,8,128]{2,1,0:T(8,128)S(1)} %get-tuple-element.11), channel_id=1, source_target_pairs={{0,4},{4,0},{8,12},{12,8},{16,20},{20,16},{24,28},{28,24},{1,5},{5... | collective-permute-start | bytes 12296 | tf_op jit(solution)/shard_map/ppermute | solution.py:390
  11.3 1.2 %collective-permute-done.2 = f32[1,8,128]{2,1,0:T(8,128)S(1)} collective-permute-done((f32[1,8,128]{2,1,0:T(8,128)S(1)}, f32[1,8,128]{2,1,0:T(8,128)S(1)}, u32[]{:S(2)}, u32[]{:S(2)}) %collective-permute-start.2) | collective-permute-done | bytes 4128 | tf_op jit(solution)/shard_map/ppermute | solution.py:390
  12.5 1.3 %collective-permute-start.3 = (f32[1,8,128]{2,1,0:T(8,128)S(1)}, f32[1,8,128]{2,1,0:T(8,128)S(1)}, u32[]{:S(2)}, u32[]{:S(2)}) collective-permute-start(f32[1,8,128]{2,1,0:T(8,128)S(1)} %add.18), channel_id=1, source_target_pairs={{0,8},{4,12},{8,0},{12,4},{16,24},{20,28},{24,16},{28,20},{1,9},{5... | collective-permute-start | bytes 12296 | tf_op jit(solution)/shard_map/ppermute | solution.py:390
  13.8 3.7 %shard_map.88 = (f32[5,34,16,128]{3,2,1,0:T(8,128)S(1)}, f32[5,32,16,128]{3,2,1,0:T(8,128)S(1)}) custom-call(f32[16,4096]{1,0:T(8,128)S(1)} %bitcast.14, f32[3,16,4096]{2,1,0:T(8,128)S(1)} %bitcast.8, f32[16,4096]{1,0:T(8,128)S(1)} %bitcast.18), custom_call_target="tpu_custom_call" | custom-call | flops 100000000 | bytes 10000000 | tf_op jit(solution)/shard_map/pallas_call | solution.py:393
  17.5 0.0 collective-permute-done.3
  17.5 2.4 %collective-permute-start.4 = (f32[1,8,128]{2,1,0:T(8,128)S(1)}, f32[1,8,128]{2,1,0:T(8,128)S(1)}, u32[]{:S(2)}, u32[]{:S(2)}) collective-permute-start(f32[1,8,128]{2,1,0:T(8,128)S(1)} %add.19), channel_id=1, source_target_pairs={{0,16},{4,20},{8,24},{12,28},{16,0},{20,4},{24,8},{28,12},{1,17},{... | collective-permute-start | bytes 12296 | tf_op jit(solution)/shard_map/ppermute | solution.py:390
  19.9 0.0 copy-done.1
  19.9 0.0 copy-start.4
  19.9 0.0 copy-start.5
  19.9 3.2 %shard_map.89 = (f32[5,32,16,128]{3,2,1,0:T(8,128)S(1)}, f32[8,128]{1,0:T(8,128)S(1)}) custom-call(f32[16,4096]{1,0:T(8,128)S(1)} %bitcast.15, f32[3,16,4096]{2,1,0:T(8,128)S(1)} %bitcast.9, f32[16,4096]{1,0:T(8,128)S(1)} %bitcast.19, f32[5,16,4096]{2,1,0:T(8,128)S(1)} %bitcast.10, f32[5,34,16,128]{3,2,1,0:T(8,128)S(1)} %get-tuple-element.12.fy, ...), custom_call_target="tpu_custom_call" | custom-call | flops 100000000 | bytes 10000000 | tf_op jit(solution)/shard_map/pallas_call | solution.py:407
  23.7 0.0 collective-permute-done.4
  23.7 0.0 collective-permute-done.1.across
  23.7 0.0 collective-permute-done.chip
  23.7 0.0 copy-done.4
  23.7 0.0 copy-done.5
  23.7 2.5 %shard_map.90 = (f32[5,16,4096]{2,1,0:T(8,128)}, f32[8,128]{1,0:T(8,128)S(1)}) custom-call(s32[1,4]{1,0:T(1,128)S(1)} %copy-done.4, s32[1]{0:T(128)S(6)} %copy.9.counts, s32[1,4]{1,0:T(1,128)S(1)} %copy-done.5, f32[4,8,4096]{2,1,0:T(8,128)S(1)} %collective-permute-done.chip, f32[4,8,4096]{2,1,0:T(8,128)S(1)} %collective-permute-done.1.across, ...), custom_call_target="tpu_custom_call" | custom-call | flops 1000000 | bytes 4000000 | tf_op jit(solution)/shard_map/pallas_call | solution.py:416
  26.2 1.7 %collective-permute-start.5 = (f32[8,128]{1,0:T(8,128)S(1)}, f32[8,128]{1,0:T(8,128)S(1)}, u32[]{:S(2)}, u32[]{:S(2)}) collective-permute-start(f32[8,128]{1,0:T(8,128)S(1)} %get-tuple-element.17), channel_id=1, source_target_pairs={{0,1},{1,2},{2,3},{3,0},{4,5},{5,6},{6,7},{7,4},{8,9},{9,10},{10,1... | collective-permute-start | bytes 12296 | tf_op jit(solution)/shard_map/ppermute | solution.py:426
  27.9 1.8 %collective-permute-start.6 = (f32[8,128]{1,0:T(8,128)S(1)}, f32[8,128]{1,0:T(8,128)S(1)}, u32[]{:S(2)}, u32[]{:S(2)}) collective-permute-start(f32[8,128]{1,0:T(8,128)S(1)} %get-tuple-element.17), channel_id=1, source_target_pairs={{0,2},{1,3},{2,0},{3,1},{4,6},{5,7},{6,4},{7,5},{8,10},{9,11},{10,... | collective-permute-start | bytes 12296 | tf_op jit(solution)/shard_map/ppermute | solution.py:426
  29.7 0.0 collective-permute-start.7
  29.7 0.0 collective-permute-done.5
  29.7 1.3 %collective-permute-done.6 = f32[8,128]{1,0:T(8,128)S(1)} collective-permute-done((f32[8,128]{1,0:T(8,128)S(1)}, f32[8,128]{1,0:T(8,128)S(1)}, u32[]{:S(2)}, u32[]{:S(2)}) %collective-permute-start.6) | collective-permute-done | bytes 4128 | tf_op jit(solution)/shard_map/ppermute | solution.py:426
  31.0 1.7 %collective-permute-done.7 = f32[8,128]{1,0:T(8,128)S(1)} collective-permute-done((f32[8,128]{1,0:T(8,128)S(1)}, f32[8,128]{1,0:T(8,128)S(1)}, u32[]{:S(2)}, u32[]{:S(2)}) %collective-permute-start.7) | collective-permute-done | bytes 4128 | tf_op jit(solution)/shard_map/ppermute | solution.py:426
  32.8 0.5 %slice.3 = f32[1,1]{1,0:T(1,128)} slice(f32[8,128]{1,0:T(8,128)S(1)} %add_add_fusion), slice={[0:1], [0:1]} | slice | bytes 8 | tf_op jit(solution)/shard_map/slice | solution.py:429
  (4 shorter events, 0.0 us)
Async XLA Ops:
  0.6 1.1 %copy-start = (f32[1,3,16,4096]{3,2,1,0:T(8,128)S(1)}, f32[1,3,16,4096]{3,2,1,0:T(8,128)}, u32[]{:S(2)}) copy-start(f32[1,3,16,4096]{3,2,1,0:T(8,128)} %param.8) | copy-start | bytes 2359300
  1.8 0.9 %copy-start.2 = (f32[1,16,4096]{2,1,0:T(8,128)S(1)}, f32[1,16,4096]{2,1,0:T(8,128)}, u32[]{:S(2)}) copy-start(f32[1,16,4096]{2,1,0:T(8,128)} %param.7) | copy-start | bytes 786436
  2.7 0.9 %copy-start.3 = (f32[1,16,4096]{2,1,0:T(8,128)S(1)}, f32[1,16,4096]{2,1,0:T(8,128)}, u32[]{:S(2)}) copy-start(f32[1,16,4096]{2,1,0:T(8,128)} %param.9) | copy-start | bytes 786436
  4.5 15.4 %copy-start.1 = (f32[1,5,16,4096]{3,2,1,0:T(8,128)S(1)}, f32[1,5,16,4096]{3,2,1,0:T(8,128)}, u32[]{:S(2)}) copy-start(f32[1,5,16,4096]{3,2,1,0:T(8,128)} %param.10) | copy-start | bytes 3932164
  4.5 19.2 %collective-permute-start.1 = (f32[4,8,4096]{2,1,0:T(8,128)S(1)}, f32[4,8,4096]{2,1,0:T(8,128)S(1)}, u32[]{:S(2)}, u32[]{:S(2)}) collective-permute-start(f32[4,8,4096]{2,1,0:T(8,128)S(1)} %get-tuple-element.10), channel_id=1, source_target_pairs={{1,2},{2,1},{5,6},{6,5},{9,10},{10,9},{13,14},{14,13},{17,18},{18,... | collective-permute-start | bytes 1572872 | tf_op jit(solution)/shard_map/ppermute | solution.py:386
  9.9 13.8 %collective-permute-start = (f32[4,8,4096]{2,1,0:T(8,128)S(1)}, f32[4,8,4096]{2,1,0:T(8,128)S(1)}, u32[]{:S(2)}, u32[]{:S(2)}) collective-permute-start(f32[4,8,4096]{2,1,0:T(8,128)S(1)} %shard_map.86), channel_id=1, source_target_pairs={{0,1},{1,0},{2,3},{3,2},{4,5},{5,4},{6,7},{7,6},{8,9},{9,8},{10,11... | collective-permute-start | bytes 1572872 | tf_op jit(solution)/shard_map/ppermute | solution.py:387
  10.0 2.5 %collective-permute-start.2 = (f32[1,8,128]{2,1,0:T(8,128)S(1)}, f32[1,8,128]{2,1,0:T(8,128)S(1)}, u32[]{:S(2)}, u32[]{:S(2)}) collective-permute-start(f32[1,8,128]{2,1,0:T(8,128)S(1)} %get-tuple-element.11), channel_id=1, source_target_pairs={{0,4},{4,0},{8,12},{12,8},{16,20},{20,16},{24,28},{28,24},{1,5},{5... | collective-permute-start | bytes 12296 | tf_op jit(solution)/shard_map/ppermute | solution.py:390
  12.5 5.0 %collective-permute-start.3 = (f32[1,8,128]{2,1,0:T(8,128)S(1)}, f32[1,8,128]{2,1,0:T(8,128)S(1)}, u32[]{:S(2)}, u32[]{:S(2)}) collective-permute-start(f32[1,8,128]{2,1,0:T(8,128)S(1)} %add.18), channel_id=1, source_target_pairs={{0,8},{4,12},{8,0},{12,4},{16,24},{20,28},{24,16},{28,20},{1,9},{5... | collective-permute-start | bytes 12296 | tf_op jit(solution)/shard_map/ppermute | solution.py:390
  17.5 6.2 %collective-permute-start.4 = (f32[1,8,128]{2,1,0:T(8,128)S(1)}, f32[1,8,128]{2,1,0:T(8,128)S(1)}, u32[]{:S(2)}, u32[]{:S(2)}) collective-permute-start(f32[1,8,128]{2,1,0:T(8,128)S(1)} %add.19), channel_id=1, source_target_pairs={{0,16},{4,20},{8,24},{12,28},{16,0},{20,4},{24,8},{28,12},{1,17},{... | collective-permute-start | bytes 12296 | tf_op jit(solution)/shard_map/ppermute | solution.py:390
  19.9 3.9 %copy-start.4 = (s32[1,4]{1,0:T(1,128)S(1)}, s32[1,4]{1,0:T(1,128)}, u32[]{:S(2)}) copy-start(s32[1,4]{1,0:T(1,128)} %partners.1) | copy-start | bytes 52
  19.9 3.9 %copy-start.5 = (s32[1,4]{1,0:T(1,128)S(1)}, s32[1,4]{1,0:T(1,128)}, u32[]{:S(2)}) copy-start(s32[1,4]{1,0:T(1,128)} %orient.1) | copy-start | bytes 52
  26.2 3.5 %collective-permute-start.5 = (f32[8,128]{1,0:T(8,128)S(1)}, f32[8,128]{1,0:T(8,128)S(1)}, u32[]{:S(2)}, u32[]{:S(2)}) collective-permute-start(f32[8,128]{1,0:T(8,128)S(1)} %get-tuple-element.17), channel_id=1, source_target_pairs={{0,1},{1,2},{2,3},{3,0},{4,5},{5,6},{6,7},{7,4},{8,9},{9,10},{10,1... | collective-permute-start | bytes 12296 | tf_op jit(solution)/shard_map/ppermute | solution.py:426
  27.9 3.1 %collective-permute-start.6 = (f32[8,128]{1,0:T(8,128)S(1)}, f32[8,128]{1,0:T(8,128)S(1)}, u32[]{:S(2)}, u32[]{:S(2)}) collective-permute-start(f32[8,128]{1,0:T(8,128)S(1)} %get-tuple-element.17), channel_id=1, source_target_pairs={{0,2},{1,3},{2,0},{3,1},{4,6},{5,7},{6,4},{7,5},{8,10},{9,11},{10,... | collective-permute-start | bytes 12296 | tf_op jit(solution)/shard_map/ppermute | solution.py:426
  29.7 3.0 %collective-permute-start.7 = (f32[8,128]{1,0:T(8,128)S(1)}, f32[8,128]{1,0:T(8,128)S(1)}, u32[]{:S(2)}, u32[]{:S(2)}) collective-permute-start(f32[8,128]{1,0:T(8,128)S(1)} %get-tuple-element.17), channel_id=1, source_target_pairs={{0,3},{1,0},{2,1},{3,2},{4,7},{5,4},{6,5},{7,6},{8,11},{9,8},{10,9... | collective-permute-start | bytes 12296 | tf_op jit(solution)/shard_map/ppermute | solution.py:426

commit v2 on v1

v2 whole, which is shorter than its diff:
```python
import jax
import jax.numpy as jnp
from jax import lax
from jax.experimental import pallas as pl
from jax.experimental.pallas import tpu as pltpu
from jax.sharding import PartitionSpec as P


STENCIL = (0.75, -0.15, 1.0 / 60.0)
gamma_less = 0.4
viscosity = 0.5
conduction = 1.5
penalty = 4.0
LANES = 128
SUB = 8
CHUNK = 4
WIDE = 4
F32 = jnp.float32
VMEM_LIMIT = 20 * 1024 * 1024

_ONE = {k: STENCIL[k - 1] for k in (1, 2, 3)}
_ONE.update({-k: -STENCIL[k - 1] for k in (1, 2, 3)})
TWICE = [sum(_ONE[a] * _ONE[b] for a in _ONE for b in _ONE if a + b == m) for m in range(7)]


def tile_iota(axis):
    return lax.broadcasted_iota(jnp.int32, (SUB, LANES), axis)


def coefficients(index, extent):
    inside = (index >= 0) & (index < extent)
    end = (index == 0) | (index == extent - 1)
    second = (index == 1) | (index == extent - 2)
    fourth = (index == 2) | (index == extent - 3)
    one = jnp.where(fourth, 2.0 / 3.0, jnp.where(second, 0.5, jnp.where(end, 1.0, STENCIL[0])))
    two = jnp.where(fourth, -1.0 / 12.0, jnp.where(second | end, 0.0, STENCIL[1]))
    three = jnp.where(fourth | second | end, 0.0, STENCIL[2])
    point = jnp.where(index == 0, -1.0, jnp.where(index == extent - 1, 1.0, 0.0))
    return [jnp.where(inside, c, 0.0).astype(F32) for c in (one, two, three, point)]


def load_state(refs, rt, t):
    density, momentum, energy = refs
    rows = slice(rt * SUB, (rt + 1) * SUB)
    cols = pl.ds(t * LANES if isinstance(t, int) else pl.multiple_of(t * LANES, LANES), LANES)
    return [density[rows, cols]] + [momentum[a, rows, cols] for a in range(3)] + [energy[rows, cols]]


def primitive_of(state):
    rho, m0, m1, m2, e = state
    inv = 1.0 / rho
    u = [m0 * inv, m1 * inv, m2 * inv]
    p = gamma_less * (e - 0.5 * (m0 * u[0] + m1 * u[1] + m2 * u[2]))
    return u, p, p * inv


def convective(state, u, p, d):
    n = u[d]
    out = [state[1 + d]]
    for a in range(3):
        f = state[1 + a] * n
        out.append(f + p if a == d else f)
    out.append((state[4] + p) * n)
    return out


def contribution(state, up):
    u, p, temp = primitive_of(state)
    conv = convective(state, u, p, 0)
    row = tile_iota(0)
    shift = (lambda x, m: pltpu.roll(x, m, 0)) if up else (lambda x, m: pltpu.roll(x, SUB - m, 0))
    sign = -1.0 if up else 1.0
    keep = [None] + [(row < m) if up else (row >= SUB - m) for m in range(1, 7)]
    out = []
    for var in range(5):
        acc = None
        for m in (1, 2, 3):
            term = shift(conv[var], m) * jnp.where(keep[m], sign * STENCIL[m - 1], 0.0)
            acc = term if acc is None else acc + term
        if var:
            prim = u[var - 1] if var < 4 else temp
            scale = -viscosity * (conduction if var == 4 else 1.0)
            for m in range(1, 7):
                acc = acc + shift(prim, m) * jnp.where(keep[m], scale * TWICE[m], 0.0)
        out.append(acc)
    mass, first, second = out[0], out[1], out[2]
    if up:
        first = jnp.where(row >= 6, pltpu.roll(mass, 6, 0), first)
        second = jnp.where(row == 6, pltpu.roll(mass, 4, 0), second)
    else:
        first = jnp.where(row < 2, pltpu.roll(mass, 3, 0), first)
        second = jnp.where(row == 0, pltpu.roll(mass, 1, 0), second)
    return [first, second, out[3], out[4]]


def unpack(tiles, up):
    row = tile_iota(0)
    first, second, third, fourth = tiles
    if up:
        mass = jnp.where(row < 2, pltpu.roll(first, 2, 0), 0.0) + jnp.where(row == 2, pltpu.roll(second, 4, 0), 0.0)
        keep = row < 6
    else:
        mass = jnp.where((row == 5) | (row == 6), pltpu.roll(first, 5, 0), 0.0) + jnp.where(
            row == 7, pltpu.roll(second, 7, 0), 0.0)
        keep = row >= 2
    return [mass] + [jnp.where(keep, x, 0.0) for x in (first, second, third, fourth)]


def side_of(refs, up, out_ref, rt, first, last):
    def body(t, carry):
        cols = pl.ds(pl.multiple_of(t * LANES, LANES), LANES)
        for n, x in enumerate(contribution(load_state(refs, rt, t), up)):
            out_ref[n, :, cols] = x
        return carry

    lax.fori_loop(first, last, body, 0, unroll=2)


def by_parity(up_when, run):
    odd = lax.rem(lax.axis_index("line"), 2)

    @pl.when(odd == up_when)
    def _():
        run(True)

    @pl.when(odd != up_when)
    def _():
        run(False)


def pack_kernel(density, momentum, energy, out_ref, slots, buf, other, sems):
    rows, cols = density.shape
    row_tiles, tiles = rows // SUB, cols // LANES
    up = lax.rem(lax.axis_index("line"), 2) == 1
    mine = jnp.where(up, row_tiles - 1, 0)
    sources = [density] + [momentum.at[a] for a in range(3)] + [energy]
    halves = 2
    part = cols // halves
    copies = []
    for h in range(halves):
        for n, x in enumerate(sources):
            at = pl.ds(pl.multiple_of(mine * SUB, SUB), SUB)
            copies.append(pltpu.make_async_copy(
                x.at[at, pl.ds(h * part, part)], buf.at[n, :, pl.ds(h * part, part)], sems.at[h, n]))
    bottom = [pltpu.make_async_copy(x.at[:, pl.ds(0, LANES)], other.at[n], sems.at[halves, n])
              for n, x in enumerate(sources)]
    for c in copies + bottom:
        c.start()

    refs = (buf.at[0], buf.at[1:4], buf.at[4])
    for h in range(halves):
        for c in copies[h * 5:(h + 1) * 5]:
            c.wait()
        by_parity(1, lambda up_side: side_of(refs, up_side, out_ref, 0, h * tiles // halves, (h + 1) * tiles // halves))

    for c in bottom:
        c.wait()
    width = slot_width(row_tiles)
    per = LANES // width
    block = lax.axis_index("blk")
    lane = tile_iota(1)
    base = lax.rem(block, per) * width
    value = jnp.zeros((SUB, LANES), F32)
    for rt in range(row_tiles):
        for var in range(5):
            x = other[var, rt * SUB:(rt + 1) * SUB, 0:1]
            value = jnp.where(lane == base + (var * row_tiles + rt), x, value)
    for n in range(slots.shape[0]):
        slots[n] = jnp.where(block // per == n, value, 0.0)


def slot_width(row_tiles):
    width = 1
    while width < 5 * row_tiles:
        width *= 2
    return width


def whole():
    return pl.BlockSpec(memory_space=pltpu.VMEM)


def params():
    return pltpu.CompilerParams(vmem_limit_bytes=VMEM_LIMIT)


def lane_weights(ref, cols):
    for n, start in enumerate((0, LANES, cols - LANES)):
        at = start + tile_iota(1)
        one, _, _, point = coefficients(at, cols)
        for c, w in enumerate((one, point)
                              + tuple(coefficients(at - 2, cols)[1:3]) + tuple(coefficients(at + 2, cols)[1:3])):
            ref[n, c] = w


def lane_difference(tiles, weights):
    lane = tile_iota(1)
    count = len(tiles) - 2

    def shift(values, k):
        return [pltpu.roll(x, (LANES - k) % LANES, 1) for x in values]

    ahead = shift(tiles[1:], 1)
    behind = shift(tiles[:-1], -1)
    plus = [jnp.where(lane < LANES - 1, ahead[j], ahead[j + 1]) for j in range(count)]
    minus = [jnp.where(lane >= 1, behind[j + 1], behind[j]) for j in range(count)]
    far = [weights(j + 1, 2) * v + weights(j + 1, 3) * p
           for j, (v, p) in enumerate(zip(tiles[1:], plus + [ahead[count]]))]
    back = [weights(j, 4) * v + weights(j, 5) * m for j, (v, m) in enumerate(zip(tiles[:-1], [behind[0]] + minus))]
    far, back = shift(far, 2), shift(back, -2)
    out = []
    for j in range(count):
        f = jnp.where(lane < LANES - 2, far[j], far[j + 1])
        b = jnp.where(lane >= 2, back[j + 1], back[j])
        out.append((weights(j + 1, 0) * (plus[j] - minus[j]) + weights(j + 1, 1) * tiles[j + 1]) + (f - b))
    return out


def weights_at(ref, t0, tiles):
    which = [jnp.where(t0 + j - 1 <= 0, 0, jnp.where(t0 + j - 1 >= tiles - 1, 2, 1)) for j in range(WIDE + 2)]
    return lambda j, c: ref[which[j], c]


def apply(weights, at):
    one, two, three, point = weights
    return one * (at(1) - at(-1)) + two * (at(2) - at(-2)) + three * (at(3) - at(-3)) + point * at(0)


def interior(at):
    one, two, three = STENCIL
    return one * (at(1) - at(-1)) + two * (at(2) - at(-2)) + three * (at(3) - at(-3))


def first_kernel(density, momentum, energy, lists,
                 prim, press, xd_ref, near_ref, mix_ref, fx, xcoef):
    refs = (density, momentum, energy)
    rows, cols = density.shape
    row_tiles, tiles = rows // SUB, cols // LANES
    line = lax.axis_index("line")
    extent = rows * lax.axis_size("line")
    zero = jnp.zeros((SUB, LANES), F32)
    for g in range(row_tiles + 1):
        for c, w in enumerate(coefficients(line * rows - 3 + g * SUB + tile_iota(0), extent)):
            xcoef[0, g, c] = w
    for r in range(row_tiles):
        for c, w in enumerate(coefficients(line * rows + r * SUB + tile_iota(0), extent)):
            xcoef[1, r, c] = w
    for var in range(4):
        for r in range(row_tiles + 2):
            prim[var, 0, r * SUB:(r + 1) * SUB, :] = zero
            prim[var, tiles + 1, r * SUB:(r + 1) * SUB, :] = zero
    for j in range(CHUNK):
        for r in range(row_tiles + 1):
            fx[j, 0, r * SUB:(r + 1) * SUB, :] = zero

    def body(step, carry):
        for j in range(CHUNK):
            t = step * CHUNK + j
            flux = []
            for rt in range(row_tiles):
                state = load_state(refs, rt, t)
                u, p, temp = primitive_of(state)
                at = slice((rt + 1) * SUB, (rt + 2) * SUB)
                for var, x in enumerate(u + [temp]):
                    prim[var, t + 1, at, :] = x
                press[t, rt * SUB:(rt + 1) * SUB, :] = p
                flux.append(convective(state, u, p, 0))
            for var in range(4):
                prim[var, t + 1, 0:SUB, :] = zero
                prim[var, t + 1, (row_tiles + 1) * SUB:(row_tiles + 2) * SUB, :] = zero
            for var in range(4):
                scale = -viscosity * (conduction if var == 3 else 1.0)
                for g in range(row_tiles + 1):
                    base = SUB - 3 + g * SUB
                    at = lambda k: prim[var, t + 1, base + k:base + k + SUB, :]
                    if 0 < g < row_tiles:
                        d = interior(at)
                    else:
                        d = apply([xcoef[0, g, c] for c in range(4)], at)
                    fx[j, var + 1, g * SUB:(g + 1) * SUB, :] = scale * d
            for rt in range(row_tiles):
                place = slice(3 + rt * SUB, 3 + (rt + 1) * SUB)
                for var, f in enumerate(flux[rt]):
                    fx[j, var, place, :] = fx[j, var, place, :] + f if var else f
            for var in range(5):
                for rt in range(row_tiles):
                    w = [xcoef[1, rt, c] for c in range(4)]
                    base = 3 + rt * SUB
                    xd_ref[var, t, rt * SUB:(rt + 1) * SUB, :] = apply(
                        w, lambda k: fx[j, var, base + k:base + k + SUB, :])
        return carry

    lax.fori_loop(0, tiles // CHUNK, body, 0)
    by_parity(0, lambda up: side_of(refs, up, near_ref, row_tiles - 1 if up else 0, 0, tiles))

    width = slot_width(row_tiles)
    per = LANES // width
    lane = tile_iota(1)

    def spread(ref, k):
        return jnp.broadcast_to(ref[0:1, k:k + 1], (SUB, LANES))

    count = spread(lists, 0) >> 16
    share = 1.0 / count.astype(F32)
    flipped = (lane % width) // row_tiles == 2
    for n in range(mix_ref.shape[0]):
        weight = zero
        for k in range(lists.shape[1]):
            turn = 1.0 - 2.0 * (spread(lists, k) & 1).astype(F32)
            hit = (lane // width + n * per == ((spread(lists, k) >> 1) & 0x7FFF)) & (k < count)
            weight = weight + jnp.where(hit, share * jnp.where(flipped, turn, 1.0), 0.0)
        mix_ref[n] = weight


def second_kernel(density, momentum, energy, prim, press, fy_ref, edge):
    refs = (density, momentum, energy)
    rows, cols = density.shape
    row_tiles, tiles = rows // SUB, cols // LANES
    zero = jnp.zeros((SUB, LANES), F32)
    lane_weights(edge, cols)
    for var in range(5):
        for r in range(row_tiles):
            fy_ref[var, 0, r * SUB:(r + 1) * SUB, :] = zero
            fy_ref[var, tiles + 1, r * SUB:(r + 1) * SUB, :] = zero

    def store(rt, t, grads):
        at = slice((rt + 1) * SUB, (rt + 2) * SUB)
        own = slice(rt * SUB, (rt + 1) * SUB)
        u = [prim[a, t + 1, at, :] for a in range(3)]
        for var, f in enumerate(convective(load_state(refs, rt, t), u, press[t, own, :], 1)):
            scale = viscosity * (conduction if var == 4 else 1.0)
            fy_ref[var, t + 1, own, :] = f - scale * grads[var - 1] if var else f

    def body(step, carry):
        t0 = step * WIDE
        weights = weights_at(edge, t0, tiles)
        for rt in range(row_tiles):
            at = slice((rt + 1) * SUB, (rt + 2) * SUB)
            grads = [lane_difference([prim[var, t0 + j, at, :] for j in range(WIDE + 2)], weights) for var in range(4)]
            for j in range(WIDE):
                store(rt, t0 + j, [g[j] for g in grads])
        return carry

    lax.fori_loop(0, tiles // WIDE, body, 0)


def volume_kernel(density, momentum, energy, adjoint, fy, xd, res_ref, sum_ref, edge):
    refs = (density, momentum, energy)
    rows, cols = density.shape
    row_tiles, tiles = rows // SUB, cols // LANES
    lane_weights(edge, cols)

    def body(step, accs):
        t0 = step * WIDE
        accs = list(accs)
        weights = weights_at(edge, t0, tiles)
        for rt in range(row_tiles):
            own = slice(rt * SUB, (rt + 1) * SUB)
            for var in range(5):
                dy = lane_difference([fy[var, t0 + j, own, :] for j in range(WIDE + 2)], weights)
                for j in range(WIDE):
                    t = t0 + j
                    r = xd[var, t, own, :] + dy[j]
                    res_ref[var, t, own, :] = r
                    weighted = adjoint[var, own, pl.ds(pl.multiple_of(t * LANES, LANES), LANES)] * r
                    accs[j % len(accs)] = accs[j % len(accs)] + weighted
        return tuple(accs)

    zero = jnp.zeros((SUB, LANES), F32)
    accs = lax.fori_loop(0, tiles // WIDE, body, (zero,) * 4)
    acc = (accs[0] + accs[1]) + (accs[2] + accs[3])
    weight = jnp.where(tile_iota(1) == LANES - 1, penalty, 0.0)
    last = tiles - 1
    for rt in range(row_tiles):
        own = slice(rt * SUB, (rt + 1) * SUB)
        for var, x in enumerate(load_state(refs, rt, last)):
            extra = weight * x
            res_ref[var, last, own, :] = res_ref[var, last, own, :] + extra
            acc = acc + adjoint[var, own, last * LANES:] * extra
    sum_ref[...] = acc


def border_kernel(chip, across, slots, mix, res, adjoint, total, out_ref, sum_ref, stage, sems):
    rows, cols = adjoint.shape[1:]
    row_tiles, tiles = rows // SUB, cols // LANES
    odd = lax.rem(lax.axis_index("line"), 2) == 1

    def body(t, acc):
        at = pl.ds(pl.multiple_of(t * LANES, LANES), LANES)
        near = [chip[n, :, at] for n in range(4)]
        far = [across[n, :, at] for n in range(4)]
        below = unpack([jnp.where(odd, a, b) for a, b in zip(near, far)], True)
        above = unpack([jnp.where(odd, b, a) for a, b in zip(near, far)], False)
        for var in range(5):
            for rt in range(row_tiles):
                own = slice(rt * SUB, (rt + 1) * SUB)
                r = res[var, t, own, :]
                for there, extra in ((0, below[var]), (row_tiles - 1, above[var])):
                    if rt == there:
                        r = r + extra
                        acc = acc + adjoint[var, own, at] * extra
                stage[var, own, at] = r
        return acc

    parts = 4
    size = tiles // parts
    copies = []
    acc = total[...]
    lane = tile_iota(1)
    for n in range(parts - 1, -1, -1):
        acc = lax.fori_loop(n * size, (n + 1) * size, body, acc, unroll=2)
        if n == parts - 1:
            target = slots[0] * mix[0]
            for m in range(1, slots.shape[0]):
                target = target + slots[m] * mix[m]
            step = slot_width(row_tiles)
            while step < LANES:
                target = target + pltpu.roll(target, step, 1)
                step *= 2
            for var in range(5):
                for rt in range(row_tiles):
                    own = slice(rt * SUB, (rt + 1) * SUB)
                    moved = pltpu.roll(target, LANES - 1 - (var * row_tiles + rt), 1)
                    extra = jnp.where(lane == LANES - 1, -penalty * moved, 0.0)
                    cut = slice((tiles - 1) * LANES, tiles * LANES)
                    stage[var, own, cut] = stage[var, own, cut] + extra
                    acc = acc + adjoint[var, own, cut] * extra
        cut = pl.ds(n * size * LANES, size * LANES)
        copies.append(pltpu.make_async_copy(stage.at[:, :, cut], out_ref.at[:, :, cut], sems.at[n]))
        copies[-1].start()
    points = rows * lax.axis_size("line") * cols
    sum_ref[...] = jnp.full((SUB, LANES), jnp.sum(acc) / points)
    for c in copies:
        c.wait()


def total_kernel(*refs):
    total = refs[0][...]
    for x in refs[1:-1]:
        total = total + x[...]
    refs[-1][0] = total[0, 0]


def per_device(density, momentum, energy, adjoint, partners, counts, orient):
    rows, cols = density.shape[1:]
    row_tiles, tiles = rows // SUB, cols // LANES
    lines, blocks = lax.axis_size("line"), lax.axis_size("blk")
    state = (density[0], momentum[0], energy[0])
    shape = jax.ShapeDtypeStruct
    pieces = -(-blocks * slot_width(row_tiles) // LANES)
    packed = shape((4, SUB, cols), F32)
    flat = shape((pieces, SUB, LANES), F32)
    anywhere = pl.BlockSpec(memory_space=pl.ANY)
    in_hbm = pl.BlockSpec(memory_space=pltpu.HBM)
    dma = pltpu.SemaphoreType.DMA

    def cost(micros):
        return pl.CostEstimate(flops=micros * 10**6, bytes_accessed=micros * 3 * 10**6, transcendentals=0)

    send_far, slots = pl.pallas_call(
        pack_kernel, out_shape=[packed, flat], in_specs=[in_hbm] * 3, out_specs=[whole()] * 2,
        scratch_shapes=[pltpu.VMEM((5, SUB, cols), F32), pltpu.VMEM((5, rows, LANES), F32), dma((3, 5))],
        compiler_params=params(), cost_estimate=cost(2),
    )(*[pltpu.with_memory_space_constraint(x, pltpu.HBM) for x in state])
    far = lax.ppermute(send_far, "line", [p for i in range(1, lines - 1, 2) for p in ((i, i + 1), (i + 1, i))])
    rounds = [slots]
    hop = 1
    while hop < blocks:
        got = lax.ppermute(rounds[-1], "blk", [(i, i ^ hop) for i in range(blocks)])
        rounds.append(rounds[-1] + got)
        hop *= 2
    slots = rounds[-1]

    lists = (counts[:, None] << 16) + (partners << 1) + orient
    prim, press, xd, send_near, mix = pl.pallas_call(
        first_kernel,
        out_shape=[shape((4, tiles + 2, rows + 2 * SUB, LANES), F32), shape((tiles, rows, LANES), F32),
                   shape((5, tiles, rows, LANES), F32), packed, flat],
        in_specs=[whole()] * 4, out_specs=[whole()] * 5,
        scratch_shapes=[
            pltpu.VMEM((CHUNK, 5, rows + SUB, LANES), F32),
            pltpu.VMEM((2, row_tiles + 1, 4, SUB, LANES), F32),
        ],
        compiler_params=params(), cost_estimate=cost(3),
    )(*state, lists)
    near = lax.ppermute(send_near, "line", [(i, i ^ 1) for i in range(lines)])
    fy = pl.pallas_call(
        second_kernel, out_shape=shape((5, tiles + 2, rows, LANES), F32),
        in_specs=[whole()] * 5, out_specs=whole(), scratch_shapes=[pltpu.VMEM((3, 6, SUB, LANES), F32)],
        compiler_params=params(), cost_estimate=cost(2),
    )(*state, prim, press)
    res, total = pl.pallas_call(
        volume_kernel,
        out_shape=[shape((5, tiles, rows, LANES), F32), shape((SUB, LANES), F32)],
        in_specs=[whole()] * 6, out_specs=[whole()] * 2,
        scratch_shapes=[pltpu.VMEM((3, 6, SUB, LANES), F32)], compiler_params=params(), cost_estimate=cost(2),
    )(*state, adjoint[0], fy, xd)
    result, part = pl.pallas_call(
        border_kernel,
        out_shape=[shape((5, rows, cols), F32), shape((SUB, LANES), F32)],
        in_specs=[whole()] * 7, out_specs=[anywhere, whole()],
        scratch_shapes=[pltpu.VMEM((5, rows, cols), F32), dma((4,))],
        compiler_params=params(), cost_estimate=cost(2),
    )(near, far, slots, mix, res, adjoint[0], total)
    if lines <= 4:
        parts = [part] + [lax.ppermute(part, "line", [(i, i ^ s) for i in range(lines)]) for s in range(1, lines)]
        correction = pl.pallas_call(
            total_kernel, out_shape=shape((1,), F32), in_specs=[whole()] * lines,
            out_specs=pl.BlockSpec(memory_space=pltpu.SMEM), compiler_params=params(),
        )(*parts)
    else:
        correction = lax.psum(part, "line")[0, 0:1]
    return result[None], correction


def solution(mesh):
    return jax.shard_map(
        per_device,
        mesh=mesh,
        in_specs=(
            P("blk", "line", None),
            P("blk", None, "line", None),
            P("blk", "line", None),
            P("blk", None, "line", None),
            P("blk", None),
            P("blk"),
            P("blk", None),
        ),
        out_specs=(P("blk", None, "line", None), P("blk")),
        check_vma=False,
    )
```

time: 35.3 us -> 37.3 us (1.057); the launches traced: 35 us -> 36.6 us
  Pallas kernels: 10.9 us -> 13.2 us
  between operations: 3.18 us -> 1.37 us
  waiting for transfers between devices: 4.26 us -> 5.38 us
  other arithmetic: 0.02 us -> 0.69 us
  local copies, waits for them, and re-layouts: 3.55 us -> 3.05 us
    pallas_call x3 -> x4, Pallas kernels: 5.24 us -> 7.73 us  [the longest x1 2.64 us: per_device(): pl.pallas_call(first_kernel, out_shape=[shape((4, tiles + 2, rows + 2 * S...]
    ppermute x6, waiting for transfers between devices: 4.25 us -> 5.37 us  [the longest x3 2.99 us: per_device(): lax.ppermute(part, 'line', [(i, i ^ s) for i in range(lines)])]
    pallas_call x1, Pallas kernels: 2.47 us -> 1.59 us  [per_device(): pl.pallas_call(border_kernel, out_shape=[shape((5, rows, cols), F32), sha...]
    pallas_call x1, Pallas kernels: 3.16 us -> 3.91 us  [per_device(): pl.pallas_call(volume_kernel, out_shape=[shape((5, tiles, rows, LANES), F...]
    add x4, other arithmetic: 0.02 us -> 0.69 us  [the longest x1 0.68 us: per_device(): lists = (counts[:, None] << 16) + (partners << 1) + orient]
    slice x1 -> x0, local copies, waits for them, and re-layouts: 0.51 us -> none  [per_device(): correction = whole_sum[0, 0:1] / (rows * lines * cols)]
    unnamed x12 -> x14, local copies, waits for them, and re-layouts: 3.04 us -> 3.05 us
  transfers between devices with their start and end apart: 8 -> 8, of which waited for: 3 -> 4; matrix products, arithmetic and copies ran while one was open for 0% -> 0% of each run, Pallas kernels for 22% -> 23%
where the time goes in v2:
time: 37.3 us; the launch traced here: 36.6 us
  Pallas kernels  13.2 us (35%)
  starting transfers between devices  12.9 us (35%)
  waiting for transfers between devices  5.38 us (14%)
  local copies, waits for them, and re-layouts  3.05 us (8%)
  between operations  1.37 us (4%)
  other arithmetic  0.69 us (2%)
    ppermute x3, starting transfers between devices, per_device(): got = lax.ppermute(rounds[-1], 'blk', [(i, i ^ hop) for i in range(blocks)])  4.91 us
    ppermute x1, starting transfers between devices, per_device(): lax.ppermute(send_far, 'line', [p for i in range(1, lines - 1, 2) for p i...  4.49 us
    pallas_call x1, Pallas kernels, per_device(): pl.pallas_call(volume_kernel, out_shape=[shape((5, tiles, rows, LANES), F...  3.91 us
    ppermute x3, starting transfers between devices, per_device(): lax.ppermute(part, 'line', [(i, i ^ s) for i in range(lines)])  3.42 us
    unnamed x14, local copies, waits for them, and re-layouts  3.05 us
    ppermute x3, waiting for transfers between devices, per_device(): lax.ppermute(part, 'line', [(i, i ^ s) for i in range(lines)])  2.99 us
    pallas_call x1, Pallas kernels, per_device(): pl.pallas_call(first_kernel, out_shape=[shape((4, tiles + 2, rows + 2 * S...  2.64 us
    pallas_call x1, Pallas kernels, per_device(): pl.pallas_call(second_kernel, out_shape=shape((5, tiles + 2, rows, LANES)...  2.6 us
  transfers between devices with their start and end apart: 8, of which 4 were waited for; matrix products, arithmetic and copies ran while one was open for 0% of the time, Pallas kernels for 23%

profile of v2, /device:TPU:1, one launch (start us, length us, event | category | flops | bytes accessed | tf_op | source)
XLA Modules:
  0.0 36.6 jit_solution(17581550748266346714)
XLA Ops:
  1.3 0.7 %add_add_fusion.lists = s32[1,4]{1,0:T(1,128)S(1)} fusion(s32[1,4]{1,0:T(1,128)} %param.13, s32[1,4]{1,0:T(1,128)} %param.11, s32[]{:T(128)} %bitcast.3), kind=kLoop, calls=%fused_computation | loop fusion | flops 12 | bytes 52 | tf_op jit(solution)/shard_map/add | solution.py:474
  2.0 0.0 copy-start
  2.0 1.1 %copy-done = f32[1,3,16,4096]{3,2,1,0:T(8,128)S(1)} copy-done((f32[1,3,16,4096]{3,2,1,0:T(8,128)S(1)}, f32[1,3,16,4096]{3,2,1,0:T(8,128)}, u32[]{:S(2)}) %copy-start) | copy-done | bytes 786456
  3.1 0.0 copy-start.3
  3.1 0.9 %copy-done.3 = f32[1,16,4096]{2,1,0:T(8,128)S(1)} copy-done((f32[1,16,4096]{2,1,0:T(8,128)S(1)}, f32[1,16,4096]{2,1,0:T(8,128)}, u32[]{:S(2)}) %copy-start.3) | copy-done | bytes 262168
  4.0 0.0 copy-start.5
  4.0 0.9 %copy-done.5 = f32[1,16,4096]{2,1,0:T(8,128)S(1)} copy-done((f32[1,16,4096]{2,1,0:T(8,128)S(1)}, f32[1,16,4096]{2,1,0:T(8,128)}, u32[]{:S(2)}) %copy-start.5) | copy-done | bytes 262168
  5.0 0.0 copy-start.1
  5.0 0.0 copy-start.4
  5.0 0.0 copy-start.6
  5.0 2.6 %shard_map.86 = (f32[4,34,32,128]{3,2,1,0:T(8,128)S(1)}, f32[32,16,128]{2,1,0:T(8,128)S(1)}, f32[5,32,16,128]{3,2,1,0:T(8,128)S(1)}, f32[4,8,4096]{2,1,0:T(8,128)S(1)}, f32[1,8,128]{2,1,0:T(8,128)S(1)}) custom-call(f32[16,4096]{1,0:T(8,128)S(1)} %bitcast.13, f32[3,16,4096]{2,1,0:T(8,128)S(1)} %bitcast.7, f32[16,4096]{1,0:T(8,128)S(1)} %bitcast.17, ...), custom_call_target="tpu_custom_call" | custom-call | flops 3000000 | bytes 9000000 | tf_op jit(solution)/shard_map/pallas_call | solution.py:475
  7.6 0.1 collective-permute-start
  7.7 1.9 %shard_map.87 = (f32[4,8,4096]{2,1,0:T(8,128)S(1)}, f32[1,8,128]{2,1,0:T(8,128)S(1)}) custom-call(f32[16,4096]{1,0:T(8,128)} %bitcast.12, f32[3,16,4096]{2,1,0:T(8,128)} %bitcast.6, f32[16,4096]{1,0:T(8,128)} %bitcast.16), custom_call_target="tpu_custom_call" | custom-call | flops 2000000 | bytes 6000000 | tf_op jit(solution)/shard_map/pallas_call | solution.py:460
  9.7 4.5 %collective-permute-start.1 = (f32[4,8,4096]{2,1,0:T(8,128)S(1)}, f32[4,8,4096]{2,1,0:T(8,128)S(1)}, u32[]{:S(2)}, u32[]{:S(2)}) collective-permute-start(f32[4,8,4096]{2,1,0:T(8,128)S(1)} %get-tuple-element.14), channel_id=1, source_target_pairs={{1,2},{2,1},{5,6},{6,5},{9,10},{10,9},{13,14},{14,13},{17,18},{18,... | collective-permute-start | bytes 1572872 | tf_op jit(solution)/shard_map/ppermute | solution.py:465
  14.2 1.3 %collective-permute-start.2 = (f32[1,8,128]{2,1,0:T(8,128)S(1)}, f32[1,8,128]{2,1,0:T(8,128)S(1)}, u32[]{:S(2)}, u32[]{:S(2)}) collective-permute-start(f32[1,8,128]{2,1,0:T(8,128)S(1)} %get-tuple-element.15), channel_id=1, source_target_pairs={{0,4},{4,0},{8,12},{12,8},{16,20},{20,16},{24,28},{28,24},{1,5},{5... | collective-permute-start | bytes 12296 | tf_op jit(solution)/shard_map/ppermute | solution.py:469
  15.5 1.2 %collective-permute-done.2 = f32[1,8,128]{2,1,0:T(8,128)S(1)} collective-permute-done((f32[1,8,128]{2,1,0:T(8,128)S(1)}, f32[1,8,128]{2,1,0:T(8,128)S(1)}, u32[]{:S(2)}, u32[]{:S(2)}) %collective-permute-start.2) | collective-permute-done | bytes 4128 | tf_op jit(solution)/shard_map/ppermute | solution.py:469
  16.7 1.3 %collective-permute-start.3 = (f32[1,8,128]{2,1,0:T(8,128)S(1)}, f32[1,8,128]{2,1,0:T(8,128)S(1)}, u32[]{:S(2)}, u32[]{:S(2)}) collective-permute-start(f32[1,8,128]{2,1,0:T(8,128)S(1)} %add.26), channel_id=1, source_target_pairs={{0,8},{4,12},{8,0},{12,4},{16,24},{20,28},{24,16},{28,20},{1,9},{5... | collective-permute-start | bytes 12296 | tf_op jit(solution)/shard_map/ppermute | solution.py:469
  18.0 1.2 %collective-permute-done.3 = f32[1,8,128]{2,1,0:T(8,128)S(1)} collective-permute-done((f32[1,8,128]{2,1,0:T(8,128)S(1)}, f32[1,8,128]{2,1,0:T(8,128)S(1)}, u32[]{:S(2)}, u32[]{:S(2)}) %collective-permute-start.3) | collective-permute-done | bytes 4128 | tf_op jit(solution)/shard_map/ppermute | solution.py:469
  19.2 2.3 %collective-permute-start.4 = (f32[1,8,128]{2,1,0:T(8,128)S(1)}, f32[1,8,128]{2,1,0:T(8,128)S(1)}, u32[]{:S(2)}, u32[]{:S(2)}) collective-permute-start(f32[1,8,128]{2,1,0:T(8,128)S(1)} %add.27), channel_id=1, source_target_pairs={{0,16},{4,20},{8,24},{12,28},{16,0},{20,4},{24,8},{28,12},{1,17},{... | collective-permute-start | bytes 12296 | tf_op jit(solution)/shard_map/ppermute | solution.py:469
  21.5 0.0 copy-done.1
  21.5 0.0 copy-done.4
  21.5 0.0 copy-done.6
  21.5 0.0 copy-start.2
  21.5 2.6 %shard_map.88.fy = f32[5,34,16,128]{3,2,1,0:T(8,128)S(1)} custom-call(f32[16,4096]{1,0:T(8,128)S(1)} %bitcast.14, f32[3,16,4096]{2,1,0:T(8,128)S(1)} %bitcast.8, f32[16,4096]{1,0:T(8,128)S(1)} %bitcast.18, f32[4,34,32,128]{3,2,1,0:T(8,128)S(1)} %get-tuple-element.17.prim, f32[32,16,128]{2,1,0:T(8,128)S(1)} %get-tuple-element.18.press), custom_call_target="tpu_custom_call" | custom-call | flops 2000000 | bytes 6000000 | tf_op jit(solution)/shard_map/pallas_call | solution.py:487
  24.1 0.0 copy-done.2
  24.1 3.9 %shard_map.89 = (f32[5,32,16,128]{3,2,1,0:T(8,128)S(1)}, f32[8,128]{1,0:T(8,128)S(1)}) custom-call(f32[16,4096]{1,0:T(8,128)S(1)} %bitcast.15, f32[3,16,4096]{2,1,0:T(8,128)S(1)} %bitcast.9, f32[16,4096]{1,0:T(8,128)S(1)} %bitcast.19, f32[5,16,4096]{2,1,0:T(8,128)S(1)} %bitcast.10, f32[5,34,16,128]{3,2,1,0:T(8,128)S(1)} %shard_map.88.fy, ...), custom_call_target="tpu_custom_call" | custom-call | flops 2000000 | bytes 6000000 | tf_op jit(solution)/shard_map/pallas_call | solution.py:492
  28.0 0.0 collective-permute-done.4
  28.0 0.0 collective-permute-done.chip
  28.0 0.0 collective-permute-done.1.across
  28.1 1.6 %shard_map.90 = (f32[5,16,4096]{2,1,0:T(8,128)}, f32[8,128]{1,0:T(8,128)S(1)}) custom-call(f32[4,8,4096]{2,1,0:T(8,128)S(1)} %collective-permute-done.chip, f32[4,8,4096]{2,1,0:T(8,128)S(1)} %collective-permute-done.1.across, f32[1,8,128]{2,1,0:T(8,128)S(1)} %add.28.slots, f32[1,8,128]{2,1,0:T(8,128)S(1)} %get-tuple-element.16.mix, ...), custom_call_target="tpu_custom_call" | custom-call | flops 2000000 | bytes 6000000 | tf_op jit(solution)/shard_map/pallas_call | solution.py:498
  29.7 0.3 collective-permute-start.5
  30.0 3.0 %collective-permute-start.6 = (f32[8,128]{1,0:T(8,128)S(1)}, f32[8,128]{1,0:T(8,128)S(1)}, u32[]{:S(2)}, u32[]{:S(2)}) collective-permute-start(f32[8,128]{1,0:T(8,128)S(1)} %get-tuple-element.23.refs_0_), channel_id=1, source_target_pairs={{0,2},{1,3},{2,0},{3,1},{4,6},{5,7},{6,4},{7,5},{8,10},{9,11},{10,... | collective-permute-start | bytes 12296 | tf_op jit(solution)/shard_map/ppermute | solution.py:506
  33.0 0.0 collective-permute-start.7
  33.1 0.0 collective-permute-done.5.refs_1_
  33.1 0.9 %collective-permute-done.6.refs_2_ = f32[8,128]{1,0:T(8,128)S(1)} collective-permute-done((f32[8,128]{1,0:T(8,128)S(1)}, f32[8,128]{1,0:T(8,128)S(1)}, u32[]{:S(2)}, u32[]{:S(2)}) %collective-permute-start.6) | collective-permute-done | bytes 4128 | tf_op jit(solution)/shard_map/ppermute | solution.py:506
  34.0 2.0 %collective-permute-done.7.refs_3_ = f32[8,128]{1,0:T(8,128)S(1)} collective-permute-done((f32[8,128]{1,0:T(8,128)S(1)}, f32[8,128]{1,0:T(8,128)S(1)}, u32[]{:S(2)}, u32[]{:S(2)}) %collective-permute-start.7) | collective-permute-done | bytes 4128 | tf_op jit(solution)/shard_map/ppermute | solution.py:506
  36.1 0.6 %shard_map.91 = f32[1]{0:T(128)} custom-call(f32[8,128]{1,0:T(8,128)S(1)} %get-tuple-element.23.refs_0_, f32[8,128]{1,0:T(8,128)S(1)} %collective-permute-done.5.refs_1_, f32[8,128]{1,0:T(8,128)S(1)} %collective-permute-done.6.refs_2_, f32[8,128]{1,0:T(8,128)S(1)} %collective-permute-done.7.refs_3_), custom_call_target="tpu_custom_call" | custom-call | tf_op jit(solution)/shard_map/pallas_call | solution.py:507
  (3 shorter events, 0.0 us)
Async XLA Ops:
  2.0 1.1 %copy-start = (f32[1,3,16,4096]{3,2,1,0:T(8,128)S(1)}, f32[1,3,16,4096]{3,2,1,0:T(8,128)}, u32[]{:S(2)}) copy-start(f32[1,3,16,4096]{3,2,1,0:T(8,128)} %param.8) | copy-start | bytes 2359300
  3.1 0.9 %copy-start.3 = (f32[1,16,4096]{2,1,0:T(8,128)S(1)}, f32[1,16,4096]{2,1,0:T(8,128)}, u32[]{:S(2)}) copy-start(f32[1,16,4096]{2,1,0:T(8,128)} %param.7) | copy-start | bytes 786436
  4.0 0.9 %copy-start.5 = (f32[1,16,4096]{2,1,0:T(8,128)S(1)}, f32[1,16,4096]{2,1,0:T(8,128)}, u32[]{:S(2)}) copy-start(f32[1,16,4096]{2,1,0:T(8,128)} %param.9) | copy-start | bytes 786436
  5.0 16.5 %copy-start.1 = (f32[1,3,16,4096]{3,2,1,0:T(8,128)S(1)}, f32[1,3,16,4096]{3,2,1,0:T(8,128)}, u32[]{:S(2)}) copy-start(f32[1,3,16,4096]{3,2,1,0:T(8,128)} %param.8) | copy-start | bytes 2359300
  5.0 16.5 %copy-start.4 = (f32[1,16,4096]{2,1,0:T(8,128)S(1)}, f32[1,16,4096]{2,1,0:T(8,128)}, u32[]{:S(2)}) copy-start(f32[1,16,4096]{2,1,0:T(8,128)} %param.7) | copy-start | bytes 786436
  5.0 16.5 %copy-start.6 = (f32[1,16,4096]{2,1,0:T(8,128)S(1)}, f32[1,16,4096]{2,1,0:T(8,128)}, u32[]{:S(2)}) copy-start(f32[1,16,4096]{2,1,0:T(8,128)} %param.9) | copy-start | bytes 786436
  7.6 20.4 %collective-permute-start = (f32[4,8,4096]{2,1,0:T(8,128)S(1)}, f32[4,8,4096]{2,1,0:T(8,128)S(1)}, u32[]{:S(2)}, u32[]{:S(2)}) collective-permute-start(f32[4,8,4096]{2,1,0:T(8,128)S(1)} %get-tuple-element.13), channel_id=1, source_target_pairs={{0,1},{1,0},{2,3},{3,2},{4,5},{5,4},{6,7},{7,6},{8,9},{9,8},{10,11... | collective-permute-start | bytes 1572872 | tf_op jit(solution)/shard_map/ppermute | solution.py:486
  9.7 18.4 %collective-permute-start.1 = (f32[4,8,4096]{2,1,0:T(8,128)S(1)}, f32[4,8,4096]{2,1,0:T(8,128)S(1)}, u32[]{:S(2)}, u32[]{:S(2)}) collective-permute-start(f32[4,8,4096]{2,1,0:T(8,128)S(1)} %get-tuple-element.14), channel_id=1, source_target_pairs={{1,2},{2,1},{5,6},{6,5},{9,10},{10,9},{13,14},{14,13},{17,18},{18,... | collective-permute-start | bytes 1572872 | tf_op jit(solution)/shard_map/ppermute | solution.py:465
  14.2 2.5 %collective-permute-start.2 = (f32[1,8,128]{2,1,0:T(8,128)S(1)}, f32[1,8,128]{2,1,0:T(8,128)S(1)}, u32[]{:S(2)}, u32[]{:S(2)}) collective-permute-start(f32[1,8,128]{2,1,0:T(8,128)S(1)} %get-tuple-element.15), channel_id=1, source_target_pairs={{0,4},{4,0},{8,12},{12,8},{16,20},{20,16},{24,28},{28,24},{1,5},{5... | collective-permute-start | bytes 12296 | tf_op jit(solution)/shard_map/ppermute | solution.py:469
  16.7 2.5 %collective-permute-start.3 = (f32[1,8,128]{2,1,0:T(8,128)S(1)}, f32[1,8,128]{2,1,0:T(8,128)S(1)}, u32[]{:S(2)}, u32[]{:S(2)}) collective-permute-start(f32[1,8,128]{2,1,0:T(8,128)S(1)} %add.26), channel_id=1, source_target_pairs={{0,8},{4,12},{8,0},{12,4},{16,24},{20,28},{24,16},{28,20},{1,9},{5... | collective-permute-start | bytes 12296 | tf_op jit(solution)/shard_map/ppermute | solution.py:469
  19.2 8.9 %collective-permute-start.4 = (f32[1,8,128]{2,1,0:T(8,128)S(1)}, f32[1,8,128]{2,1,0:T(8,128)S(1)}, u32[]{:S(2)}, u32[]{:S(2)}) collective-permute-start(f32[1,8,128]{2,1,0:T(8,128)S(1)} %add.27), channel_id=1, source_target_pairs={{0,16},{4,20},{8,24},{12,28},{16,0},{20,4},{24,8},{28,12},{1,17},{... | collective-permute-start | bytes 12296 | tf_op jit(solution)/shard_map/ppermute | solution.py:469
  21.5 2.6 %copy-start.2 = (f32[1,5,16,4096]{3,2,1,0:T(8,128)S(1)}, f32[1,5,16,4096]{3,2,1,0:T(8,128)}, u32[]{:S(2)}) copy-start(f32[1,5,16,4096]{3,2,1,0:T(8,128)} %param.10) | copy-start | bytes 3932164
  29.7 3.4 %collective-permute-start.5 = (f32[8,128]{1,0:T(8,128)S(1)}, f32[8,128]{1,0:T(8,128)S(1)}, u32[]{:S(2)}, u32[]{:S(2)}) collective-permute-start(f32[8,128]{1,0:T(8,128)S(1)} %get-tuple-element.23.refs_0_), channel_id=1, source_target_pairs={{0,1},{1,0},{2,3},{3,2},{4,5},{5,4},{6,7},{7,6},{8,9},{9,8},{10,11... | collective-permute-start | bytes 12296 | tf_op jit(solution)/shard_map/ppermute | solution.py:506
  30.0 4.0 %collective-permute-start.6 = (f32[8,128]{1,0:T(8,128)S(1)}, f32[8,128]{1,0:T(8,128)S(1)}, u32[]{:S(2)}, u32[]{:S(2)}) collective-permute-start(f32[8,128]{1,0:T(8,128)S(1)} %get-tuple-element.23.refs_0_), channel_id=1, source_target_pairs={{0,2},{1,3},{2,0},{3,1},{4,6},{5,7},{6,4},{7,5},{8,10},{9,11},{10,... | collective-permute-start | bytes 12296 | tf_op jit(solution)/shard_map/ppermute | solution.py:506
  33.0 3.0 %collective-permute-start.7 = (f32[8,128]{1,0:T(8,128)S(1)}, f32[8,128]{1,0:T(8,128)S(1)}, u32[]{:S(2)}, u32[]{:S(2)}) collective-permute-start(f32[8,128]{1,0:T(8,128)S(1)} %get-tuple-element.23.refs_0_), channel_id=1, source_target_pairs={{0,3},{1,2},{2,1},{3,0},{4,7},{5,6},{6,5},{7,4},{8,11},{9,10},{10,... | collective-permute-start | bytes 12296 | tf_op jit(solution)/shard_map/ppermute | solution.py:506

commit v3 on v2

--- a/solution.py
+++ b/solution.py
@@ -1,5 +1,6 @@
 import jax
 import jax.numpy as jnp
+import numpy as np
 from jax import lax
 from jax.experimental import pallas as pl
 from jax.experimental.pallas import tpu as pltpu
@@ -14,7 +15,8 @@
 LANES = 128
 SUB = 8
 CHUNK = 4
-WIDE = 4
+WIDE = 16
+PIECES = 3
 F32 = jnp.float32
 VMEM_LIMIT = 20 * 1024 * 1024
 
@@ -184,41 +186,53 @@
     return pltpu.CompilerParams(vmem_limit_bytes=VMEM_LIMIT)
 
 
-def lane_weights(ref, cols):
+def line_operator(cols):
+    out = np.zeros((3, 2 * LANES, LANES), np.float32)
     for n, start in enumerate((0, LANES, cols - LANES)):
-        at = start + tile_iota(1)
-        one, _, _, point = coefficients(at, cols)
-        for c, w in enumerate((one, point)
-                              + tuple(coefficients(at - 2, cols)[1:3]) + tuple(coefficients(at + 2, cols)[1:3])):
-            ref[n, c] = w
-
-
-def lane_difference(tiles, weights):
-    lane = tile_iota(1)
-    count = len(tiles) - 2
-
-    def shift(values, k):
-        return [pltpu.roll(x, (LANES - k) % LANES, 1) for x in values]
-
-    ahead = shift(tiles[1:], 1)
-    behind = shift(tiles[:-1], -1)
-    plus = [jnp.where(lane < LANES - 1, ahead[j], ahead[j + 1]) for j in range(count)]
-    minus = [jnp.where(lane >= 1, behind[j + 1], behind[j]) for j in range(count)]
-    far = [weights(j + 1, 2) * v + weights(j + 1, 3) * p
-           for j, (v, p) in enumerate(zip(tiles[1:], plus + [ahead[count]]))]
-    back = [weights(j, 4) * v + weights(j, 5) * m for j, (v, m) in enumerate(zip(tiles[:-1], [behind[0]] + minus))]
-    far, back = shift(far, 2), shift(back, -2)
-    out = []
-    for j in range(count):
-        f = jnp.where(lane < LANES - 2, far[j], far[j + 1])
-        b = jnp.where(lane >= 2, back[j + 1], back[j])
-        out.append((weights(j + 1, 0) * (plus[j] - minus[j]) + weights(j + 1, 1) * tiles[j + 1]) + (f - b))
-    return out
-
-
-def weights_at(ref, t0, tiles):
-    which = [jnp.where(t0 + j - 1 <= 0, 0, jnp.where(t0 + j - 1 >= tiles - 1, 2, 1)) for j in range(WIDE + 2)]
-    return lambda j, c: ref[which[j], c]
+        for lane in range(LANES):
+            at = start + lane
+            edge = min(at, cols - 1 - at)
+            if edge == 0:
+                terms = {0: -60, 1: 60} if at == 0 else {0: 60, -1: -60}
+            else:
+                half = {1: (30,), 2: (40, -5)}.get(edge, (45, -9, 1))
+                terms = {sign * (k + 1): sign * c for k, c in enumerate(half) for sign in (1, -1)}
+            for offset, c in terms.items():
+                out[n, (lane + offset) % (2 * LANES), lane] = c
+    return np.tile(out, (1, PIECES, 1)).astype(jnp.bfloat16)
+
+
+def split(x):
+    pieces = []
+    for _ in range(PIECES):
+        piece = x.astype(jnp.bfloat16)
+        pieces.append(piece)
+        x = x - piece.astype(F32)
+    return pieces
+
+
+def wide_of(tiles):
+    return max(w for w in range(1, WIDE + 1) if tiles % w == 0 and 2 * w <= tiles)
+
+
+def lane_differences(lhs, operator, tile_of, wide, count, step, last):
+    rows = lhs.shape[0] // (wide * count)
+    lane = lax.broadcasted_iota(jnp.int32, (rows, LANES), 1)
+    for var in range(count):
+        for j in range(wide):
+            at = slice((j * count + var) * rows, (j * count + var + 1) * rows)
+            cur = split(tile_of(var, j))
+            mix = split(jnp.where(lane < LANES // 2, tile_of(var, j + 1), tile_of(var, j - 1)))
+            for n in range(PIECES):
+                lhs[at, 2 * n * LANES:(2 * n + 1) * LANES] = cur[n]
+                lhs[at, (2 * n + 1) * LANES:(2 * n + 2) * LANES] = mix[n]
+    out = jnp.dot(lhs[...], operator[1], preferred_element_type=F32)
+    which = jnp.where(step == 0, 0, jnp.where(step == last, 2, 1))
+    size = count * rows
+    start = pl.multiple_of(jnp.where(step == last, (wide - 1) * size, 0), size)
+    end = jnp.dot(lhs[pl.ds(start, size), :], operator[which], preferred_element_type=F32)
+    return (lambda var, j: out[(j * count + var) * rows:(j * count + var + 1) * rows],
+            lambda var: end[var * rows:(var + 1) * rows])
 
 
 def apply(weights, at):
@@ -312,71 +326,75 @@
         mix_ref[n] = weight
 
 
-def second_kernel(density, momentum, energy, prim, press, fy_ref, edge):
+def second_kernel(density, momentum, energy, prim, press, operator, fy_ref, lhs):
+    rows, cols = density.shape
+    tiles = cols // LANES
+    wide = wide_of(tiles)
+    last = tiles // wide - 1
+    zero = jnp.zeros((rows, LANES), F32)
+    for var in range(5):
+        fy_ref[var, 0] = zero
+        fy_ref[var, tiles + 1] = zero
+    own = slice(SUB, SUB + rows)
+
+    def store(t, grads):
+        cut = pl.ds(pl.multiple_of(t * LANES, LANES), LANES)
+        state = [density[:, cut]] + [momentum[a, :, cut] for a in range(3)] + [energy[:, cut]]
+        u = [prim[a, t + 1, own, :] for a in range(3)]
+        for var, f in enumerate(convective(state, u, press[t], 1)):
+            scale = viscosity * (conduction if var == 4 else 1.0) / 60.0
+            fy_ref[var, t + 1] = f - scale * grads(var - 1) if var else f
+
+    def body(step, carry):
+        t0 = step * wide
+        inner, end = lane_differences(
+            lhs, operator, lambda var, j: prim[var, t0 + j + 1, own, :], wide, 4, step, last)
+        for j in range(wide):
+            store(t0 + j, lambda var: inner(var, j))
+        store(jnp.where(step == last, tiles - 1, t0), end)
+        return carry
+
+    lax.fori_loop(0, last + 1, body, 0)
+
+
+def volume_kernel(density, momentum, energy, adjoint, fy, xd, operator, res_ref, sum_ref, lhs):
     refs = (density, momentum, energy)
     rows, cols = density.shape
     row_tiles, tiles = rows // SUB, cols // LANES
-    zero = jnp.zeros((SUB, LANES), F32)
-    lane_weights(edge, cols)
-    for var in range(5):
-        for r in range(row_tiles):
-            fy_ref[var, 0, r * SUB:(r + 1) * SUB, :] = zero
-            fy_ref[var, tiles + 1, r * SUB:(r + 1) * SUB, :] = zero
-
-    def store(rt, t, grads):
-        at = slice((rt + 1) * SUB, (rt + 2) * SUB)
-        own = slice(rt * SUB, (rt + 1) * SUB)
-        u = [prim[a, t + 1, at, :] for a in range(3)]
-        for var, f in enumerate(convective(load_state(refs, rt, t), u, press[t, own, :], 1)):
-            scale = viscosity * (conduction if var == 4 else 1.0)
-            fy_ref[var, t + 1, own, :] = f - scale * grads[var - 1] if var else f
-
-    def body(step, carry):
-        t0 = step * WIDE
-        weights = weights_at(edge, t0, tiles)
-        for rt in range(row_tiles):
-            at = slice((rt + 1) * SUB, (rt + 2) * SUB)
-            grads = [lane_difference([prim[var, t0 + j, at, :] for j in range(WIDE + 2)], weights) for var in range(4)]
-            for j in range(WIDE):
-                store(rt, t0 + j, [g[j] for g in grads])
-        return carry
-
-    lax.fori_loop(0, tiles // WIDE, body, 0)
-
-
-def volume_kernel(density, momentum, energy, adjoint, fy, xd, res_ref, sum_ref, edge):
-    refs = (density, momentum, energy)
-    rows, cols = density.shape
-    row_tiles, tiles = rows // SUB, cols // LANES
-    lane_weights(edge, cols)
+    wide = wide_of(tiles)
+    last = tiles // wide - 1
 
     def body(step, accs):
-        t0 = step * WIDE
+        t0 = step * wide
         accs = list(accs)
-        weights = weights_at(edge, t0, tiles)
-        for rt in range(row_tiles):
-            own = slice(rt * SUB, (rt + 1) * SUB)
-            for var in range(5):
-                dy = lane_difference([fy[var, t0 + j, own, :] for j in range(WIDE + 2)], weights)
-                for j in range(WIDE):
-                    t = t0 + j
-                    r = xd[var, t, own, :] + dy[j]
-                    res_ref[var, t, own, :] = r
-                    weighted = adjoint[var, own, pl.ds(pl.multiple_of(t * LANES, LANES), LANES)] * r
-                    accs[j % len(accs)] = accs[j % len(accs)] + weighted
+        inner, end = lane_differences(lhs, operator, lambda var, j: fy[var, t0 + j + 1], wide, 5, step, last)
+        at_end = jnp.where(step == last, tiles - 1, t0)
+        for var in range(5):
+            for j in range(wide):
+                t = t0 + j
+                r = xd[var, t] + inner(var, j) * (1.0 / 60.0)
+                res_ref[var, t] = r
+                accs[j % 2] = accs[j % 2] + adjoint[var, :, pl.ds(pl.multiple_of(t * LANES, LANES), LANES)] * r
+        for var in range(5):
+            r = xd[var, at_end] + end(var) * (1.0 / 60.0)
+            change = r - res_ref[var, at_end]
+            res_ref[var, at_end] = r
+            accs[var % 2] = accs[var % 2] + adjoint[var, :, pl.ds(pl.multiple_of(at_end * LANES, LANES), LANES)] * change
         return tuple(accs)
 
-    zero = jnp.zeros((SUB, LANES), F32)
-    accs = lax.fori_loop(0, tiles // WIDE, body, (zero,) * 4)
-    acc = (accs[0] + accs[1]) + (accs[2] + accs[3])
+    zero = jnp.zeros((rows, LANES), F32)
+    one, two = lax.fori_loop(0, last + 1, body, (zero, zero))
+    both = one + two
+    acc = both[0:SUB]
+    for rt in range(1, row_tiles):
+        acc = acc + both[rt * SUB:(rt + 1) * SUB]
     weight = jnp.where(tile_iota(1) == LANES - 1, penalty, 0.0)
-    last = tiles - 1
     for rt in range(row_tiles):
         own = slice(rt * SUB, (rt + 1) * SUB)
-        for var, x in enumerate(load_state(refs, rt, last)):
+        for var, x in enumerate(load_state(refs, rt, tiles - 1)):
             extra = weight * x
-            res_ref[var, last, own, :] = res_ref[var, last, own, :] + extra
-            acc = acc + adjoint[var, own, last * LANES:] * extra
+            res_ref[var, tiles - 1, own, :] = res_ref[var, tiles - 1, own, :] + extra
+            acc = acc + adjoint[var, own, (tiles - 1) * LANES:] * extra
     sum_ref[...] = acc
 
 
@@ -471,6 +489,11 @@
         hop *= 2
     slots = rounds[-1]
 
+    operator = jnp.asarray(line_operator(cols))
+
+    def lhs_of(count):
+        return pltpu.VMEM((wide_of(tiles) * count * rows, 2 * PIECES * LANES), jnp.bfloat16)
+
     lists = (counts[:, None] << 16) + (partners << 1) + orient
     prim, press, xd, send_near, mix = pl.pallas_call(
         first_kernel,
@@ -486,15 +509,15 @@
     near = lax.ppermute(send_near, "line", [(i, i ^ 1) for i in range(lines)])
     fy = pl.pallas_call(
         second_kernel, out_shape=shape((5, tiles + 2, rows, LANES), F32),
-        in_specs=[whole()] * 5, out_specs=whole(), scratch_shapes=[pltpu.VMEM((3, 6, SUB, LANES), F32)],
+        in_specs=[whole()] * 6, out_specs=whole(), scratch_shapes=[lhs_of(4)],
         compiler_params=params(), cost_estimate=cost(2),
-    )(*state, prim, press)
+    )(*state, prim, press, operator)
     res, total = pl.pallas_call(
         volume_kernel,
         out_shape=[shape((5, tiles, rows, LANES), F32), shape((SUB, LANES), F32)],
-        in_specs=[whole()] * 6, out_specs=[whole()] * 2,
-        scratch_shapes=[pltpu.VMEM((3, 6, SUB, LANES), F32)], compiler_params=params(), cost_estimate=cost(2),
-    )(*state, adjoint[0], fy, xd)
+        in_specs=[whole()] * 7, out_specs=[whole()] * 2,
+        scratch_shapes=[lhs_of(5)], compiler_params=params(), cost_estimate=cost(2),
+    )(*state, adjoint[0], fy, xd, operator)
     result, part = pl.pallas_call(
         border_kernel,
         out_shape=[shape((5, rows, cols), F32), shape((SUB, LANES), F32)],

time: 37.3 us -> 33.8 us (0.906)
  Pallas kernels: 13.2 us -> 9.77 us
    pallas_call x1, Pallas kernels: 3.91 us -> 1.72 us  [per_device(): pl.pallas_call(volume_kernel, out_shape=[shape((5, tiles, rows, LANES), F...]
    pallas_call x1, Pallas kernels: 2.6 us -> 1.33 us  [per_device(): pl.pallas_call(second_kernel, out_shape=shape((5, tiles + 2, rows, LANES)...]
    unnamed x14 -> x16, local copies, waits for them, and re-layouts: 3.05 us -> 3.05 us
  transfers between devices with their start and end apart: 8 -> 8, of which waited for: 4 -> 4; matrix products, arithmetic and copies ran while one was open for 0% -> 0% of each run, Pallas kernels for 23% -> 15%
where the time goes in v3:
time: 33.8 us; the launch traced here: 33.2 us
  starting transfers between devices  12.9 us (38%)
  Pallas kernels  9.77 us (29%)
  waiting for transfers between devices  5.38 us (16%)
  local copies, waits for them, and re-layouts  3.05 us (9%)
  between operations  1.38 us (4%)
  other arithmetic  0.69 us (2%)
    ppermute x3, starting transfers between devices, per_device(): got = lax.ppermute(rounds[-1], 'blk', [(i, i ^ hop) for i in range(blocks)])  4.91 us
    ppermute x1, starting transfers between devices, per_device(): lax.ppermute(send_far, 'line', [p for i in range(1, lines - 1, 2) for p i...  4.49 us
    ppermute x3, starting transfers between devices, per_device(): lax.ppermute(part, 'line', [(i, i ^ s) for i in range(lines)])  3.42 us
    unnamed x16, local copies, waits for them, and re-layouts  3.05 us
    ppermute x3, waiting for transfers between devices, per_device(): lax.ppermute(part, 'line', [(i, i ^ s) for i in range(lines)])  2.99 us
    pallas_call x1, Pallas kernels, per_device(): pl.pallas_call(first_kernel, out_shape=[shape((4, tiles + 2, rows + 2 * S...  2.65 us
    ppermute x3, waiting for transfers between devices, per_device(): got = lax.ppermute(rounds[-1], 'blk', [(i, i ^ hop) for i in range(blocks)])  2.38 us
    pallas_call x1, Pallas kernels, per_device(): pl.pallas_call(pack_kernel, out_shape=[packed, flat], in_specs=[in_hbm] *...  1.93 us
  transfers between devices with their start and end apart: 8, of which 4 were waited for; matrix products, arithmetic and copies ran while one was open for 0% of the time, Pallas kernels for 15%

profile of v3, /device:TPU:1, one launch (start us, length us, event | category | flops | bytes accessed | tf_op | source)
XLA Modules:
  0.0 33.2 jit_solution(8165183899474664931)
XLA Ops:
  1.3 0.7 %add_add_fusion.lists = s32[1,4]{1,0:T(1,128)S(1)} fusion(s32[1,4]{1,0:T(1,128)} %param.14, s32[1,4]{1,0:T(1,128)} %param.12, s32[]{:T(128)} %bitcast.3), kind=kLoop, calls=%fused_computation | loop fusion | flops 12 | bytes 52 | tf_op jit(solution)/shard_map/add | solution.py:497
  2.0 0.0 copy-start
  2.0 1.1 %copy-done = f32[1,3,16,4096]{3,2,1,0:T(8,128)S(1)} copy-done((f32[1,3,16,4096]{3,2,1,0:T(8,128)S(1)}, f32[1,3,16,4096]{3,2,1,0:T(8,128)}, u32[]{:S(2)}) %copy-start) | copy-done | bytes 786456
  3.1 0.0 copy-start.3
  3.1 0.9 %copy-done.3 = f32[1,16,4096]{2,1,0:T(8,128)S(1)} copy-done((f32[1,16,4096]{2,1,0:T(8,128)S(1)}, f32[1,16,4096]{2,1,0:T(8,128)}, u32[]{:S(2)}) %copy-start.3) | copy-done | bytes 262168
  4.0 0.0 copy-start.5
  4.0 0.9 %copy-done.5 = f32[1,16,4096]{2,1,0:T(8,128)S(1)} copy-done((f32[1,16,4096]{2,1,0:T(8,128)S(1)}, f32[1,16,4096]{2,1,0:T(8,128)}, u32[]{:S(2)}) %copy-start.5) | copy-done | bytes 262168
  5.0 0.0 copy-start.1
  5.0 0.0 copy-start.4
  5.0 0.0 copy-start.6
  5.0 0.0 copy-start.7
  5.0 2.6 %shard_map.95 = (f32[4,34,32,128]{3,2,1,0:T(8,128)S(1)}, f32[32,16,128]{2,1,0:T(8,128)S(1)}, f32[5,32,16,128]{3,2,1,0:T(8,128)S(1)}, f32[4,8,4096]{2,1,0:T(8,128)S(1)}, f32[1,8,128]{2,1,0:T(8,128)S(1)}) custom-call(f32[16,4096]{1,0:T(8,128)S(1)} %bitcast.13, f32[3,16,4096]{2,1,0:T(8,128)S(1)} %bitcast.7, f32[16,4096]{1,0:T(8,128)S(1)} %bitcast.17, ...), custom_call_target="tpu_custom_call" | custom-call | flops 3000000 | bytes 9000000 | tf_op jit(solution)/shard_map/pallas_call | solution.py:498
  7.6 0.1 collective-permute-start
  7.7 1.9 %shard_map.96 = (f32[4,8,4096]{2,1,0:T(8,128)S(1)}, f32[1,8,128]{2,1,0:T(8,128)S(1)}) custom-call(f32[16,4096]{1,0:T(8,128)} %bitcast.12, f32[3,16,4096]{2,1,0:T(8,128)} %bitcast.6, f32[16,4096]{1,0:T(8,128)} %bitcast.16), custom_call_target="tpu_custom_call" | custom-call | flops 2000000 | bytes 6000000 | tf_op jit(solution)/shard_map/pallas_call | solution.py:478
  9.7 4.5 %collective-permute-start.1 = (f32[4,8,4096]{2,1,0:T(8,128)S(1)}, f32[4,8,4096]{2,1,0:T(8,128)S(1)}, u32[]{:S(2)}, u32[]{:S(2)}) collective-permute-start(f32[4,8,4096]{2,1,0:T(8,128)S(1)} %get-tuple-element.14), channel_id=1, source_target_pairs={{1,2},{2,1},{5,6},{6,5},{9,10},{10,9},{13,14},{14,13},{17,18},{18,... | collective-permute-start | bytes 1572872 | tf_op jit(solution)/shard_map/ppermute | solution.py:483
  14.2 1.3 %collective-permute-start.2 = (f32[1,8,128]{2,1,0:T(8,128)S(1)}, f32[1,8,128]{2,1,0:T(8,128)S(1)}, u32[]{:S(2)}, u32[]{:S(2)}) collective-permute-start(f32[1,8,128]{2,1,0:T(8,128)S(1)} %get-tuple-element.15), channel_id=1, source_target_pairs={{0,4},{4,0},{8,12},{12,8},{16,20},{20,16},{24,28},{28,24},{1,5},{5... | collective-permute-start | bytes 12296 | tf_op jit(solution)/shard_map/ppermute | solution.py:487
  15.5 1.2 %collective-permute-done.2 = f32[1,8,128]{2,1,0:T(8,128)S(1)} collective-permute-done((f32[1,8,128]{2,1,0:T(8,128)S(1)}, f32[1,8,128]{2,1,0:T(8,128)S(1)}, u32[]{:S(2)}, u32[]{:S(2)}) %collective-permute-start.2) | collective-permute-done | bytes 4128 | tf_op jit(solution)/shard_map/ppermute | solution.py:487
  16.7 1.3 %collective-permute-start.3 = (f32[1,8,128]{2,1,0:T(8,128)S(1)}, f32[1,8,128]{2,1,0:T(8,128)S(1)}, u32[]{:S(2)}, u32[]{:S(2)}) collective-permute-start(f32[1,8,128]{2,1,0:T(8,128)S(1)} %add.26), channel_id=1, source_target_pairs={{0,8},{4,12},{8,0},{12,4},{16,24},{20,28},{24,16},{28,20},{1,9},{5... | collective-permute-start | bytes 12296 | tf_op jit(solution)/shard_map/ppermute | solution.py:487
  18.0 1.2 %collective-permute-done.3 = f32[1,8,128]{2,1,0:T(8,128)S(1)} collective-permute-done((f32[1,8,128]{2,1,0:T(8,128)S(1)}, f32[1,8,128]{2,1,0:T(8,128)S(1)}, u32[]{:S(2)}, u32[]{:S(2)}) %collective-permute-start.3) | collective-permute-done | bytes 4128 | tf_op jit(solution)/shard_map/ppermute | solution.py:487
  19.2 2.3 %collective-permute-start.4 = (f32[1,8,128]{2,1,0:T(8,128)S(1)}, f32[1,8,128]{2,1,0:T(8,128)S(1)}, u32[]{:S(2)}, u32[]{:S(2)}) collective-permute-start(f32[1,8,128]{2,1,0:T(8,128)S(1)} %add.27), channel_id=1, source_target_pairs={{0,16},{4,20},{8,24},{12,28},{16,0},{20,4},{24,8},{28,12},{1,17},{... | collective-permute-start | bytes 12296 | tf_op jit(solution)/shard_map/ppermute | solution.py:487
  21.5 0.0 copy-done.1
  21.5 0.0 copy-done.4
  21.5 0.0 copy-done.6
  21.5 0.0 copy-done.7
  21.5 0.0 copy-start.2
  21.5 1.3 %shard_map.97.fy = f32[5,34,16,128]{3,2,1,0:T(8,128)S(1)} custom-call(f32[16,4096]{1,0:T(8,128)S(1)} %bitcast.14, f32[3,16,4096]{2,1,0:T(8,128)S(1)} %bitcast.8, f32[16,4096]{1,0:T(8,128)S(1)} %bitcast.18, f32[4,34,32,128]{3,2,1,0:T(8,128)S(1)} %get-tuple-element.17.prim, f32[32,16,128]{2,1,0:T(8,128)S(1)} %get-tuple-element.18.press, ...), custom_call_target="tpu_custom_call" | custom-call | flops 2000000 | bytes 6000000 | tf_op jit(solution)/shard_map/pallas_call | solution.py:510
  22.8 0.0 copy-done.2
  22.8 1.7 %shard_map.98 = (f32[5,32,16,128]{3,2,1,0:T(8,128)S(1)}, f32[8,128]{1,0:T(8,128)S(1)}) custom-call(f32[16,4096]{1,0:T(8,128)S(1)} %bitcast.15, f32[3,16,4096]{2,1,0:T(8,128)S(1)} %bitcast.9, f32[16,4096]{1,0:T(8,128)S(1)} %bitcast.19, f32[5,16,4096]{2,1,0:T(8,128)S(1)} %bitcast.10, f32[5,34,16,128]{3,2,1,0:T(8,128)S(1)} %shard_map.97.fy, ...), custom_call_target="tpu_custom_call" | custom-call | flops 2000000 | bytes 6000000 | tf_op jit(solution)/shard_map/pallas_call | solution.py:515
  24.6 0.0 collective-permute-done.4
  24.6 0.0 collective-permute-done.chip
  24.6 0.0 collective-permute-done.1.across
  24.6 1.6 %shard_map.99 = (f32[5,16,4096]{2,1,0:T(8,128)}, f32[8,128]{1,0:T(8,128)S(1)}) custom-call(f32[4,8,4096]{2,1,0:T(8,128)S(1)} %collective-permute-done.chip, f32[4,8,4096]{2,1,0:T(8,128)S(1)} %collective-permute-done.1.across, f32[1,8,128]{2,1,0:T(8,128)S(1)} %add.28.slots, f32[1,8,128]{2,1,0:T(8,128)S(1)} %get-tuple-element.16.mix, ...), custom_call_target="tpu_custom_call" | custom-call | flops 2000000 | bytes 6000000 | tf_op jit(solution)/shard_map/pallas_call | solution.py:521
  26.2 0.3 %collective-permute-start.5 = (f32[8,128]{1,0:T(8,128)S(1)}, f32[8,128]{1,0:T(8,128)S(1)}, u32[]{:S(2)}, u32[]{:S(2)}) collective-permute-start(f32[8,128]{1,0:T(8,128)S(1)} %get-tuple-element.23.refs_0_), channel_id=1, source_target_pairs={{0,1},{1,0},{2,3},{3,2},{4,5},{5,4},{6,7},{7,6},{8,9},{9,8},{10,11... | collective-permute-start | bytes 12296 | tf_op jit(solution)/shard_map/ppermute | solution.py:529
  26.5 3.0 %collective-permute-start.6 = (f32[8,128]{1,0:T(8,128)S(1)}, f32[8,128]{1,0:T(8,128)S(1)}, u32[]{:S(2)}, u32[]{:S(2)}) collective-permute-start(f32[8,128]{1,0:T(8,128)S(1)} %get-tuple-element.23.refs_0_), channel_id=1, source_target_pairs={{0,2},{1,3},{2,0},{3,1},{4,6},{5,7},{6,4},{7,5},{8,10},{9,11},{10,... | collective-permute-start | bytes 12296 | tf_op jit(solution)/shard_map/ppermute | solution.py:529
  29.6 0.0 collective-permute-start.7
  29.6 0.0 collective-permute-done.5.refs_1_
  29.6 0.9 %collective-permute-done.6.refs_2_ = f32[8,128]{1,0:T(8,128)S(1)} collective-permute-done((f32[8,128]{1,0:T(8,128)S(1)}, f32[8,128]{1,0:T(8,128)S(1)}, u32[]{:S(2)}, u32[]{:S(2)}) %collective-permute-start.6) | collective-permute-done | bytes 4128 | tf_op jit(solution)/shard_map/ppermute | solution.py:529
  30.6 2.0 %collective-permute-done.7.refs_3_ = f32[8,128]{1,0:T(8,128)S(1)} collective-permute-done((f32[8,128]{1,0:T(8,128)S(1)}, f32[8,128]{1,0:T(8,128)S(1)}, u32[]{:S(2)}, u32[]{:S(2)}) %collective-permute-start.7) | collective-permute-done | bytes 4128 | tf_op jit(solution)/shard_map/ppermute | solution.py:529
  32.6 0.6 %shard_map.100 = f32[1]{0:T(128)} custom-call(f32[8,128]{1,0:T(8,128)S(1)} %get-tuple-element.23.refs_0_, f32[8,128]{1,0:T(8,128)S(1)} %collective-permute-done.5.refs_1_, f32[8,128]{1,0:T(8,128)S(1)} %collective-permute-done.6.refs_2_, f32[8,128]{1,0:T(8,128)S(1)} %collective-permute-done.7.refs_3_), custom_call_target="tpu_custom_call" | custom-call | tf_op jit(solution)/shard_map/pallas_call | solution.py:530
  (3 shorter events, 0.0 us)
Async XLA Ops:
  2.0 1.1 %copy-start = (f32[1,3,16,4096]{3,2,1,0:T(8,128)S(1)}, f32[1,3,16,4096]{3,2,1,0:T(8,128)}, u32[]{:S(2)}) copy-start(f32[1,3,16,4096]{3,2,1,0:T(8,128)} %param.9) | copy-start | bytes 2359300
  3.1 0.9 %copy-start.3 = (f32[1,16,4096]{2,1,0:T(8,128)S(1)}, f32[1,16,4096]{2,1,0:T(8,128)}, u32[]{:S(2)}) copy-start(f32[1,16,4096]{2,1,0:T(8,128)} %param.8) | copy-start | bytes 786436
  4.0 0.9 %copy-start.5 = (f32[1,16,4096]{2,1,0:T(8,128)S(1)}, f32[1,16,4096]{2,1,0:T(8,128)}, u32[]{:S(2)}) copy-start(f32[1,16,4096]{2,1,0:T(8,128)} %param.10) | copy-start | bytes 786436
  5.0 16.5 %copy-start.1 = (f32[1,3,16,4096]{3,2,1,0:T(8,128)S(1)}, f32[1,3,16,4096]{3,2,1,0:T(8,128)}, u32[]{:S(2)}) copy-start(f32[1,3,16,4096]{3,2,1,0:T(8,128)} %param.9) | copy-start | bytes 2359300
  5.0 16.5 %copy-start.4 = (f32[1,16,4096]{2,1,0:T(8,128)S(1)}, f32[1,16,4096]{2,1,0:T(8,128)}, u32[]{:S(2)}) copy-start(f32[1,16,4096]{2,1,0:T(8,128)} %param.8) | copy-start | bytes 786436
  5.0 16.5 %copy-start.6 = (f32[1,16,4096]{2,1,0:T(8,128)S(1)}, f32[1,16,4096]{2,1,0:T(8,128)}, u32[]{:S(2)}) copy-start(f32[1,16,4096]{2,1,0:T(8,128)} %param.10) | copy-start | bytes 786436
  5.0 16.5 %copy-start.7 = (bf16[3,768,128]{2,1,0:T(8,128)(2,1)S(1)}, bf16[3,768,128]{2,1,0:T(8,128)(2,1)}, u32[]{:S(2)}) copy-start(bf16[3,768,128]{2,1,0:T(8,128)(2,1)} %constant.7.clone.operator) | copy-start | bytes 1769476
  7.6 16.9 %collective-permute-start = (f32[4,8,4096]{2,1,0:T(8,128)S(1)}, f32[4,8,4096]{2,1,0:T(8,128)S(1)}, u32[]{:S(2)}, u32[]{:S(2)}) collective-permute-start(f32[4,8,4096]{2,1,0:T(8,128)S(1)} %get-tuple-element.13), channel_id=1, source_target_pairs={{0,1},{1,0},{2,3},{3,2},{4,5},{5,4},{6,7},{7,6},{8,9},{9,8},{10,11... | collective-permute-start | bytes 1572872 | tf_op jit(solution)/shard_map/ppermute | solution.py:509
  9.7 14.9 %collective-permute-start.1 = (f32[4,8,4096]{2,1,0:T(8,128)S(1)}, f32[4,8,4096]{2,1,0:T(8,128)S(1)}, u32[]{:S(2)}, u32[]{:S(2)}) collective-permute-start(f32[4,8,4096]{2,1,0:T(8,128)S(1)} %get-tuple-element.14), channel_id=1, source_target_pairs={{1,2},{2,1},{5,6},{6,5},{9,10},{10,9},{13,14},{14,13},{17,18},{18,... | collective-permute-start | bytes 1572872 | tf_op jit(solution)/shard_map/ppermute | solution.py:483
  14.2 2.5 %collective-permute-start.2 = (f32[1,8,128]{2,1,0:T(8,128)S(1)}, f32[1,8,128]{2,1,0:T(8,128)S(1)}, u32[]{:S(2)}, u32[]{:S(2)}) collective-permute-start(f32[1,8,128]{2,1,0:T(8,128)S(1)} %get-tuple-element.15), channel_id=1, source_target_pairs={{0,4},{4,0},{8,12},{12,8},{16,20},{20,16},{24,28},{28,24},{1,5},{5... | collective-permute-start | bytes 12296 | tf_op jit(solution)/shard_map/ppermute | solution.py:487
  16.7 2.5 %collective-permute-start.3 = (f32[1,8,128]{2,1,0:T(8,128)S(1)}, f32[1,8,128]{2,1,0:T(8,128)S(1)}, u32[]{:S(2)}, u32[]{:S(2)}) collective-permute-start(f32[1,8,128]{2,1,0:T(8,128)S(1)} %add.26), channel_id=1, source_target_pairs={{0,8},{4,12},{8,0},{12,4},{16,24},{20,28},{24,16},{28,20},{1,9},{5... | collective-permute-start | bytes 12296 | tf_op jit(solution)/shard_map/ppermute | solution.py:487
  19.2 5.4 %collective-permute-start.4 = (f32[1,8,128]{2,1,0:T(8,128)S(1)}, f32[1,8,128]{2,1,0:T(8,128)S(1)}, u32[]{:S(2)}, u32[]{:S(2)}) collective-permute-start(f32[1,8,128]{2,1,0:T(8,128)S(1)} %add.27), channel_id=1, source_target_pairs={{0,16},{4,20},{8,24},{12,28},{16,0},{20,4},{24,8},{28,12},{1,17},{... | collective-permute-start | bytes 12296 | tf_op jit(solution)/shard_map/ppermute | solution.py:487
  21.5 1.4 %copy-start.2 = (f32[1,5,16,4096]{3,2,1,0:T(8,128)S(1)}, f32[1,5,16,4096]{3,2,1,0:T(8,128)}, u32[]{:S(2)}) copy-start(f32[1,5,16,4096]{3,2,1,0:T(8,128)} %param.11) | copy-start | bytes 3932164
  26.2 3.4 %collective-permute-start.5 = (f32[8,128]{1,0:T(8,128)S(1)}, f32[8,128]{1,0:T(8,128)S(1)}, u32[]{:S(2)}, u32[]{:S(2)}) collective-permute-start(f32[8,128]{1,0:T(8,128)S(1)} %get-tuple-element.23.refs_0_), channel_id=1, source_target_pairs={{0,1},{1,0},{2,3},{3,2},{4,5},{5,4},{6,7},{7,6},{8,9},{9,8},{10,11... | collective-permute-start | bytes 12296 | tf_op jit(solution)/shard_map/ppermute | solution.py:529
  26.5 4.0 %collective-permute-start.6 = (f32[8,128]{1,0:T(8,128)S(1)}, f32[8,128]{1,0:T(8,128)S(1)}, u32[]{:S(2)}, u32[]{:S(2)}) collective-permute-start(f32[8,128]{1,0:T(8,128)S(1)} %get-tuple-element.23.refs_0_), channel_id=1, source_target_pairs={{0,2},{1,3},{2,0},{3,1},{4,6},{5,7},{6,4},{7,5},{8,10},{9,11},{10,... | collective-permute-start | bytes 12296 | tf_op jit(solution)/shard_map/ppermute | solution.py:529
  29.6 3.0 %collective-permute-start.7 = (f32[8,128]{1,0:T(8,128)S(1)}, f32[8,128]{1,0:T(8,128)S(1)}, u32[]{:S(2)}, u32[]{:S(2)}) collective-permute-start(f32[8,128]{1,0:T(8,128)S(1)} %get-tuple-element.23.refs_0_), channel_id=1, source_target_pairs={{0,3},{1,2},{2,1},{3,0},{4,7},{5,6},{6,5},{7,4},{8,11},{9,10},{10,... | collective-permute-start | bytes 12296 | tf_op jit(solution)/shard_map/ppermute | solution.py:529

commit v4 on v3

--- a/solution.py
+++ b/solution.py
@@ -41,6 +41,10 @@
     return [jnp.where(inside, c, 0.0).astype(F32) for c in (one, two, three, point)]
 
 
+def parts_of(state):
+    return state.at[0], state.at[1:4], state.at[4]
+
+
 def load_state(refs, rt, t):
     density, momentum, energy = refs
     rows = slice(rt * SUB, (rt + 1) * SUB)
@@ -66,25 +70,34 @@
     return out
 
 
-def contribution(state, up):
+def contribution(state, up, pad):
     u, p, temp = primitive_of(state)
     conv = convective(state, u, p, 0)
-    row = tile_iota(0)
-    shift = (lambda x, m: pltpu.roll(x, m, 0)) if up else (lambda x, m: pltpu.roll(x, SUB - m, 0))
+    middle = slice(SUB, 2 * SUB)
+    for n, x in enumerate(conv + u + [temp]):
+        pad[n, middle, :] = x
     sign = -1.0 if up else 1.0
-    keep = [None] + [(row < m) if up else (row >= SUB - m) for m in range(1, 7)]
+
+    def shifted(n, m):
+        start = 2 * SUB - m if up else m
+        return pad[n, start:start + SUB, :]
+
     out = []
     for var in range(5):
         acc = None
         for m in (1, 2, 3):
-            term = shift(conv[var], m) * jnp.where(keep[m], sign * STENCIL[m - 1], 0.0)
+            term = shifted(var, m) * (sign * STENCIL[m - 1])
             acc = term if acc is None else acc + term
         if var:
-            prim = u[var - 1] if var < 4 else temp
             scale = -viscosity * (conduction if var == 4 else 1.0)
             for m in range(1, 7):
-                acc = acc + shift(prim, m) * jnp.where(keep[m], scale * TWICE[m], 0.0)
+                acc = acc + shifted(4 + var, m) * (scale * TWICE[m])
         out.append(acc)
+    return place_mass(out, up)
+
+
+def place_mass(out, up):
+    row = tile_iota(0)
     mass, first, second = out[0], out[1], out[2]
     if up:
         first = jnp.where(row >= 6, pltpu.roll(mass, 6, 0), first)
@@ -108,14 +121,26 @@
     return [mass] + [jnp.where(keep, x, 0.0) for x in (first, second, third, fourth)]
 
 
-def side_of(refs, up, out_ref, rt, first, last):
-    def body(t, carry):
-        cols = pl.ds(pl.multiple_of(t * LANES, LANES), LANES)
-        for n, x in enumerate(contribution(load_state(refs, rt, t), up)):
-            out_ref[n, :, cols] = x
+def side_of(refs, up, out_ref, rt, first, last, pad):
+    ways = pad.shape[0]
+
+    def body(step, carry):
+        for j in range(ways):
+            t = step * ways + j
+            cols = pl.ds(pl.multiple_of(t * LANES, LANES), LANES)
+            for n, x in enumerate(contribution(load_state(refs, rt, t), up, pad.at[j])):
+                out_ref[n, :, cols] = x
         return carry
 
-    lax.fori_loop(first, last, body, 0, unroll=2)
+    lax.fori_loop(first // ways, last // ways, body, 0)
+
+
+def clear(pad):
+    zero = jnp.zeros((SUB, LANES), F32)
+    for j in range(pad.shape[0]):
+        for n in range(pad.shape[1]):
+            pad[j, n, 0:SUB, :] = zero
+            pad[j, n, 2 * SUB:3 * SUB, :] = zero
 
 
 def by_parity(up_when, run):
@@ -130,7 +155,7 @@
         run(False)
 
 
-def pack_kernel(density, momentum, energy, out_ref, slots, buf, other, sems):
+def pack_kernel(density, momentum, energy, out_ref, slots, state_ref, pad, sems):
     rows, cols = density.shape
     row_tiles, tiles = rows // SUB, cols // LANES
     up = lax.rem(lax.axis_index("line"), 2) == 1
@@ -138,24 +163,25 @@
     sources = [density] + [momentum.at[a] for a in range(3)] + [energy]
     halves = 2
     part = cols // halves
-    copies = []
+
+    def fetch(x, n, tile, h, sem):
+        at = pl.ds(pl.multiple_of(tile * SUB, SUB), SUB)
+        cut = pl.ds(h * part, part)
+        return pltpu.make_async_copy(x.at[at, cut], state_ref.at[n, at, cut], sem)
+
+    needed = [[fetch(x, n, mine, h, sems.at[h, n]) for n, x in enumerate(sources)] for h in range(halves)]
+    rest = [fetch(x, n, jnp.where(mine == 0, k, k - 1), h, sems.at[halves * k + h, n])
+            for k in range(1, row_tiles) for h in range(halves) for n, x in enumerate(sources)]
+    for c in sum(needed, []) + rest:
+        c.start()
+    clear(pad)
+    refs = parts_of(state_ref)
     for h in range(halves):
-        for n, x in enumerate(sources):
-            at = pl.ds(pl.multiple_of(mine * SUB, SUB), SUB)
-            copies.append(pltpu.make_async_copy(
-                x.at[at, pl.ds(h * part, part)], buf.at[n, :, pl.ds(h * part, part)], sems.at[h, n]))
-    bottom = [pltpu.make_async_copy(x.at[:, pl.ds(0, LANES)], other.at[n], sems.at[halves, n])
-              for n, x in enumerate(sources)]
-    for c in copies + bottom:
-        c.start()
-
-    refs = (buf.at[0], buf.at[1:4], buf.at[4])
-    for h in range(halves):
-        for c in copies[h * 5:(h + 1) * 5]:
+        for c in needed[h]:
             c.wait()
-        by_parity(1, lambda up_side: side_of(refs, up_side, out_ref, 0, h * tiles // halves, (h + 1) * tiles // halves))
-
-    for c in bottom:
+        by_parity(1, lambda up_side: side_of(
+            refs, up_side, out_ref, row_tiles - 1 if up_side else 0, h * tiles // halves, (h + 1) * tiles // halves, pad))
+    for c in rest:
         c.wait()
     width = slot_width(row_tiles)
     per = LANES // width
@@ -165,7 +191,7 @@
     value = jnp.zeros((SUB, LANES), F32)
     for rt in range(row_tiles):
         for var in range(5):
-            x = other[var, rt * SUB:(rt + 1) * SUB, 0:1]
+            x = state_ref[var, rt * SUB:(rt + 1) * SUB, 0:LANES][:, 0:1]
             value = jnp.where(lane == base + (var * row_tiles + rt), x, value)
     for n in range(slots.shape[0]):
         slots[n] = jnp.where(block // per == n, value, 0.0)
@@ -245,10 +271,10 @@
     return one * (at(1) - at(-1)) + two * (at(2) - at(-2)) + three * (at(3) - at(-3))
 
 
-def first_kernel(density, momentum, energy, lists,
+def first_kernel(state_ref, counts, partners, orient,
                  prim, press, xd_ref, near_ref, mix_ref, fx, xcoef):
-    refs = (density, momentum, energy)
-    rows, cols = density.shape
+    refs = parts_of(state_ref)
+    rows, cols = state_ref.shape[1:]
     row_tiles, tiles = rows // SUB, cols // LANES
     line = lax.axis_index("line")
     extent = rows * lax.axis_size("line")
@@ -264,8 +290,11 @@
             prim[var, 0, r * SUB:(r + 1) * SUB, :] = zero
             prim[var, tiles + 1, r * SUB:(r + 1) * SUB, :] = zero
     for j in range(CHUNK):
-        for r in range(row_tiles + 1):
-            fx[j, 0, r * SUB:(r + 1) * SUB, :] = zero
+        for var in range(5):
+            for r in range(row_tiles + 3):
+                fx[j, var, r * SUB:(r + 1) * SUB, :] = zero
+    odd = lax.rem(line, 2)
+    beyond = pl.multiple_of((rows + SUB) * (1 - odd), SUB)
 
     def body(step, carry):
         for j in range(CHUNK):
@@ -291,21 +320,24 @@
                         d = interior(at)
                     else:
                         d = apply([xcoef[0, g, c] for c in range(4)], at)
-                    fx[j, var + 1, g * SUB:(g + 1) * SUB, :] = scale * d
+                    fx[j, var + 1, (g + 1) * SUB:(g + 2) * SUB, :] = scale * d
             for rt in range(row_tiles):
-                place = slice(3 + rt * SUB, 3 + (rt + 1) * SUB)
+                place = slice(11 + rt * SUB, 11 + (rt + 1) * SUB)
                 for var, f in enumerate(flux[rt]):
                     fx[j, var, place, :] = fx[j, var, place, :] + f if var else f
             for var in range(5):
                 for rt in range(row_tiles):
                     w = [xcoef[1, rt, c] for c in range(4)]
-                    base = 3 + rt * SUB
+                    base = 11 + rt * SUB
                     xd_ref[var, t, rt * SUB:(rt + 1) * SUB, :] = apply(
                         w, lambda k: fx[j, var, base + k:base + k + SUB, :])
+            out = [interior(lambda k: fx[j, var, pl.ds(beyond + (3 + k), SUB), :]) for var in range(5)]
+            cut = pl.ds(pl.multiple_of(t * LANES, LANES), LANES)
+            for n, (a, b) in enumerate(zip(place_mass(out, True), place_mass(out, False))):
+                near_ref[n, :, cut] = jnp.where(odd == 1, b, a) if n < 2 else a
         return carry
 
     lax.fori_loop(0, tiles // CHUNK, body, 0)
-    by_parity(0, lambda up: side_of(refs, up, near_ref, row_tiles - 1 if up else 0, 0, tiles))
 
     width = slot_width(row_tiles)
     per = LANES // width
@@ -314,20 +346,20 @@
     def spread(ref, k):
         return jnp.broadcast_to(ref[0:1, k:k + 1], (SUB, LANES))
 
-    count = spread(lists, 0) >> 16
+    count = spread(counts, 0)
     share = 1.0 / count.astype(F32)
     flipped = (lane % width) // row_tiles == 2
     for n in range(mix_ref.shape[0]):
         weight = zero
-        for k in range(lists.shape[1]):
-            turn = 1.0 - 2.0 * (spread(lists, k) & 1).astype(F32)
-            hit = (lane // width + n * per == ((spread(lists, k) >> 1) & 0x7FFF)) & (k < count)
+        for k in range(partners.shape[1]):
+            turn = 1.0 - 2.0 * spread(orient, k).astype(F32)
+            hit = (lane // width + n * per == spread(partners, k)) & (k < count)
             weight = weight + jnp.where(hit, share * jnp.where(flipped, turn, 1.0), 0.0)
         mix_ref[n] = weight
 
 
-def second_kernel(density, momentum, energy, prim, press, operator, fy_ref, lhs):
-    rows, cols = density.shape
+def second_kernel(state_ref, prim, press, operator, fy_ref, lhs):
+    rows, cols = state_ref.shape[1:]
     tiles = cols // LANES
     wide = wide_of(tiles)
     last = tiles // wide - 1
@@ -339,7 +371,7 @@
 
     def store(t, grads):
         cut = pl.ds(pl.multiple_of(t * LANES, LANES), LANES)
-        state = [density[:, cut]] + [momentum[a, :, cut] for a in range(3)] + [energy[:, cut]]
+        state = [state_ref[n, :, cut] for n in range(5)]
         u = [prim[a, t + 1, own, :] for a in range(3)]
         for var, f in enumerate(convective(state, u, press[t], 1)):
             scale = viscosity * (conduction if var == 4 else 1.0) / 60.0
@@ -357,9 +389,9 @@
     lax.fori_loop(0, last + 1, body, 0)
 
 
-def volume_kernel(density, momentum, energy, adjoint, fy, xd, operator, res_ref, sum_ref, lhs):
-    refs = (density, momentum, energy)
-    rows, cols = density.shape
+def volume_kernel(state_ref, adjoint, fy, xd, operator, res_ref, sum_ref, lhs):
+    refs = parts_of(state_ref)
+    rows, cols = state_ref.shape[1:]
     row_tiles, tiles = rows // SUB, cols // LANES
     wide = wide_of(tiles)
     last = tiles // wide - 1
@@ -398,56 +430,81 @@
     sum_ref[...] = acc
 
 
-def border_kernel(chip, across, slots, mix, res, adjoint, total, out_ref, sum_ref, stage, sems):
+def received(chip, across, t):
+    odd = lax.rem(lax.axis_index("line"), 2) == 1
+    at = pl.ds(pl.multiple_of(t * LANES, LANES), LANES)
+    near = [chip[n, :, at] for n in range(4)]
+    far = [across[n, :, at] for n in range(4)]
+    below = unpack([jnp.where(odd, a, b) for a, b in zip(near, far)], True)
+    above = unpack([jnp.where(odd, b, a) for a, b in zip(near, far)], False)
+    return below, above
+
+
+def border_sum_kernel(chip, across, slots, mix, adjoint, total, column_ref, sum_ref):
     rows, cols = adjoint.shape[1:]
     row_tiles, tiles = rows // SUB, cols // LANES
-    odd = lax.rem(lax.axis_index("line"), 2) == 1
-
-    def body(t, acc):
+
+    def body(step, accs):
+        accs = list(accs)
+        for j in range(2):
+            t = step * 2 + j
+            at = pl.ds(pl.multiple_of(t * LANES, LANES), LANES)
+            below, above = received(chip, across, t)
+            for var in range(5):
+                accs[j] = accs[j] + adjoint[var, 0:SUB, at] * below[var]
+                accs[2 + j] = accs[2 + j] + adjoint[var, rows - SUB:rows, at] * above[var]
+        return tuple(accs)
+
+    zero = jnp.zeros((SUB, LANES), F32)
+    accs = lax.fori_loop(0, tiles // 2, body, (zero,) * 4)
+    acc = (total[...] + accs[0]) + (accs[1] + accs[2]) + accs[3]
+    lane = tile_iota(1)
+    target = slots[0] * mix[0]
+    for m in range(1, slots.shape[0]):
+        target = target + slots[m] * mix[m]
+    step = slot_width(row_tiles)
+    while step < LANES:
+        target = target + pltpu.roll(target, step, 1)
+        step *= 2
+    for var in range(5):
+        for rt in range(row_tiles):
+            own = slice(rt * SUB, (rt + 1) * SUB)
+            moved = pltpu.roll(target, LANES - 1 - (var * row_tiles + rt), 1)
+            extra = jnp.where(lane == LANES - 1, -penalty * moved, 0.0)
+            column_ref[var, own, :] = extra
+            acc = acc + adjoint[var, own, (tiles - 1) * LANES:tiles * LANES] * extra
+    points = rows * lax.axis_size("line") * cols
+    sum_ref[...] = jnp.full((SUB, LANES), jnp.sum(acc) / points)
+
+
+def border_kernel(chip, across, column, res, out_ref, stage, sems):
+    rows, cols = stage.shape[1:]
+    row_tiles, tiles = rows // SUB, cols // LANES
+
+    def body(t, carry):
         at = pl.ds(pl.multiple_of(t * LANES, LANES), LANES)
-        near = [chip[n, :, at] for n in range(4)]
-        far = [across[n, :, at] for n in range(4)]
-        below = unpack([jnp.where(odd, a, b) for a, b in zip(near, far)], True)
-        above = unpack([jnp.where(odd, b, a) for a, b in zip(near, far)], False)
+        below, above = received(chip, across, t)
         for var in range(5):
             for rt in range(row_tiles):
-                own = slice(rt * SUB, (rt + 1) * SUB)
-                r = res[var, t, own, :]
+                r = res[var, t, rt * SUB:(rt + 1) * SUB, :]
                 for there, extra in ((0, below[var]), (row_tiles - 1, above[var])):
                     if rt == there:
                         r = r + extra
-                        acc = acc + adjoint[var, own, at] * extra
-                stage[var, own, at] = r
-        return acc
+                stage[var, rt * SUB:(rt + 1) * SUB, at] = r
+        return carry
 
     parts = 4
     size = tiles // parts
     copies = []
-    acc = total[...]
-    lane = tile_iota(1)
     for n in range(parts - 1, -1, -1):
-        acc = lax.fori_loop(n * size, (n + 1) * size, body, acc, unroll=2)
+        lax.fori_loop(n * size, (n + 1) * size, body, 0, unroll=2)
         if n == parts - 1:
-            target = slots[0] * mix[0]
-            for m in range(1, slots.shape[0]):
-                target = target + slots[m] * mix[m]
-            step = slot_width(row_tiles)
-            while step < LANES:
-                target = target + pltpu.roll(target, step, 1)
-                step *= 2
+            cut = slice((tiles - 1) * LANES, tiles * LANES)
             for var in range(5):
-                for rt in range(row_tiles):
-                    own = slice(rt * SUB, (rt + 1) * SUB)
-                    moved = pltpu.roll(target, LANES - 1 - (var * row_tiles + rt), 1)
-                    extra = jnp.where(lane == LANES - 1, -penalty * moved, 0.0)
-                    cut = slice((tiles - 1) * LANES, tiles * LANES)
-                    stage[var, own, cut] = stage[var, own, cut] + extra
-                    acc = acc + adjoint[var, own, cut] * extra
+                stage[var, :, cut] = stage[var, :, cut] + column[var]
         cut = pl.ds(n * size * LANES, size * LANES)
         copies.append(pltpu.make_async_copy(stage.at[:, :, cut], out_ref.at[:, :, cut], sems.at[n]))
         copies[-1].start()
-    points = rows * lax.axis_size("line") * cols
-    sum_ref[...] = jnp.full((SUB, LANES), jnp.sum(acc) / points)
     for c in copies:
         c.wait()
 
@@ -475,9 +532,11 @@
     def cost(micros):
         return pl.CostEstimate(flops=micros * 10**6, bytes_accessed=micros * 3 * 10**6, transcendentals=0)
 
-    send_far, slots = pl.pallas_call(
-        pack_kernel, out_shape=[packed, flat], in_specs=[in_hbm] * 3, out_specs=[whole()] * 2,
-        scratch_shapes=[pltpu.VMEM((5, SUB, cols), F32), pltpu.VMEM((5, rows, LANES), F32), dma((3, 5))],
+    pad = pltpu.VMEM((4, 9, 3 * SUB, LANES), F32)
+    send_far, slots, held = pl.pallas_call(
+        pack_kernel, out_shape=[packed, flat, shape((5, rows, cols), F32)],
+        in_specs=[in_hbm] * 3, out_specs=[whole()] * 3,
+        scratch_shapes=[pad, dma((2 * row_tiles, 5))],
         compiler_params=params(), cost_estimate=cost(2),
     )(*[pltpu.with_memory_space_constraint(x, pltpu.HBM) for x in state])
     far = lax.ppermute(send_far, "line", [p for i in range(1, lines - 1, 2) for p in ((i, i + 1), (i + 1, i))])
@@ -494,39 +553,45 @@
     def lhs_of(count):
         return pltpu.VMEM((wide_of(tiles) * count * rows, 2 * PIECES * LANES), jnp.bfloat16)
 
-    lists = (counts[:, None] << 16) + (partners << 1) + orient
+    count_row = lax.pad(counts, jnp.int32(0), [(0, LANES - 1, 0)]).reshape(1, LANES)
     prim, press, xd, send_near, mix = pl.pallas_call(
         first_kernel,
         out_shape=[shape((4, tiles + 2, rows + 2 * SUB, LANES), F32), shape((tiles, rows, LANES), F32),
                    shape((5, tiles, rows, LANES), F32), packed, flat],
         in_specs=[whole()] * 4, out_specs=[whole()] * 5,
         scratch_shapes=[
-            pltpu.VMEM((CHUNK, 5, rows + SUB, LANES), F32),
+            pltpu.VMEM((CHUNK, 5, rows + 3 * SUB, LANES), F32),
             pltpu.VMEM((2, row_tiles + 1, 4, SUB, LANES), F32),
         ],
         compiler_params=params(), cost_estimate=cost(3),
-    )(*state, lists)
+    )(held, count_row, partners, orient)
     near = lax.ppermute(send_near, "line", [(i, i ^ 1) for i in range(lines)])
     fy = pl.pallas_call(
         second_kernel, out_shape=shape((5, tiles + 2, rows, LANES), F32),
-        in_specs=[whole()] * 6, out_specs=whole(), scratch_shapes=[lhs_of(4)],
+        in_specs=[whole()] * 4, out_specs=whole(), scratch_shapes=[lhs_of(4)],
         compiler_params=params(), cost_estimate=cost(2),
-    )(*state, prim, press, operator)
+    )(held, prim, press, operator)
     res, total = pl.pallas_call(
         volume_kernel,
         out_shape=[shape((5, tiles, rows, LANES), F32), shape((SUB, LANES), F32)],
-        in_specs=[whole()] * 7, out_specs=[whole()] * 2,
+        in_specs=[whole()] * 5, out_specs=[whole()] * 2,
         scratch_shapes=[lhs_of(5)], compiler_params=params(), cost_estimate=cost(2),
-    )(*state, adjoint[0], fy, xd, operator)
-    result, part = pl.pallas_call(
-        border_kernel,
-        out_shape=[shape((5, rows, cols), F32), shape((SUB, LANES), F32)],
-        in_specs=[whole()] * 7, out_specs=[anywhere, whole()],
+    )(held, adjoint[0], fy, xd, operator)
+    column, part = pl.pallas_call(
+        border_sum_kernel,
+        out_shape=[shape((5, rows, LANES), F32), shape((SUB, LANES), F32)],
+        in_specs=[whole()] * 6, out_specs=[whole()] * 2, compiler_params=params(), cost_estimate=cost(1),
+    )(near, far, slots, mix, adjoint[0], total)
+    result = pl.pallas_call(
+        border_kernel, out_shape=shape((5, rows, cols), F32),
+        in_specs=[whole()] * 4, out_specs=anywhere,
         scratch_shapes=[pltpu.VMEM((5, rows, cols), F32), dma((4,))],
         compiler_params=params(), cost_estimate=cost(2),
-    )(near, far, slots, mix, res, adjoint[0], total)
+    )(near, far, column, res)
     if lines <= 4:
-        parts = [part] + [lax.ppermute(part, "line", [(i, i ^ s) for i in range(lines)]) for s in range(1, lines)]
+        parts = [part]
+        for n in range(1, lines):
+            parts.append(lax.ppermute(part, "line", [(i, i ^ n) for i in range(lines)]))
         correction = pl.pallas_call(
             total_kernel, out_shape=shape((1,), F32), in_specs=[whole()] * lines,
             out_specs=pl.BlockSpec(memory_space=pltpu.SMEM), compiler_params=params(),

time: 33.8 us -> 28.8 us (0.85)
  the two profiles are of different devices: /device:TPU:1 before, /device:TPU:0 now
where the time goes in v4:
time: 28.8 us; the launch traced here: 28.7 us
  starting transfers between devices  12.6 us (44%)
  Pallas kernels  9.87 us (34%)
  waiting for transfers between devices  4.74 us (16%)
  between operations  1.44 us (5%)
    ppermute x3, starting transfers between devices, per_device(): got = lax.ppermute(rounds[-1], 'blk', [(i, i ^ hop) for i in range(blocks)])  5.68 us
    ppermute x1, starting transfers between devices, per_device(): near = lax.ppermute(send_near, 'line', [(i, i ^ 1) for i in range(lines)])  4.28 us
    ppermute x3, waiting for transfers between devices, per_device(): got = lax.ppermute(rounds[-1], 'blk', [(i, i ^ hop) for i in range(blocks)])  4.12 us
    pallas_call x1, Pallas kernels, per_device(): pl.pallas_call(first_kernel, out_shape=[shape((4, tiles + 2, rows + 2 * S...  2.28 us
    pallas_call x1, Pallas kernels, per_device(): pl.pallas_call(pack_kernel, out_shape=[packed, flat, shape((5, rows, cols...  1.93 us
    ppermute x3, starting transfers between devices, per_device(): parts.append(lax.ppermute(part, 'line', [(i, i ^ n) for i in range(lines)]))  1.92 us
    pallas_call x1, Pallas kernels, per_device(): pl.pallas_call(volume_kernel, out_shape=[shape((5, tiles, rows, LANES), F...  1.72 us
    pallas_call x1, Pallas kernels, per_device(): pl.pallas_call(second_kernel, out_shape=shape((5, tiles + 2, rows, LANES)...  1.32 us
  transfers between devices with their start and end apart: 8, of which 3 were waited for; matrix products, arithmetic and copies ran while one was open for 0% of the time, Pallas kernels for 23%

profile of v4, /device:TPU:0, one launch (start us, length us, event | category | flops | bytes accessed | tf_op | source)
XLA Modules:
  0.0 28.7 jit_solution(10667227573890386633)
XLA Ops:
  0.6 0.0 copy-start.3
  0.6 0.0 copy-start.2
  0.7 0.0 copy-start.1
  0.7 1.9 %shard_map.95 = (f32[4,8,4096]{2,1,0:T(8,128)S(1)}, f32[1,8,128]{2,1,0:T(8,128)S(1)}, f32[5,16,4096]{2,1,0:T(8,128)S(1)}) custom-call(f32[16,4096]{1,0:T(8,128)} %bitcast.11, f32[3,16,4096]{2,1,0:T(8,128)} %bitcast.10, f32[16,4096]{1,0:T(8,128)} %bitcast.12), custom_call_target="tpu_custom_call" | custom-call | flops 2000000 | bytes 6000000 | tf_op jit(solution)/shard_map/pallas_call | solution.py:536
  2.6 0.7 %collective-permute-start.1 = (f32[4,8,4096]{2,1,0:T(8,128)S(1)}, f32[4,8,4096]{2,1,0:T(8,128)S(1)}, u32[]{:S(2)}, u32[]{:S(2)}) collective-permute-start(f32[4,8,4096]{2,1,0:T(8,128)S(1)} %get-tuple-element.16), channel_id=1, source_target_pairs={{1,2},{2,1},{5,6},{6,5},{9,10},{10,9},{13,14},{14,13},{17,18},{18,... | collective-permute-start | bytes 1572872 | tf_op jit(solution)/shard_map/ppermute | solution.py:542
  4.0 0.0 copy-done.3
  4.0 0.0 copy-done.2
  4.0 2.3 %shard_map.96 = (f32[4,34,32,128]{3,2,1,0:T(8,128)S(1)}, f32[32,16,128]{2,1,0:T(8,128)S(1)}, f32[5,32,16,128]{3,2,1,0:T(8,128)S(1)}, f32[4,8,4096]{2,1,0:T(8,128)S(1)}, f32[1,8,128]{2,1,0:T(8,128)S(1)}) custom-call(f32[5,16,4096]{2,1,0:T(8,128)S(1)} %get-tuple-element.14.state_ref, s32[1,128]{1,0:T(1,128)S(1)} %pad_bitcast_fusion.counts, ...), custom_call_target="tpu_custom_call" | custom-call | flops 3000000 | bytes 9000000 | tf_op jit(solution)/shard_map/pallas_call | solution.py:557
  6.3 4.3 %collective-permute-start = (f32[4,8,4096]{2,1,0:T(8,128)S(1)}, f32[4,8,4096]{2,1,0:T(8,128)S(1)}, u32[]{:S(2)}, u32[]{:S(2)}) collective-permute-start(f32[4,8,4096]{2,1,0:T(8,128)S(1)} %get-tuple-element.15), channel_id=1, source_target_pairs={{0,1},{1,0},{2,3},{3,2},{4,5},{5,4},{6,7},{7,6},{8,9},{9,8},{10,11... | collective-permute-start | bytes 1572872 | tf_op jit(solution)/shard_map/ppermute | solution.py:568
  10.6 1.5 %collective-permute-start.2 = (f32[1,8,128]{2,1,0:T(8,128)S(1)}, f32[1,8,128]{2,1,0:T(8,128)S(1)}, u32[]{:S(2)}, u32[]{:S(2)}) collective-permute-start(f32[1,8,128]{2,1,0:T(8,128)S(1)} %get-tuple-element.17), channel_id=1, source_target_pairs={{0,4},{4,0},{8,12},{12,8},{16,20},{20,16},{24,28},{28,24},{1,5},{5... | collective-permute-start | bytes 12296 | tf_op jit(solution)/shard_map/ppermute | solution.py:546
  12.1 2.1 %collective-permute-done.2 = f32[1,8,128]{2,1,0:T(8,128)S(1)} collective-permute-done((f32[1,8,128]{2,1,0:T(8,128)S(1)}, f32[1,8,128]{2,1,0:T(8,128)S(1)}, u32[]{:S(2)}, u32[]{:S(2)}) %collective-permute-start.2) | collective-permute-done | bytes 4128 | tf_op jit(solution)/shard_map/ppermute | solution.py:546
  14.2 1.6 %collective-permute-start.3 = (f32[1,8,128]{2,1,0:T(8,128)S(1)}, f32[1,8,128]{2,1,0:T(8,128)S(1)}, u32[]{:S(2)}, u32[]{:S(2)}) collective-permute-start(f32[1,8,128]{2,1,0:T(8,128)S(1)} %add.11), channel_id=1, source_target_pairs={{0,8},{4,12},{8,0},{12,4},{16,24},{20,28},{24,16},{28,20},{1,9},{5... | collective-permute-start | bytes 12296 | tf_op jit(solution)/shard_map/ppermute | solution.py:546
  15.7 2.0 %collective-permute-done.3 = f32[1,8,128]{2,1,0:T(8,128)S(1)} collective-permute-done((f32[1,8,128]{2,1,0:T(8,128)S(1)}, f32[1,8,128]{2,1,0:T(8,128)S(1)}, u32[]{:S(2)}, u32[]{:S(2)}) %collective-permute-start.3) | collective-permute-done | bytes 4128 | tf_op jit(solution)/shard_map/ppermute | solution.py:546
  17.8 2.6 %collective-permute-start.4 = (f32[1,8,128]{2,1,0:T(8,128)S(1)}, f32[1,8,128]{2,1,0:T(8,128)S(1)}, u32[]{:S(2)}, u32[]{:S(2)}) collective-permute-start(f32[1,8,128]{2,1,0:T(8,128)S(1)} %add.12), channel_id=1, source_target_pairs={{0,16},{4,20},{8,24},{12,28},{16,0},{20,4},{24,8},{28,12},{1,17},{... | collective-permute-start | bytes 12296 | tf_op jit(solution)/shard_map/ppermute | solution.py:546
  20.4 0.0 copy-done.1
  20.4 0.0 copy-start
  20.4 1.3 %shard_map.97.fy = f32[5,34,16,128]{3,2,1,0:T(8,128)S(1)} custom-call(f32[5,16,4096]{2,1,0:T(8,128)S(1)} %get-tuple-element.14.state_ref, f32[4,34,32,128]{3,2,1,0:T(8,128)S(1)} %get-tuple-element.19.prim, f32[32,16,128]{2,1,0:T(8,128)S(1)} %get-tuple-element.20.press, bf16[3,768,128]{2,1,0:T(8,128)(2,1)S(1)} %copy-done.1), custom_call_target="tpu_custom_call" | custom-call | flops 2000000 | bytes 6000000 | tf_op jit(solution)/shard_map/pallas_call | solution.py:569
  21.7 0.0 copy-done
  21.7 1.7 %shard_map.98 = (f32[5,32,16,128]{3,2,1,0:T(8,128)S(1)}, f32[8,128]{1,0:T(8,128)S(1)}) custom-call(f32[5,16,4096]{2,1,0:T(8,128)S(1)} %get-tuple-element.14.state_ref, f32[5,16,4096]{2,1,0:T(8,128)S(1)} %bitcast.7, f32[5,34,16,128]{3,2,1,0:T(8,128)S(1)} %shard_map.97.fy, f32[5,32,16,128]{3,2,1,0:T(8,128)S(1)} %get-tuple-element.21.xd, ...), custom_call_target="tpu_custom_call" | custom-call | flops 2000000 | bytes 6000000 | tf_op jit(solution)/shard_map/pallas_call | solution.py:574
  23.4 0.0 collective-permute-done.4
  23.4 0.0 collective-permute-done.1.across
  23.5 0.0 collective-permute-done.chip
  23.5 0.9 %shard_map.99 = (f32[5,16,128]{2,1,0:T(8,128)S(1)}, f32[8,128]{1,0:T(8,128)S(1)}) custom-call(f32[4,8,4096]{2,1,0:T(8,128)S(1)} %collective-permute-done.chip, f32[4,8,4096]{2,1,0:T(8,128)S(1)} %collective-permute-done.1.across, f32[1,8,128]{2,1,0:T(8,128)S(1)} %add.13.slots, f32[1,8,128]{2,1,0:T(8,128)S(1)} %get-tuple-element.18.mix, ...), custom_call_target="tpu_custom_call" | custom-call | flops 1000000 | bytes 3000000 | tf_op jit(solution)/shard_map/pallas_call | solution.py:580
  24.3 0.1 collective-permute-start.7
  24.4 0.1 collective-permute-start.6
  24.5 1.7 %collective-permute-start.5 = (f32[8,128]{1,0:T(8,128)S(1)}, f32[8,128]{1,0:T(8,128)S(1)}, u32[]{:S(2)}, u32[]{:S(2)}) collective-permute-start(f32[8,128]{1,0:T(8,128)S(1)} %get-tuple-element.25.refs_0_), channel_id=1, source_target_pairs={{0,1},{1,0},{2,3},{3,2},{4,5},{5,4},{6,7},{7,6},{8,9},{9,8},{10,11... | collective-permute-start | bytes 12296 | tf_op jit(solution)/shard_map/ppermute | solution.py:594
  26.3 1.2 %shard_map.100 = f32[5,16,4096]{2,1,0:T(8,128)} custom-call(f32[4,8,4096]{2,1,0:T(8,128)S(1)} %collective-permute-done.chip, f32[4,8,4096]{2,1,0:T(8,128)S(1)} %collective-permute-done.1.across, f32[5,16,128]{2,1,0:T(8,128)S(1)} %get-tuple-element.23.column, f32[5,32,16,128]{3,2,1,0:T(8,128)S(1)} %get-tuple-element.24.res), custom_call_target="tpu_custom_call" | custom-call | flops 2000000 | bytes 6000000 | tf_op jit(solution)/shard_map/pallas_call | solution.py:585
  27.5 0.0 collective-permute-done.7.refs_3_
  27.5 0.6 %collective-permute-done.6.refs_2_ = f32[8,128]{1,0:T(8,128)S(1)} collective-permute-done((f32[8,128]{1,0:T(8,128)S(1)}, f32[8,128]{1,0:T(8,128)S(1)}, u32[]{:S(2)}, u32[]{:S(2)}) %collective-permute-start.6) | collective-permute-done | bytes 4128 | tf_op jit(solution)/shard_map/ppermute | solution.py:594
  28.1 0.0 collective-permute-done.5.refs_1_
  28.1 0.6 %shard_map.101 = f32[1]{0:T(128)} custom-call(f32[8,128]{1,0:T(8,128)S(1)} %get-tuple-element.25.refs_0_, f32[8,128]{1,0:T(8,128)S(1)} %collective-permute-done.5.refs_1_, f32[8,128]{1,0:T(8,128)S(1)} %collective-permute-done.6.refs_2_, f32[8,128]{1,0:T(8,128)S(1)} %collective-permute-done.7.refs_3_), custom_call_target="tpu_custom_call" | custom-call | tf_op jit(solution)/shard_map/pallas_call | solution.py:595
  (4 shorter events, 0.0 us)
Async XLA Ops:
  0.6 3.3 %copy-start.3 = (s32[1,4]{1,0:T(1,128)S(1)}, s32[1,4]{1,0:T(1,128)}, u32[]{:S(2)}) copy-start(s32[1,4]{1,0:T(1,128)} %orient.1) | copy-start | bytes 52
  0.6 3.3 %copy-start.2 = (s32[1,4]{1,0:T(1,128)S(1)}, s32[1,4]{1,0:T(1,128)}, u32[]{:S(2)}) copy-start(s32[1,4]{1,0:T(1,128)} %partners.1) | copy-start | bytes 52
  0.7 19.7 %copy-start.1 = (bf16[3,768,128]{2,1,0:T(8,128)(2,1)S(1)}, bf16[3,768,128]{2,1,0:T(8,128)(2,1)}, u32[]{:S(2)}) copy-start(bf16[3,768,128]{2,1,0:T(8,128)(2,1)} %constant.4.clone.operator) | copy-start | bytes 1769476
  2.6 20.9 %collective-permute-start.1 = (f32[4,8,4096]{2,1,0:T(8,128)S(1)}, f32[4,8,4096]{2,1,0:T(8,128)S(1)}, u32[]{:S(2)}, u32[]{:S(2)}) collective-permute-start(f32[4,8,4096]{2,1,0:T(8,128)S(1)} %get-tuple-element.16), channel_id=1, source_target_pairs={{1,2},{2,1},{5,6},{6,5},{9,10},{10,9},{13,14},{14,13},{17,18},{18,... | collective-permute-start | bytes 1572872 | tf_op jit(solution)/shard_map/ppermute | solution.py:542
  6.3 17.2 %collective-permute-start = (f32[4,8,4096]{2,1,0:T(8,128)S(1)}, f32[4,8,4096]{2,1,0:T(8,128)S(1)}, u32[]{:S(2)}, u32[]{:S(2)}) collective-permute-start(f32[4,8,4096]{2,1,0:T(8,128)S(1)} %get-tuple-element.15), channel_id=1, source_target_pairs={{0,1},{1,0},{2,3},{3,2},{4,5},{5,4},{6,7},{7,6},{8,9},{9,8},{10,11... | collective-permute-start | bytes 1572872 | tf_op jit(solution)/shard_map/ppermute | solution.py:568
  10.6 3.6 %collective-permute-start.2 = (f32[1,8,128]{2,1,0:T(8,128)S(1)}, f32[1,8,128]{2,1,0:T(8,128)S(1)}, u32[]{:S(2)}, u32[]{:S(2)}) collective-permute-start(f32[1,8,128]{2,1,0:T(8,128)S(1)} %get-tuple-element.17), channel_id=1, source_target_pairs={{0,4},{4,0},{8,12},{12,8},{16,20},{20,16},{24,28},{28,24},{1,5},{5... | collective-permute-start | bytes 12296 | tf_op jit(solution)/shard_map/ppermute | solution.py:546
  14.2 3.6 %collective-permute-start.3 = (f32[1,8,128]{2,1,0:T(8,128)S(1)}, f32[1,8,128]{2,1,0:T(8,128)S(1)}, u32[]{:S(2)}, u32[]{:S(2)}) collective-permute-start(f32[1,8,128]{2,1,0:T(8,128)S(1)} %add.11), channel_id=1, source_target_pairs={{0,8},{4,12},{8,0},{12,4},{16,24},{20,28},{24,16},{28,20},{1,9},{5... | collective-permute-start | bytes 12296 | tf_op jit(solution)/shard_map/ppermute | solution.py:546
  17.8 5.7 %collective-permute-start.4 = (f32[1,8,128]{2,1,0:T(8,128)S(1)}, f32[1,8,128]{2,1,0:T(8,128)S(1)}, u32[]{:S(2)}, u32[]{:S(2)}) collective-permute-start(f32[1,8,128]{2,1,0:T(8,128)S(1)} %add.12), channel_id=1, source_target_pairs={{0,16},{4,20},{8,24},{12,28},{16,0},{20,4},{24,8},{28,12},{1,17},{... | collective-permute-start | bytes 12296 | tf_op jit(solution)/shard_map/ppermute | solution.py:546
  20.4 1.3 %copy-start = (f32[1,5,16,4096]{3,2,1,0:T(8,128)S(1)}, f32[1,5,16,4096]{3,2,1,0:T(8,128)}, u32[]{:S(2)}) copy-start(f32[1,5,16,4096]{3,2,1,0:T(8,128)} %param.11) | copy-start | bytes 3932164
  24.3 3.1 %collective-permute-start.7 = (f32[8,128]{1,0:T(8,128)S(1)}, f32[8,128]{1,0:T(8,128)S(1)}, u32[]{:S(2)}, u32[]{:S(2)}) collective-permute-start(f32[8,128]{1,0:T(8,128)S(1)} %get-tuple-element.25.refs_0_), channel_id=1, source_target_pairs={{0,3},{1,2},{2,1},{3,0},{4,7},{5,6},{6,5},{7,4},{8,11},{9,10},{10,... | collective-permute-start | bytes 12296 | tf_op jit(solution)/shard_map/ppermute | solution.py:594
  24.4 3.7 %collective-permute-start.6 = (f32[8,128]{1,0:T(8,128)S(1)}, f32[8,128]{1,0:T(8,128)S(1)}, u32[]{:S(2)}, u32[]{:S(2)}) collective-permute-start(f32[8,128]{1,0:T(8,128)S(1)} %get-tuple-element.25.refs_0_), channel_id=1, source_target_pairs={{0,2},{1,3},{2,0},{3,1},{4,6},{5,7},{6,4},{7,5},{8,10},{9,11},{10,... | collective-permute-start | bytes 12296 | tf_op jit(solution)/shard_map/ppermute | solution.py:594
  24.5 3.6 %collective-permute-start.5 = (f32[8,128]{1,0:T(8,128)S(1)}, f32[8,128]{1,0:T(8,128)S(1)}, u32[]{:S(2)}, u32[]{:S(2)}) collective-permute-start(f32[8,128]{1,0:T(8,128)S(1)} %get-tuple-element.25.refs_0_), channel_id=1, source_target_pairs={{0,1},{1,0},{2,3},{3,2},{4,5},{5,4},{6,7},{7,6},{8,9},{9,8},{10,11... | collective-permute-start | bytes 12296 | tf_op jit(solution)/shard_map/ppermute | solution.py:594

commit v5 on v4

--- a/solution.py
+++ b/solution.py
@@ -446,31 +446,28 @@
 
     def body(step, accs):
         accs = list(accs)
-        for j in range(2):
-            t = step * 2 + j
+        for j in range(4):
+            t = step * 4 + j
             at = pl.ds(pl.multiple_of(t * LANES, LANES), LANES)
             below, above = received(chip, across, t)
             for var in range(5):
-                accs[j] = accs[j] + adjoint[var, 0:SUB, at] * below[var]
-                accs[2 + j] = accs[2 + j] + adjoint[var, rows - SUB:rows, at] * above[var]
+                accs[j] = accs[j] + (adjoint[var, 0:SUB, at] * below[var] + adjoint[var, rows - SUB:rows, at] * above[var])
         return tuple(accs)
 
     zero = jnp.zeros((SUB, LANES), F32)
-    accs = lax.fori_loop(0, tiles // 2, body, (zero,) * 4)
-    acc = (total[...] + accs[0]) + (accs[1] + accs[2]) + accs[3]
+    accs = lax.fori_loop(0, tiles // 4, body, (zero,) * 4)
+    acc = total[...] + ((accs[0] + accs[1]) + (accs[2] + accs[3]))
     lane = tile_iota(1)
+    width = slot_width(row_tiles)
     target = slots[0] * mix[0]
     for m in range(1, slots.shape[0]):
         target = target + slots[m] * mix[m]
-    step = slot_width(row_tiles)
-    while step < LANES:
-        target = target + pltpu.roll(target, step, 1)
-        step *= 2
     for var in range(5):
         for rt in range(row_tiles):
             own = slice(rt * SUB, (rt + 1) * SUB)
-            moved = pltpu.roll(target, LANES - 1 - (var * row_tiles + rt), 1)
-            extra = jnp.where(lane == LANES - 1, -penalty * moved, 0.0)
+            mine = lane % width == var * row_tiles + rt
+            value = jnp.sum(jnp.where(mine, target, 0.0), axis=1, keepdims=True)
+            extra = jnp.where(lane == LANES - 1, -penalty * value, 0.0)
             column_ref[var, own, :] = extra
             acc = acc + adjoint[var, own, (tiles - 1) * LANES:tiles * LANES] * extra
     points = rows * lax.axis_size("line") * cols

time: 28.8 us -> 28.5 us (0.990)
  Pallas kernels: 9.87 us -> 9.58 us
    pallas_call x1, Pallas kernels: 0.86 us -> 0.57 us  [per_device(): pl.pallas_call(border_sum_kernel, out_shape=[shape((5, rows, LANES), F32)...]
where the time goes in v5:
time: 28.5 us; the launch traced here: 28.4 us
  starting transfers between devices  12.6 us (44%)
  Pallas kernels  9.58 us (34%)
  waiting for transfers between devices  4.74 us (17%)
  between operations  1.44 us (5%)
    ppermute x3, starting transfers between devices, per_device(): got = lax.ppermute(rounds[-1], 'blk', [(i, i ^ hop) for i in range(blocks)])  5.68 us
    ppermute x1, starting transfers between devices, per_device(): near = lax.ppermute(send_near, 'line', [(i, i ^ 1) for i in range(lines)])  4.28 us
    ppermute x3, waiting for transfers between devices, per_device(): got = lax.ppermute(rounds[-1], 'blk', [(i, i ^ hop) for i in range(blocks)])  4.12 us
    pallas_call x1, Pallas kernels, per_device(): pl.pallas_call(first_kernel, out_shape=[shape((4, tiles + 2, rows + 2 * S...  2.28 us
    pallas_call x1, Pallas kernels, per_device(): pl.pallas_call(pack_kernel, out_shape=[packed, flat, shape((5, rows, cols...  1.93 us
    ppermute x3, starting transfers between devices, per_device(): parts.append(lax.ppermute(part, 'line', [(i, i ^ n) for i in range(lines)]))  1.92 us
    pallas_call x1, Pallas kernels, per_device(): pl.pallas_call(volume_kernel, out_shape=[shape((5, tiles, rows, LANES), F...  1.72 us
    pallas_call x1, Pallas kernels, per_device(): pl.pallas_call(second_kernel, out_shape=shape((5, tiles + 2, rows, LANES)...  1.32 us
  transfers between devices with their start and end apart: 8, of which 3 were waited for; matrix products, arithmetic and copies ran while one was open for 0% of the time, Pallas kernels for 23%

profile of v5, /device:TPU:0, one launch (start us, length us, event | category | flops | bytes accessed | tf_op | source)
XLA Modules:
  0.0 28.4 jit_solution(17573350231988932721)
XLA Ops:
  0.6 0.0 copy-start.3
  0.6 0.0 copy-start.2
  0.7 0.0 copy-start.1
  0.7 1.9 %shard_map.95 = (f32[4,8,4096]{2,1,0:T(8,128)S(1)}, f32[1,8,128]{2,1,0:T(8,128)S(1)}, f32[5,16,4096]{2,1,0:T(8,128)S(1)}) custom-call(f32[16,4096]{1,0:T(8,128)} %bitcast.11, f32[3,16,4096]{2,1,0:T(8,128)} %bitcast.10, f32[16,4096]{1,0:T(8,128)} %bitcast.12), custom_call_target="tpu_custom_call" | custom-call | flops 2000000 | bytes 6000000 | tf_op jit(solution)/shard_map/pallas_call | solution.py:533
  2.6 0.7 %collective-permute-start.1 = (f32[4,8,4096]{2,1,0:T(8,128)S(1)}, f32[4,8,4096]{2,1,0:T(8,128)S(1)}, u32[]{:S(2)}, u32[]{:S(2)}) collective-permute-start(f32[4,8,4096]{2,1,0:T(8,128)S(1)} %get-tuple-element.16), channel_id=1, source_target_pairs={{1,2},{2,1},{5,6},{6,5},{9,10},{10,9},{13,14},{14,13},{17,18},{18,... | collective-permute-start | bytes 1572872 | tf_op jit(solution)/shard_map/ppermute | solution.py:539
  4.0 0.0 copy-done.3
  4.0 0.0 copy-done.2
  4.0 2.3 %shard_map.96 = (f32[4,34,32,128]{3,2,1,0:T(8,128)S(1)}, f32[32,16,128]{2,1,0:T(8,128)S(1)}, f32[5,32,16,128]{3,2,1,0:T(8,128)S(1)}, f32[4,8,4096]{2,1,0:T(8,128)S(1)}, f32[1,8,128]{2,1,0:T(8,128)S(1)}) custom-call(f32[5,16,4096]{2,1,0:T(8,128)S(1)} %get-tuple-element.14.state_ref, s32[1,128]{1,0:T(1,128)S(1)} %pad_bitcast_fusion.counts, ...), custom_call_target="tpu_custom_call" | custom-call | flops 3000000 | bytes 9000000 | tf_op jit(solution)/shard_map/pallas_call | solution.py:554
  6.3 4.3 %collective-permute-start = (f32[4,8,4096]{2,1,0:T(8,128)S(1)}, f32[4,8,4096]{2,1,0:T(8,128)S(1)}, u32[]{:S(2)}, u32[]{:S(2)}) collective-permute-start(f32[4,8,4096]{2,1,0:T(8,128)S(1)} %get-tuple-element.15), channel_id=1, source_target_pairs={{0,1},{1,0},{2,3},{3,2},{4,5},{5,4},{6,7},{7,6},{8,9},{9,8},{10,11... | collective-permute-start | bytes 1572872 | tf_op jit(solution)/shard_map/ppermute | solution.py:565
  10.6 1.5 %collective-permute-start.2 = (f32[1,8,128]{2,1,0:T(8,128)S(1)}, f32[1,8,128]{2,1,0:T(8,128)S(1)}, u32[]{:S(2)}, u32[]{:S(2)}) collective-permute-start(f32[1,8,128]{2,1,0:T(8,128)S(1)} %get-tuple-element.17), channel_id=1, source_target_pairs={{0,4},{4,0},{8,12},{12,8},{16,20},{20,16},{24,28},{28,24},{1,5},{5... | collective-permute-start | bytes 12296 | tf_op jit(solution)/shard_map/ppermute | solution.py:543
  12.1 2.1 %collective-permute-done.2 = f32[1,8,128]{2,1,0:T(8,128)S(1)} collective-permute-done((f32[1,8,128]{2,1,0:T(8,128)S(1)}, f32[1,8,128]{2,1,0:T(8,128)S(1)}, u32[]{:S(2)}, u32[]{:S(2)}) %collective-permute-start.2) | collective-permute-done | bytes 4128 | tf_op jit(solution)/shard_map/ppermute | solution.py:543
  14.2 1.6 %collective-permute-start.3 = (f32[1,8,128]{2,1,0:T(8,128)S(1)}, f32[1,8,128]{2,1,0:T(8,128)S(1)}, u32[]{:S(2)}, u32[]{:S(2)}) collective-permute-start(f32[1,8,128]{2,1,0:T(8,128)S(1)} %add.11), channel_id=1, source_target_pairs={{0,8},{4,12},{8,0},{12,4},{16,24},{20,28},{24,16},{28,20},{1,9},{5... | collective-permute-start | bytes 12296 | tf_op jit(solution)/shard_map/ppermute | solution.py:543
  15.7 2.0 %collective-permute-done.3 = f32[1,8,128]{2,1,0:T(8,128)S(1)} collective-permute-done((f32[1,8,128]{2,1,0:T(8,128)S(1)}, f32[1,8,128]{2,1,0:T(8,128)S(1)}, u32[]{:S(2)}, u32[]{:S(2)}) %collective-permute-start.3) | collective-permute-done | bytes 4128 | tf_op jit(solution)/shard_map/ppermute | solution.py:543
  17.8 2.6 %collective-permute-start.4 = (f32[1,8,128]{2,1,0:T(8,128)S(1)}, f32[1,8,128]{2,1,0:T(8,128)S(1)}, u32[]{:S(2)}, u32[]{:S(2)}) collective-permute-start(f32[1,8,128]{2,1,0:T(8,128)S(1)} %add.12), channel_id=1, source_target_pairs={{0,16},{4,20},{8,24},{12,28},{16,0},{20,4},{24,8},{28,12},{1,17},{... | collective-permute-start | bytes 12296 | tf_op jit(solution)/shard_map/ppermute | solution.py:543
  20.4 0.0 copy-done.1
  20.4 0.0 copy-start
  20.4 1.3 %shard_map.97.fy = f32[5,34,16,128]{3,2,1,0:T(8,128)S(1)} custom-call(f32[5,16,4096]{2,1,0:T(8,128)S(1)} %get-tuple-element.14.state_ref, f32[4,34,32,128]{3,2,1,0:T(8,128)S(1)} %get-tuple-element.19.prim, f32[32,16,128]{2,1,0:T(8,128)S(1)} %get-tuple-element.20.press, bf16[3,768,128]{2,1,0:T(8,128)(2,1)S(1)} %copy-done.1), custom_call_target="tpu_custom_call" | custom-call | flops 2000000 | bytes 6000000 | tf_op jit(solution)/shard_map/pallas_call | solution.py:566
  21.7 0.0 copy-done
  21.7 1.7 %shard_map.98 = (f32[5,32,16,128]{3,2,1,0:T(8,128)S(1)}, f32[8,128]{1,0:T(8,128)S(1)}) custom-call(f32[5,16,4096]{2,1,0:T(8,128)S(1)} %get-tuple-element.14.state_ref, f32[5,16,4096]{2,1,0:T(8,128)S(1)} %bitcast.7, f32[5,34,16,128]{3,2,1,0:T(8,128)S(1)} %shard_map.97.fy, f32[5,32,16,128]{3,2,1,0:T(8,128)S(1)} %get-tuple-element.21.xd, ...), custom_call_target="tpu_custom_call" | custom-call | flops 2000000 | bytes 6000000 | tf_op jit(solution)/shard_map/pallas_call | solution.py:571
  23.4 0.0 collective-permute-done.4
  23.4 0.0 collective-permute-done.1.across
  23.5 0.0 collective-permute-done.chip
  23.5 0.6 %shard_map.99 = (f32[5,16,128]{2,1,0:T(8,128)S(1)}, f32[8,128]{1,0:T(8,128)S(1)}) custom-call(f32[4,8,4096]{2,1,0:T(8,128)S(1)} %collective-permute-done.chip, f32[4,8,4096]{2,1,0:T(8,128)S(1)} %collective-permute-done.1.across, f32[1,8,128]{2,1,0:T(8,128)S(1)} %add.13.slots, f32[1,8,128]{2,1,0:T(8,128)S(1)} %get-tuple-element.18.mix, ...), custom_call_target="tpu_custom_call" | custom-call | flops 1000000 | bytes 3000000 | tf_op jit(solution)/shard_map/pallas_call | solution.py:577
  24.0 0.1 collective-permute-start.7
  24.1 0.1 collective-permute-start.6
  24.3 1.7 %collective-permute-start.5 = (f32[8,128]{1,0:T(8,128)S(1)}, f32[8,128]{1,0:T(8,128)S(1)}, u32[]{:S(2)}, u32[]{:S(2)}) collective-permute-start(f32[8,128]{1,0:T(8,128)S(1)} %get-tuple-element.25.refs_0_), channel_id=1, source_target_pairs={{0,1},{1,0},{2,3},{3,2},{4,5},{5,4},{6,7},{7,6},{8,9},{9,8},{10,11... | collective-permute-start | bytes 12296 | tf_op jit(solution)/shard_map/ppermute | solution.py:591
  26.0 1.2 %shard_map.100 = f32[5,16,4096]{2,1,0:T(8,128)} custom-call(f32[4,8,4096]{2,1,0:T(8,128)S(1)} %collective-permute-done.chip, f32[4,8,4096]{2,1,0:T(8,128)S(1)} %collective-permute-done.1.across, f32[5,16,128]{2,1,0:T(8,128)S(1)} %get-tuple-element.23.column, f32[5,32,16,128]{3,2,1,0:T(8,128)S(1)} %get-tuple-element.24.res), custom_call_target="tpu_custom_call" | custom-call | flops 2000000 | bytes 6000000 | tf_op jit(solution)/shard_map/pallas_call | solution.py:582
  27.2 0.0 collective-permute-done.7.refs_3_
  27.2 0.6 %collective-permute-done.6.refs_2_ = f32[8,128]{1,0:T(8,128)S(1)} collective-permute-done((f32[8,128]{1,0:T(8,128)S(1)}, f32[8,128]{1,0:T(8,128)S(1)}, u32[]{:S(2)}, u32[]{:S(2)}) %collective-permute-start.6) | collective-permute-done | bytes 4128 | tf_op jit(solution)/shard_map/ppermute | solution.py:591
  27.8 0.0 collective-permute-done.5.refs_1_
  27.8 0.6 %shard_map.101 = f32[1]{0:T(128)} custom-call(f32[8,128]{1,0:T(8,128)S(1)} %get-tuple-element.25.refs_0_, f32[8,128]{1,0:T(8,128)S(1)} %collective-permute-done.5.refs_1_, f32[8,128]{1,0:T(8,128)S(1)} %collective-permute-done.6.refs_2_, f32[8,128]{1,0:T(8,128)S(1)} %collective-permute-done.7.refs_3_), custom_call_target="tpu_custom_call" | custom-call | tf_op jit(solution)/shard_map/pallas_call | solution.py:592
  (4 shorter events, 0.0 us)
Async XLA Ops:
  0.6 3.3 %copy-start.3 = (s32[1,4]{1,0:T(1,128)S(1)}, s32[1,4]{1,0:T(1,128)}, u32[]{:S(2)}) copy-start(s32[1,4]{1,0:T(1,128)} %orient.1) | copy-start | bytes 52
  0.6 3.3 %copy-start.2 = (s32[1,4]{1,0:T(1,128)S(1)}, s32[1,4]{1,0:T(1,128)}, u32[]{:S(2)}) copy-start(s32[1,4]{1,0:T(1,128)} %partners.1) | copy-start | bytes 52
  0.7 19.7 %copy-start.1 = (bf16[3,768,128]{2,1,0:T(8,128)(2,1)S(1)}, bf16[3,768,128]{2,1,0:T(8,128)(2,1)}, u32[]{:S(2)}) copy-start(bf16[3,768,128]{2,1,0:T(8,128)(2,1)} %constant.4.clone.operator) | copy-start | bytes 1769476
  2.6 20.9 %collective-permute-start.1 = (f32[4,8,4096]{2,1,0:T(8,128)S(1)}, f32[4,8,4096]{2,1,0:T(8,128)S(1)}, u32[]{:S(2)}, u32[]{:S(2)}) collective-permute-start(f32[4,8,4096]{2,1,0:T(8,128)S(1)} %get-tuple-element.16), channel_id=1, source_target_pairs={{1,2},{2,1},{5,6},{6,5},{9,10},{10,9},{13,14},{14,13},{17,18},{18,... | collective-permute-start | bytes 1572872 | tf_op jit(solution)/shard_map/ppermute | solution.py:539
  6.3 17.2 %collective-permute-start = (f32[4,8,4096]{2,1,0:T(8,128)S(1)}, f32[4,8,4096]{2,1,0:T(8,128)S(1)}, u32[]{:S(2)}, u32[]{:S(2)}) collective-permute-start(f32[4,8,4096]{2,1,0:T(8,128)S(1)} %get-tuple-element.15), channel_id=1, source_target_pairs={{0,1},{1,0},{2,3},{3,2},{4,5},{5,4},{6,7},{7,6},{8,9},{9,8},{10,11... | collective-permute-start | bytes 1572872 | tf_op jit(solution)/shard_map/ppermute | solution.py:565
  10.6 3.6 %collective-permute-start.2 = (f32[1,8,128]{2,1,0:T(8,128)S(1)}, f32[1,8,128]{2,1,0:T(8,128)S(1)}, u32[]{:S(2)}, u32[]{:S(2)}) collective-permute-start(f32[1,8,128]{2,1,0:T(8,128)S(1)} %get-tuple-element.17), channel_id=1, source_target_pairs={{0,4},{4,0},{8,12},{12,8},{16,20},{20,16},{24,28},{28,24},{1,5},{5... | collective-permute-start | bytes 12296 | tf_op jit(solution)/shard_map/ppermute | solution.py:543
  14.2 3.6 %collective-permute-start.3 = (f32[1,8,128]{2,1,0:T(8,128)S(1)}, f32[1,8,128]{2,1,0:T(8,128)S(1)}, u32[]{:S(2)}, u32[]{:S(2)}) collective-permute-start(f32[1,8,128]{2,1,0:T(8,128)S(1)} %add.11), channel_id=1, source_target_pairs={{0,8},{4,12},{8,0},{12,4},{16,24},{20,28},{24,16},{28,20},{1,9},{5... | collective-permute-start | bytes 12296 | tf_op jit(solution)/shard_map/ppermute | solution.py:543
  17.8 5.7 %collective-permute-start.4 = (f32[1,8,128]{2,1,0:T(8,128)S(1)}, f32[1,8,128]{2,1,0:T(8,128)S(1)}, u32[]{:S(2)}, u32[]{:S(2)}) collective-permute-start(f32[1,8,128]{2,1,0:T(8,128)S(1)} %add.12), channel_id=1, source_target_pairs={{0,16},{4,20},{8,24},{12,28},{16,0},{20,4},{24,8},{28,12},{1,17},{... | collective-permute-start | bytes 12296 | tf_op jit(solution)/shard_map/ppermute | solution.py:543
  20.4 1.3 %copy-start = (f32[1,5,16,4096]{3,2,1,0:T(8,128)S(1)}, f32[1,5,16,4096]{3,2,1,0:T(8,128)}, u32[]{:S(2)}) copy-start(f32[1,5,16,4096]{3,2,1,0:T(8,128)} %param.11) | copy-start | bytes 3932164
  24.0 3.1 %collective-permute-start.7 = (f32[8,128]{1,0:T(8,128)S(1)}, f32[8,128]{1,0:T(8,128)S(1)}, u32[]{:S(2)}, u32[]{:S(2)}) collective-permute-start(f32[8,128]{1,0:T(8,128)S(1)} %get-tuple-element.25.refs_0_), channel_id=1, source_target_pairs={{0,3},{1,2},{2,1},{3,0},{4,7},{5,6},{6,5},{7,4},{8,11},{9,10},{10,... | collective-permute-start | bytes 12296 | tf_op jit(solution)/shard_map/ppermute | solution.py:591
  24.1 3.7 %collective-permute-start.6 = (f32[8,128]{1,0:T(8,128)S(1)}, f32[8,128]{1,0:T(8,128)S(1)}, u32[]{:S(2)}, u32[]{:S(2)}) collective-permute-start(f32[8,128]{1,0:T(8,128)S(1)} %get-tuple-element.25.refs_0_), channel_id=1, source_target_pairs={{0,2},{1,3},{2,0},{3,1},{4,6},{5,7},{6,4},{7,5},{8,10},{9,11},{10,... | collective-permute-start | bytes 12296 | tf_op jit(solution)/shard_map/ppermute | solution.py:591
  24.3 3.6 %collective-permute-start.5 = (f32[8,128]{1,0:T(8,128)S(1)}, f32[8,128]{1,0:T(8,128)S(1)}, u32[]{:S(2)}, u32[]{:S(2)}) collective-permute-start(f32[8,128]{1,0:T(8,128)S(1)} %get-tuple-element.25.refs_0_), channel_id=1, source_target_pairs={{0,1},{1,0},{2,3},{3,2},{4,5},{5,4},{6,7},{7,6},{8,9},{9,8},{10,11... | collective-permute-start | bytes 12296 | tf_op jit(solution)/shard_map/ppermute | solution.py:591
